TPU v7x, 256 devices: a whole 4x4x8 slice. The times are simulated.
256 devices in a mesh: dp: 4 (over y), seq: 16 (over z, core), fsdp: 4 (over x).
Axes of the slice: x: 4, y: 4, z: 8, core: 2. Of those that a mesh axis runs over, the one named last changes fastest.
Arguments:
- signal: bfloat16 [16, 2048, 1024], P(('dp', 'fsdp'), 'seq'), may hold values from -100 to 100
- w_query: bfloat16 [1024, 512], P('fsdp'), may hold values from -1 to 1
- w_key: bfloat16 [1024, 512], P('fsdp'), may hold values from -1 to 1
- w_value: bfloat16 [1024, 512], P('fsdp'), may hold values from -0.1875 to 0.1875
- w_output: bfloat16 [1024, 512], P('fsdp'), may hold values from -0.25 to 0.25
- upstream: bfloat16 [16, 2048, 1024], P(('dp', 'fsdp'), 'seq'), may hold values from -6 to 6
Outputs:
- output: bfloat16 [16, 2048, 1024], P(('dp', 'fsdp'), 'seq')
- grad_signal: bfloat16 [16, 2048, 1024], P(('dp', 'fsdp'), 'seq')
- grad_query: float32 [1024, 512], P('fsdp')
- grad_key: float32 [1024, 512], P('fsdp')
- grad_value: float32 [1024, 512], P('fsdp')
- grad_output: float32 [1024, 512], P('fsdp')
All inputs are finite; a program needn't handle non-finite values.
Results may differ from a plain program's by a relative error of at most 0.02.
The roundings to bfloat16 on the way count: a program that leaves them out, or rounds other values in their place, can miss the bound.
Values may be sent and summed in bfloat16 or wider, within the bound.
No kernel may reach another device: no remote copies, remote signals or barrier semaphores. Data moves between devices by JAX's collectives and lax.ppermute only.
A program may use at most 128 MiB of HBM per device.

v0:
```python
import jax
import jax.numpy as jnp
from jax import lax
from jax.experimental import pallas as pl
from jax.experimental.pallas import tpu as pltpu
from jax.sharding import Mesh
from jax.sharding import PartitionSpec as P


HSIZE = 64
LOG2E = 1.4426950408889634
F32 = jnp.float32
BF16 = jnp.bfloat16


def vmem(count):
    return [pl.BlockSpec(memory_space=pltpu.VMEM) for _ in range(count)]


def smem():
    return pl.BlockSpec(memory_space=pltpu.SMEM)


def call(kernel, ids, args, outs, scratch=()):
    return pl.pallas_call(
        kernel,
        in_specs=[smem()] + vmem(len(args)),
        out_specs=vmem(len(outs)),
        out_shape=[jax.ShapeDtypeStruct(s, d) for s, d in outs],
        scratch_shapes=list(scratch),
    )(ids, *args)


def normalize(rows):
    wide = rows.astype(F32)
    centre = wide - jnp.mean(wide, axis=-1, keepdims=True)
    variance = jnp.mean(centre * centre, axis=-1, keepdims=True)
    inverse = lax.rsqrt(variance + 1e-05)
    return centre * inverse, inverse


def dot(a, b, dims):
    return lax.dot_general(a, b, (dims, ((), ())), preferred_element_type=F32)


def low_lanes(shape):
    return lax.broadcasted_iota(jnp.int32, shape, len(shape) - 1) < HSIZE


def shift(value, axis, size, by):
    return lax.ppermute(value, axis, [(i, (i + by) % size) for i in range(size)])


def pair(value):
    return shift(value, "core", 2, 1)


def block_of(ids, step):
    return pl.multiple_of(lax.rem(ids[1] + step, 4) * 256, 256)


def stack_kernel(ids, sig, up, both):
    both[0] = normalize(sig[...])[0].astype(BF16)
    both[1] = up[...]


def whole_weight(piece):
    return jnp.concatenate([part[...] for part in piece], axis=0)


def project_kernel(ids, own, oth, w0t, w0b, w1t, w1b, w2t, w2b, w3t, w3b, heads, first, second):
    core = ids[0]
    for half, both in enumerate((own, oth)):
        at = core if half == 0 else 1 - core
        rows = pl.ds(pl.multiple_of(at * 128, 128), 128)
        first[rows, :] = both[0]
        second[rows, :] = jnp.where(core == 0, both[0], both[1])
    one = two = None
    for step, piece in enumerate(((w0t, w0b), (w1t, w1b), (w2t, w2b), (w3t, w3b))):
        cols = pl.ds(block_of(ids, step), 256)
        weight = whole_weight(piece)
        a = dot(first[:, cols], weight[:, :512], ((1,), (0,)))
        b = dot(second[:, cols], weight[:, 512:], ((1,), (0,)))
        one = a if one is None else one + a
        two = b if two is None else two + b
    mask = low_lanes((256, 128))
    for pair in range(4):
        lanes = slice(128 * pair, 128 * pair + 128)
        t1, t2 = one[:, lanes], two[:, lanes]
        heads[2 * pair] = jnp.where(mask, t1, pltpu.roll(t2, 64, 1)).astype(BF16)
        heads[2 * pair + 1] = jnp.where(mask, pltpu.roll(t1, 64, 1), t2).astype(BF16)


def attention_kernel(ids, own, other, send, keep, kv, qg, acc):
    core = ids[0]
    keys, block = kv.shape[0], 256

    @pl.when(core == 0)
    def _():
        kv[...] = own[...]
        qg[...] = other[0:1024, :]

    @pl.when(core != 0)
    def _():
        kv[...] = other[...]
        qg[...] = own[1024:2048, :]

    low = low_lanes((keys, 128))
    zero = jnp.zeros((), BF16)
    pairs = kv[...]
    key_rows = jnp.where(low, pairs, zero)
    value_rows = jnp.where(low, zero, pairs)
    key_cols = key_rows.astype(F32).T.astype(BF16)
    value_cols = value_rows.astype(F32).T.astype(BF16)
    low_q = low_lanes((block, 128))
    scale = jnp.where(low_lanes((1, 128)), HSIZE**-0.5, 1.0).astype(F32)
    acc[...] = jnp.zeros_like(acc)

    def step(i, carry):
        rows = pl.ds(pl.multiple_of(i * block, block), block)
        qb = qg[rows, :]
        s = dot(key_rows, qb, ((1,), (1,)))
        top = jnp.max(s, axis=0, keepdims=True)
        e = jnp.exp2((s - top) * (HSIZE**-0.5 * LOG2E))
        inv = 1.0 / jnp.sum(e, axis=0, keepdims=True)
        att = e * inv
        grad = dot(value_rows, qb, ((1,), (1,)))
        delta = jnp.sum(att * grad, axis=0, keepdims=True)
        weights = att.astype(BF16)
        gs = (att * (grad - delta)).astype(BF16)
        qk = jnp.where(low_q, qb, zero)
        qv = jnp.where(low_q, zero, qb)
        acc[...] += dot(gs, qk, ((1,), (0,))) + dot(weights, qv, ((1,), (0,)))
        turned = dot(key_cols, gs, ((1,), (0,))) + dot(value_cols, weights, ((1,), (0,)))
        result = (turned.T * scale).astype(BF16)

        send[pl.ds(pl.multiple_of(keys + i * block, block), block), :] = result
        return carry

    lax.fori_loop(0, 1024 // block, step, 0)

    total = acc[...] * scale
    keep[...] = total
    send[0:keys, :] = jnp.where(core == 0, 0.0, total).astype(BF16)


def merge_kernel(ids, keep, send, recv, moved, columns):
    core = ids[0]
    keys = keep.shape[0]
    half = keys // 2
    kv = (keep[...] + recv[0:keys, :].astype(F32)).astype(BF16)
    own, oth = send[keys:, :], recv[keys:, :]
    low = jnp.where(core == 0, own, oth)
    high = jnp.where(core == 0, oth, own)
    columns[:, 0:128] = kv
    columns[0:half, 128:256] = low
    columns[half:keys, 128:256] = high
    moved[0:half, :] = jnp.where(core == 0, kv[0:half], low)
    moved[half:keys, :] = jnp.where(core == 0, kv[half:keys], high)


def unpack(heads):
    mask = low_lanes((256, 128))
    one, two = [], []
    for pair in range(4):
        a, b = heads[2 * pair].astype(F32), heads[2 * pair + 1].astype(F32)
        one.append(jnp.where(mask, a, pltpu.roll(b, 64, 1)).astype(BF16))
        two.append(jnp.where(mask, pltpu.roll(a, 64, 1), b).astype(BF16))
    return jnp.concatenate(one, axis=1), jnp.concatenate(two, axis=1)


def outer_kernel(ids, columns, x0, r1, l1, r2, l2, r3, l3, r4, l4, keep, send, acc):
    core, place = ids[0], ids[2]

    def term(step, rows):
        start = lax.rem(place + step, 8) * 256
        chunk = columns[pl.ds(pl.multiple_of(start, 256), 256), :]
        return dot(rows, chunk, ((0,), (0,)))

    acc[...] = term(0, x0[...]) + term(7, r1[...]) + term(1, l1[...])
    acc[...] += term(6, r2[...]) + term(2, l2[...])
    acc[...] += term(5, r3[...]) + term(3, l3[...])
    acc[...] += term(4, jnp.concatenate([r4[...], l4[...]], axis=0))
    lane = lax.broadcasted_iota(jnp.int32, (32, 256), 1)
    mine = (lane < 192) == (core == 0)
    for part in range(4):
        for piece in range(4):
            for half in range(2):
                start = part * 256 + half * 128 + piece * 32
                value = jnp.where(mine, acc[start : start + 32, :], 0.0).astype(BF16)

                @pl.when(core == half)
                def _():
                    keep[4 * piece + part] = value

                @pl.when(core != half)
                def _():
                    send[4 * piece + part] = value


def back_kernel(ids, heads, w0t, w0b, w1t, w1b, w2t, w2b, w3t, w3b, keep, send):
    core = ids[0]
    one, two = unpack(heads)
    for step, piece in enumerate(((w0t, w0b), (w1t, w1b), (w2t, w2b), (w3t, w3b))):
        cols = pl.ds(block_of(ids, step), 256)
        weight = whole_weight(piece)
        a = dot(one, weight[:, :512], ((1,), (1,)))
        b = dot(two, weight[:, 512:], ((1,), (1,)))
        total = jnp.where(core == 0, a + b, a)
        extra = jnp.where(core == 0, 0.0, b)
        keep[0, :, cols] = jnp.where(core == 0, total[:128], total[128:])
        keep[1, :, cols] = jnp.where(core == 0, extra[:128], extra[128:])
        send[0, :, cols] = jnp.where(core == 0, total[128:], total[:128])
        send[1, :, cols] = jnp.where(core == 0, extra[128:], extra[:128])


def spread_kernel(ids, own, oth, gq, gk, gv, go):
    core = ids[0]
    mask = low_lanes((32, 128))
    scale = 32768**-0.5
    for half in range(2):
        for piece in range(4):
            rows = slice(half * 128 + piece * 32, half * 128 + piece * 32 + 32)
            for pair in range(4):
                a, b = (
                    jnp.where(core == half, own[piece, h], oth[piece, h]).astype(F32) * scale
                    for h in (2 * pair, 2 * pair + 1)
                )
                lanes = slice(128 * pair, 128 * pair + 128)
                for base, (low, high) in ((0, (gk, gv)), (128, (gq, go))):
                    ta, tb = a[:, base : base + 128], b[:, base : base + 128]
                    low[rows, lanes] = jnp.where(mask, ta, pltpu.roll(tb, 64, 1))
                    high[rows, lanes] = jnp.where(mask, pltpu.roll(ta, 64, 1), tb)


def finish_kernel(ids, sig, up, keep, recv, out, grad):
    normed_f, inverse = normalize(sig[...])
    out[...] = (sig[...].astype(F32) + keep[1] + recv[1]).astype(BF16)
    gn = keep[0] + recv[0]
    mean = jnp.mean(gn, axis=-1, keepdims=True)
    along = jnp.mean(gn * normed_f, axis=-1, keepdims=True)
    grad[...] = (up[...].astype(F32) + inverse * (gn - mean - normed_f * along)).astype(BF16)


def exchange(value, axis):
    return lax.all_to_all(value, axis, split_axis=0, concat_axis=0, tiled=True)


def body(signal, w_query, w_key, w_value, w_output, upstream):
    core, place = lax.axis_index("core"), lax.axis_index("fsdp")
    ids = jnp.stack([core, place, lax.axis_index("z")]).astype(jnp.int32)
    sig, up = signal[0], upstream[0]
    w0 = jnp.concatenate(
        [jnp.where(core == 0, w_key, w_query), jnp.where(core == 0, w_value, w_output)], axis=1
    )
    w0t, w0b = w0[:128], w0[128:]
    w1t, w3b = shift(w0t, "fsdp", 4, -1), shift(w0b, "fsdp", 4, 1)
    w1b, w3t = shift(w0b, "fsdp", 4, -1), shift(w0t, "fsdp", 4, 1)
    (own,) = call(stack_kernel, ids, [sig, up], [((2, 128, 1024), BF16)])
    oth = pair(own)
    w2t, w2b = shift(w1t, "fsdp", 4, -1), shift(w3b, "fsdp", 4, 1)
    weights = [w0t, w0b, w1t, w1b, w2t, w2b, w3t, w3b]
    x0 = jnp.concatenate(
        [
            jnp.where(core == 0, own[0], oth[1]),
            jnp.where(core == 0, oth[0], own[1]),
        ],
        axis=0,
    )
    r1, l1 = shift(x0, "z", 8, 1), shift(x0, "z", 8, -1)
    r2, l2 = shift(r1, "z", 8, 1), shift(l1, "z", 8, -1)
    r3, l3 = shift(r2, "z", 8, 1), shift(l2, "z", 8, -1)
    r4, l4 = shift(r3[:128], "z", 8, 1), shift(l3[128:], "z", 8, -1)
    heads, _, _ = call(
        project_kernel,
        ids,
        [own, oth] + weights,
        [((8, 256, 128), BF16), ((256, 1024), BF16), ((256, 1024), BF16)],
    )
    mine = exchange(heads, "z").reshape(2048, 128)
    other = pair(mine)
    send, keep = call(
        attention_kernel,
        ids,
        [mine, other],
        [((3072, 128), BF16), ((2048, 128), F32)],
        [pltpu.VMEM((2048, 128), BF16), pltpu.VMEM((1024, 128), BF16), pltpu.VMEM((2048, 128), F32)],
    )
    recv = pair(send)
    moved, columns = call(
        merge_kernel,
        ids,
        [keep, send, recv],
        [((2048, 128), BF16), ((2048, 256), BF16)],
    )
    grads = exchange(moved.reshape(8, 256, 128), "z")
    kept, sent = call(
        back_kernel,
        ids,
        [grads] + weights,
        [((2, 128, 1024), F32), ((2, 128, 1024), F32)],
    )
    got = pair(sent)
    out, grad = call(
        finish_kernel,
        ids,
        [sig, up, kept, got],
        [((128, 1024), BF16), ((128, 1024), BF16)],
    )
    share, foreign = call(
        outer_kernel,
        ids,
        [columns, x0, r1, l1, r2, l2, r3, l3, r4, l4],
        [((16, 32, 256), BF16), ((16, 32, 256), BF16)],
        [pltpu.VMEM((1024, 256), F32)],
    )
    share = share + pair(foreign)
    total = jnp.sum(exchange(share, ("dp", "fsdp")).astype(F32), axis=0).astype(BF16)
    total = exchange(jnp.broadcast_to(total[None], (8, 32, 256)), "z")
    total = exchange(jnp.broadcast_to(total[None], (4, 8, 32, 256)), "dp")
    across = pair(total)
    shares = call(spread_kernel, ids, [total, across], [((256, 512), F32)] * 4)
    return (out[None], grad[None], *shares)


def solution(mesh):
    dp, seq, fsdp = mesh.devices.shape
    split = Mesh(mesh.devices.reshape(dp, seq // 2, 2, fsdp), ("dp", "z", "core", "fsdp"))
    frames = P(("dp", "fsdp"), ("z", "core"), None)
    rows = P("fsdp", None)

    return jax.shard_map(
        body,
        mesh=split,
        in_specs=(frames, rows, rows, rows, rows, frames),
        out_specs=(frames, frames, rows, rows, rows, rows),
        check_vma=False,
    )
```

profile of v0, /device:TPU:2, one launch (start us, length us, event | category | flops | bytes accessed | tf_op | source)
XLA Modules:
  0.0 196.3 jit_solution(16967825919172466277)
XLA Ops:
  3.7 2.3 %collective-permute-start.1 = (bf16[128,1024]{1,0:T(8,128)(2,1)S(1)}, bf16[128,1024]{1,0:T(8,128)(2,1)S(1)}, u32[]{:S(2)}, u32[]{:S(2)}) collective-permute-start(bf16[128,1024]{1,0:T(8,128)(2,1)S(1)} %get-tuple-element.39.w0t), channel_id=1, source_target_pairs={{0,3},{1,0},{2,1},{3,2},{4,7},{5,4},{6,5},{7,6},{8,11},{9,8},{10,9... | collective-permute-start | bytes 786440 | tf_op jit(solution)/shard_map/ppermute | solution.py:51
  8.0 4.9 %collective-permute-done.1.w1t = bf16[128,1024]{1,0:T(8,128)(2,1)S(1)} collective-permute-done((bf16[128,1024]{1,0:T(8,128)(2,1)S(1)}, bf16[128,1024]{1,0:T(8,128)(2,1)S(1)}, u32[]{:S(2)}, u32[]{:S(2)}) %collective-permute-start.1) | collective-permute-done | bytes 262176 | tf_op jit(solution)/shard_map/ppermute | solution.py:51
  15.2 3.4 %collective-permute-done.2.w1b = bf16[128,1024]{1,0:T(8,128)(2,1)S(1)} collective-permute-done((bf16[128,1024]{1,0:T(8,128)(2,1)S(1)}, bf16[128,1024]{1,0:T(8,128)(2,1)S(1)}, u32[]{:S(2)}, u32[]{:S(2)}) %collective-permute-start.2) | collective-permute-done | bytes 262176 | tf_op jit(solution)/shard_map/ppermute | solution.py:51
  20.8 2.9 %collective-permute-done.3.w2t = bf16[128,1024]{1,0:T(8,128)(2,1)S(1)} collective-permute-done((bf16[128,1024]{1,0:T(8,128)(2,1)S(1)}, bf16[128,1024]{1,0:T(8,128)(2,1)S(1)}, u32[]{:S(2)}, u32[]{:S(2)}) %collective-permute-start.3) | collective-permute-done | bytes 262176 | tf_op jit(solution)/shard_map/ppermute | solution.py:51
  26.4 3.5 %shard_map.110 = (bf16[8,256,128]{2,1,0:T(8,128)(2,1)}, bf16[256,1024]{1,0:T(8,128)(2,1)}, bf16[256,1024]{1,0:T(8,128)(2,1)}) custom-call(s32[3]{0:T(128)} %pad_add_fusion.ids, bf16[2,128,1024]{2,1,0:T(8,128)(2,1)} %shard_map.109.own, bf16[2,128,1024]{2,1,0:T(8,128)(2,1)} %copy-done.5, bf16[128,1024]{1,0:T(8,128)(2,1)} %copy-done.2, ...), custom_call_target="tpu_custom_call" | custom-call | tf_op jit(solution)/shard_map/pallas_call | solution.py:25
  29.9 7.9 %all-to-all-start = ((bf16[8,256,128]{2,1,0:T(8,128)(2,1)}), bf16[8,256,128]{2,1,0:T(8,128)(2,1)S(1)}, u32[]{:S(2)}, u32[]{:S(2)}) async-start(bf16[8,256,128]{2,1,0:T(8,128)(2,1)} %get-tuple-element.21), calls=%async_computation | async-start | bytes 1048576 | tf_op jit(solution)/shard_map/all_to_all | solution.py:246
  41.3 22.3 %collective-permute-done.10.r1 = bf16[256,1024]{1,0:T(8,128)(2,1)S(1)} collective-permute-done((bf16[256,1024]{1,0:T(8,128)(2,1)S(1)}, bf16[256,1024]{1,0:T(8,128)(2,1)S(1)}, u32[]{:S(2)}, u32[]{:S(2)}) %collective-permute-start.10) | collective-permute-done | bytes 524320 | tf_op jit(solution)/shard_map/ppermute | solution.py:51
  63.7 3.2 %collective-permute-start.13 = (bf16[256,1024]{1,0:T(8,128)(2,1)S(1)}, bf16[256,1024]{1,0:T(8,128)(2,1)}, u32[]{:S(2)}, u32[]{:S(2)}) collective-permute-start(bf16[256,1024]{1,0:T(8,128)(2,1)S(1)} %collective-permute-done.11.l1), channel_id=1, source_target_pairs={{0,56},{8,0},{16,8},{24,16},{32,24},{40,32},{48,40},{56,48},{1,57}... | collective-permute-start | bytes 1572872 | tf_op jit(solution)/shard_map/ppermute | solution.py:51
  67.0 10.9 %collective-permute-done.12.r2 = bf16[256,1024]{1,0:T(8,128)(2,1)} collective-permute-done((bf16[256,1024]{1,0:T(8,128)(2,1)S(1)}, bf16[256,1024]{1,0:T(8,128)(2,1)}, u32[]{:S(2)}, u32[]{:S(2)}) %collective-permute-start.12) | collective-permute-done | bytes 524320 | tf_op jit(solution)/shard_map/ppermute | solution.py:51
  78.7 13.8 %shard_map.111 = (bf16[3072,128]{1,0:T(8,128)(2,1)}, f32[2048,128]{1,0:T(8,128)}) custom-call(s32[3]{0:T(128)} %pad_add_fusion.ids, bf16[2048,128]{1,0:T(8,128)(2,1)} %bitcast.14, bf16[2048,128]{1,0:T(8,128)(2,1)} %copy-done.19), custom_call_target="tpu_custom_call" | custom-call | tf_op jit(solution)/shard_map/pallas_call | solution.py:25
  92.4 3.3 %collective-permute-start.15 = (bf16[256,1024]{1,0:T(8,128)(2,1)}, bf16[256,1024]{1,0:T(8,128)(2,1)S(1)}, u32[]{:S(2)}, u32[]{:S(2)}) collective-permute-start(bf16[256,1024]{1,0:T(8,128)(2,1)} %collective-permute-done.13.l2), channel_id=1, source_target_pairs={{0,56},{8,0},{16,8},{24,16},{32,24},{40,32},{48,40},{56,48},{1,57}... | collective-permute-start | bytes 1572872 | tf_op jit(solution)/shard_map/ppermute | solution.py:51
  96.6 11.3 %collective-permute-done.15.l3 = bf16[256,1024]{1,0:T(8,128)(2,1)S(1)} collective-permute-done((bf16[256,1024]{1,0:T(8,128)(2,1)}, bf16[256,1024]{1,0:T(8,128)(2,1)S(1)}, u32[]{:S(2)}, u32[]{:S(2)}) %collective-permute-start.15) | collective-permute-done | bytes 524320 | tf_op jit(solution)/shard_map/ppermute | solution.py:51
  108.6 3.6 %collective-permute-start.17 = (bf16[128,1024]{1,0:T(8,128)(2,1)}, bf16[128,1024]{1,0:T(8,128)(2,1)}, u32[]{:S(2)}, u32[]{:S(2)}) collective-permute-start(bf16[128,1024]{1,0:T(8,128)(2,1)} %slice.39), channel_id=1, source_target_pairs={{0,56},{8,0},{16,8},{24,16},{32,24},{40,32},{48,40},{56,48},{1,57}... | collective-permute-start | bytes 786440 | tf_op jit(solution)/shard_map/ppermute | solution.py:51
  113.1 3.1 %shard_map.112 = (bf16[2048,128]{1,0:T(8,128)(2,1)}, bf16[2048,256]{1,0:T(8,128)(2,1)}) custom-call(s32[3]{0:T(128)} %pad_add_fusion.ids, f32[2048,128]{1,0:T(8,128)} %get-tuple-element.22.keep, bf16[3072,128]{1,0:T(8,128)(2,1)} %get-tuple-element.23.send, bf16[3072,128]{1,0:T(8,128)(2,1)} %copy-done.18), custom_call_target="tpu_custom_call" | custom-call | tf_op jit(solution)/shard_map/pallas_call | solution.py:25
  117.8 4.8 %shard_map.115 = (bf16[16,32,256]{2,1,0:T(8,128)(2,1)}, bf16[16,32,256]{2,1,0:T(8,128)(2,1)}) custom-call(s32[3]{0:T(128)} %pad_add_fusion.ids, bf16[2048,256]{1,0:T(8,128)(2,1)} %get-tuple-element.29.columns, bf16[256,1024]{1,0:T(8,128)(2,1)} %copy-done.8, bf16[256,1024]{1,0:T(8,128)(2,1)} %copy-done.21, bf16[256,1024]{1,0:T(8,128)(2,1)} %copy-done.22, ...), custom_call_target="tpu_custom_call" | custom-call | tf_op jit(solution)/shard_map/pallas_call | solution.py:25
  125.4 15.2 %all_to_all.25 = bf16[16,32,256]{2,1,0:T(8,128)(2,1)S(1)} all-to-all(bf16[16,32,256]{2,1,0:T(8,128)(2,1)S(1)} %add.3), channel_id=1, replica_groups=mesh['dp'=4,'z'=8,'core'=2,'fsdp'=4] {'dp','fsdp'}, dimensions={0} | all-to-all | bytes 524288 | tf_op jit(solution)/shard_map/all_to_all | solution.py:246
  140.6 5.8 %all-to-all-start.1 = ((bf16[8,256,128]{2,1,0:T(8,128)(2,1)}), bf16[8,256,128]{2,1,0:T(8,128)(2,1)S(1)}, u32[]{:S(2)}, u32[]{:S(2)}) async-start(bf16[8,256,128]{2,1,0:T(8,128)(2,1)} %bitcast.6), calls=%async_computation.1 | async-start | bytes 1048576 | tf_op jit(solution)/shard_map/all_to_all | solution.py:246
  146.5 16.6 %all-to-all-done.1.heads = bf16[8,256,128]{2,1,0:T(8,128)(2,1)S(1)} async-done(((bf16[8,256,128]{2,1,0:T(8,128)(2,1)}), bf16[8,256,128]{2,1,0:T(8,128)(2,1)S(1)}, u32[]{:S(2)}, u32[]{:S(2)}) %all-to-all-start.1) | async-done | bytes 524320 | tf_op jit(solution)/shard_map/all_to_all | solution.py:246
  163.8 3.4 %all-to-all-start.3 = ((bf16[8,32,256]{2,1,0:T(8,128)(2,1)}), bf16[8,32,256]{2,1,0:T(8,128)(2,1)S(1)}, u32[]{:S(2)}, u32[]{:S(2)}) async-start(bf16[8,32,256]{2,1,0:T(8,128)(2,1)} %broadcast_in_dim.20), calls=%async_computation.3 | async-start | bytes 262144 | tf_op jit(solution)/shard_map/all_to_all | solution.py:246
  167.2 3.9 %shard_map.113 = (f32[2,128,1024]{2,1,0:T(8,128)}, f32[2,128,1024]{2,1,0:T(8,128)}) custom-call(s32[3]{0:T(128)} %pad_add_fusion.ids, bf16[8,256,128]{2,1,0:T(8,128)(2,1)} %copy-done.7, bf16[128,1024]{1,0:T(8,128)(2,1)} %copy-done.2, bf16[128,1024]{1,0:T(8,128)(2,1)} %copy-done.1, bf16[128,1024]{1,0:T(8,128)(2,1)} %copy-done.12, ...), custom_call_target="tpu_custom_call" | custom-call | tf_op jit(solution)/shard_map/pallas_call | solution.py:25
  171.0 5.1 %all-to-all-done.3 = bf16[8,32,256]{2,1,0:T(8,128)(2,1)S(1)} async-done(((bf16[8,32,256]{2,1,0:T(8,128)(2,1)}), bf16[8,32,256]{2,1,0:T(8,128)(2,1)S(1)}, u32[]{:S(2)}, u32[]{:S(2)}) %all-to-all-start.3) | async-done | bytes 131104 | tf_op jit(solution)/shard_map/all_to_all | solution.py:246
  176.2 10.5 %all_to_all.26.own = bf16[4,8,32,256]{3,2,1,0:T(8,128)(2,1)S(1)} all-to-all(bf16[4,8,32,256]{3,2,1,0:T(8,128)(2,1)S(1)} %broadcast_in_dim.21), channel_id=1, replica_groups=mesh['dp'=4,'z'=8,'core'=2,'fsdp'=4] {'dp'}, dimensions={0} | all-to-all | bytes 1048576 | tf_op jit(solution)/shard_map/all_to_all | solution.py:246
  189.4 3.1 %shard_map.116 = (f32[256,512]{1,0:T(8,128)}, f32[256,512]{1,0:T(8,128)}, f32[256,512]{1,0:T(8,128)}, f32[256,512]{1,0:T(8,128)}) custom-call(s32[3]{0:T(128)} %pad_add_fusion.ids, bf16[4,8,32,256]{3,2,1,0:T(8,128)(2,1)} %copy-done.4, bf16[4,8,32,256]{3,2,1,0:T(8,128)(2,1)} %copy-done.20), custom_call_target="tpu_custom_call" | custom-call | tf_op jit(solution)/shard_map/pallas_call | solution.py:25
  193.5 2.8 %shard_map.114 = (bf16[128,1024]{1,0:T(8,128)(2,1)}, bf16[128,1024]{1,0:T(8,128)(2,1)}) custom-call(s32[3]{0:T(128)} %pad_add_fusion.ids, bf16[128,1024]{1,0:T(8,128)(2,1)} %bitcast.16, bf16[128,1024]{1,0:T(8,128)(2,1)} %bitcast.18, f32[2,128,1024]{2,1,0:T(8,128)} %get-tuple-element.25.keep, f32[2,128,1024]{2,1,0:T(8,128)} %copy-done.11), custom_call_target="tpu_custom_call" | custom-call | tf_op jit(solution)/shard_map/pallas_call | solution.py:25
  (97 shorter events, 27.9 us)
Async XLA Ops:
  3.5 17.3 %collective-permute-start = (bf16[2,128,1024]{2,1,0:T(8,128)(2,1)}, bf16[2,128,1024]{2,1,0:T(8,128)(2,1)S(1)}, u32[]{:S(2)}, u32[]{:S(2)}) collective-permute-start(bf16[2,128,1024]{2,1,0:T(8,128)(2,1)} %shard_map.109.own), channel_id=1, source_target_pairs={{0,4},{4,0},{1,5},{5,1},{2,6},{6,2},{3,7},{7,3},{8,12},{12,8},{9,1... | collective-permute-start | bytes 1572872 | tf_op jit(solution)/shard_map/ppermute | solution.py:51
  3.7 9.3 %collective-permute-start.1 = (bf16[128,1024]{1,0:T(8,128)(2,1)S(1)}, bf16[128,1024]{1,0:T(8,128)(2,1)S(1)}, u32[]{:S(2)}, u32[]{:S(2)}) collective-permute-start(bf16[128,1024]{1,0:T(8,128)(2,1)S(1)} %get-tuple-element.39.w0t), channel_id=1, source_target_pairs={{0,3},{1,0},{2,1},{3,2},{4,7},{5,4},{6,5},{7,6},{8,11},{9,8},{10,9... | collective-permute-start | bytes 786440 | tf_op jit(solution)/shard_map/ppermute | solution.py:51
  6.0 9.2 %collective-permute-start.4 = (bf16[128,1024]{1,0:T(8,128)(2,1)S(1)}, bf16[128,1024]{1,0:T(8,128)(2,1)S(1)}, u32[]{:S(2)}, u32[]{:S(2)}) collective-permute-start(bf16[128,1024]{1,0:T(8,128)(2,1)S(1)} %get-tuple-element.38.w0b), channel_id=1, source_target_pairs={{0,1},{1,2},{2,3},{3,0},{4,5},{5,6},{6,7},{7,4},{8,9},{9,10},{10,1... | collective-permute-start | bytes 786440 | tf_op jit(solution)/shard_map/ppermute | solution.py:51
  6.0 12.6 %collective-permute-start.2 = (bf16[128,1024]{1,0:T(8,128)(2,1)S(1)}, bf16[128,1024]{1,0:T(8,128)(2,1)S(1)}, u32[]{:S(2)}, u32[]{:S(2)}) collective-permute-start(bf16[128,1024]{1,0:T(8,128)(2,1)S(1)} %get-tuple-element.38.w0b), channel_id=1, source_target_pairs={{0,3},{1,0},{2,1},{3,2},{4,7},{5,4},{6,5},{7,6},{8,11},{9,8},{10,9... | collective-permute-start | bytes 786440 | tf_op jit(solution)/shard_map/ppermute | solution.py:51
  8.0 12.8 %collective-permute-start.6 = (bf16[128,1024]{1,0:T(8,128)(2,1)S(1)}, bf16[128,1024]{1,0:T(8,128)(2,1)S(1)}, u32[]{:S(2)}, u32[]{:S(2)}) collective-permute-start(bf16[128,1024]{1,0:T(8,128)(2,1)S(1)} %get-tuple-element.39.w0t), channel_id=1, source_target_pairs={{0,1},{1,2},{2,3},{3,0},{4,5},{5,6},{6,7},{7,4},{8,9},{9,10},{10,1... | collective-permute-start | bytes 786440 | tf_op jit(solution)/shard_map/ppermute | solution.py:51
  12.9 10.8 %collective-permute-start.3 = (bf16[128,1024]{1,0:T(8,128)(2,1)S(1)}, bf16[128,1024]{1,0:T(8,128)(2,1)S(1)}, u32[]{:S(2)}, u32[]{:S(2)}) collective-permute-start(bf16[128,1024]{1,0:T(8,128)(2,1)S(1)} %collective-permute-done.1.w1t), channel_id=1, source_target_pairs={{0,3},{1,0},{2,1},{3,2},{4,7},{5,4},{6,5},{7,6},{8,11},{9,8},{10,9... | collective-permute-start | bytes 786440 | tf_op jit(solution)/shard_map/ppermute | solution.py:51
  15.2 10.5 %collective-permute-start.5 = (bf16[128,1024]{1,0:T(8,128)(2,1)S(1)}, bf16[128,1024]{1,0:T(8,128)(2,1)S(1)}, u32[]{:S(2)}, u32[]{:S(2)}) collective-permute-start(bf16[128,1024]{1,0:T(8,128)(2,1)S(1)} %collective-permute-done.4.w3b), channel_id=1, source_target_pairs={{0,1},{1,2},{2,3},{3,0},{4,5},{5,6},{6,7},{7,4},{8,9},{9,10},{10,1... | collective-permute-start | bytes 786440 | tf_op jit(solution)/shard_map/ppermute | solution.py:51
  29.9 33.8 %all-to-all-start = ((bf16[8,256,128]{2,1,0:T(8,128)(2,1)}), bf16[8,256,128]{2,1,0:T(8,128)(2,1)S(1)}, u32[]{:S(2)}, u32[]{:S(2)}) async-start(bf16[8,256,128]{2,1,0:T(8,128)(2,1)} %get-tuple-element.21), calls=%async_computation | async-start | bytes 1048576 | tf_op jit(solution)/shard_map/all_to_all | solution.py:246
  37.9 78.3 %copy-start.8 = (bf16[256,1024]{1,0:T(8,128)(2,1)}, bf16[256,1024]{1,0:T(8,128)(2,1)S(1)}, u32[]{:S(2)}) copy-start(bf16[256,1024]{1,0:T(8,128)(2,1)S(1)} %pad_maximum_fusion.x0) | copy-start | bytes 1572868
  37.9 25.7 %collective-permute-start.10 = (bf16[256,1024]{1,0:T(8,128)(2,1)S(1)}, bf16[256,1024]{1,0:T(8,128)(2,1)S(1)}, u32[]{:S(2)}, u32[]{:S(2)}) collective-permute-start(bf16[256,1024]{1,0:T(8,128)(2,1)S(1)} %pad_maximum_fusion.x0), channel_id=1, source_target_pairs={{0,8},{8,16},{16,24},{24,32},{32,40},{40,48},{48,56},{56,0},{1,9},... | collective-permute-start | bytes 1572872 | tf_op jit(solution)/shard_map/ppermute | solution.py:51
  40.0 23.7 %collective-permute-start.11 = (bf16[256,1024]{1,0:T(8,128)(2,1)S(1)}, bf16[256,1024]{1,0:T(8,128)(2,1)S(1)}, u32[]{:S(2)}, u32[]{:S(2)}) collective-permute-start(bf16[256,1024]{1,0:T(8,128)(2,1)S(1)} %pad_maximum_fusion.x0), channel_id=1, source_target_pairs={{0,56},{8,0},{16,8},{24,16},{32,24},{40,32},{48,40},{56,48},{1,57}... | collective-permute-start | bytes 1572872 | tf_op jit(solution)/shard_map/ppermute | solution.py:51
  63.6 14.3 %collective-permute-start.12 = (bf16[256,1024]{1,0:T(8,128)(2,1)S(1)}, bf16[256,1024]{1,0:T(8,128)(2,1)}, u32[]{:S(2)}, u32[]{:S(2)}) collective-permute-start(bf16[256,1024]{1,0:T(8,128)(2,1)S(1)} %collective-permute-done.10.r1), channel_id=1, source_target_pairs={{0,8},{8,16},{16,24},{24,32},{32,40},{40,48},{48,56},{56,0},{1,9},... | collective-permute-start | bytes 1572872 | tf_op jit(solution)/shard_map/ppermute | solution.py:51
  63.6 14.2 %collective-permute-start.7 = (bf16[2048,128]{1,0:T(8,128)(2,1)S(1)}, bf16[2048,128]{1,0:T(8,128)(2,1)S(1)}, u32[]{:S(2)}, u32[]{:S(2)}) collective-permute-start(bf16[2048,128]{1,0:T(8,128)(2,1)S(1)} %bitcast.13), channel_id=1, source_target_pairs={{0,4},{4,0},{1,5},{5,1},{2,6},{6,2},{3,7},{7,3},{8,12},{12,8},{9,1... | collective-permute-start | bytes 1572872 | tf_op jit(solution)/shard_map/ppermute | solution.py:51
  63.7 28.7 %collective-permute-start.13 = (bf16[256,1024]{1,0:T(8,128)(2,1)S(1)}, bf16[256,1024]{1,0:T(8,128)(2,1)}, u32[]{:S(2)}, u32[]{:S(2)}) collective-permute-start(bf16[256,1024]{1,0:T(8,128)(2,1)S(1)} %collective-permute-done.11.l1), channel_id=1, source_target_pairs={{0,56},{8,0},{16,8},{24,16},{32,24},{40,32},{48,40},{56,48},{1,57}... | collective-permute-start | bytes 1572872 | tf_op jit(solution)/shard_map/ppermute | solution.py:51
  77.9 17.9 %collective-permute-start.14 = (bf16[256,1024]{1,0:T(8,128)(2,1)}, bf16[256,1024]{1,0:T(8,128)(2,1)S(1)}, u32[]{:S(2)}, u32[]{:S(2)}) collective-permute-start(bf16[256,1024]{1,0:T(8,128)(2,1)} %collective-permute-done.12.r2), channel_id=1, source_target_pairs={{0,8},{8,16},{16,24},{24,32},{32,40},{40,48},{48,56},{56,0},{1,9},... | collective-permute-start | bytes 1572872 | tf_op jit(solution)/shard_map/ppermute | solution.py:51
  92.4 19.8 %collective-permute-start.8 = (bf16[3072,128]{1,0:T(8,128)(2,1)}, bf16[3072,128]{1,0:T(8,128)(2,1)S(1)}, u32[]{:S(2)}, u32[]{:S(2)}) collective-permute-start(bf16[3072,128]{1,0:T(8,128)(2,1)} %get-tuple-element.23.send), channel_id=1, source_target_pairs={{0,4},{4,0},{1,5},{5,1},{2,6},{6,2},{3,7},{7,3},{8,12},{12,8},{9,1... | collective-permute-start | bytes 2359304 | tf_op jit(solution)/shard_map/ppermute | solution.py:51
  92.4 15.4 %collective-permute-start.15 = (bf16[256,1024]{1,0:T(8,128)(2,1)}, bf16[256,1024]{1,0:T(8,128)(2,1)S(1)}, u32[]{:S(2)}, u32[]{:S(2)}) collective-permute-start(bf16[256,1024]{1,0:T(8,128)(2,1)} %collective-permute-done.13.l2), channel_id=1, source_target_pairs={{0,56},{8,0},{16,8},{24,16},{32,24},{40,32},{48,40},{56,48},{1,57}... | collective-permute-start | bytes 1572872 | tf_op jit(solution)/shard_map/ppermute | solution.py:51
  96.5 19.7 %collective-permute-start.16 = (bf16[128,1024]{1,0:T(8,128)(2,1)}, bf16[128,1024]{1,0:T(8,128)(2,1)}, u32[]{:S(2)}, u32[]{:S(2)}) collective-permute-start(bf16[128,1024]{1,0:T(8,128)(2,1)} %slice.38), channel_id=1, source_target_pairs={{0,8},{8,16},{16,24},{24,32},{32,40},{40,48},{48,56},{56,0},{1,9},... | collective-permute-start | bytes 786440 | tf_op jit(solution)/shard_map/ppermute | solution.py:51
  108.6 9.2 %collective-permute-start.17 = (bf16[128,1024]{1,0:T(8,128)(2,1)}, bf16[128,1024]{1,0:T(8,128)(2,1)}, u32[]{:S(2)}, u32[]{:S(2)}) collective-permute-start(bf16[128,1024]{1,0:T(8,128)(2,1)} %slice.39), channel_id=1, source_target_pairs={{0,56},{8,0},{16,8},{24,16},{32,24},{40,32},{48,40},{56,48},{1,57}... | collective-permute-start | bytes 786440 | tf_op jit(solution)/shard_map/ppermute | solution.py:51
  122.6 1.7 collective-permute-start.18
  140.6 22.5 %all-to-all-start.1 = ((bf16[8,256,128]{2,1,0:T(8,128)(2,1)}), bf16[8,256,128]{2,1,0:T(8,128)(2,1)S(1)}, u32[]{:S(2)}, u32[]{:S(2)}) async-start(bf16[8,256,128]{2,1,0:T(8,128)(2,1)} %bitcast.6), calls=%async_computation.1 | async-start | bytes 1048576 | tf_op jit(solution)/shard_map/all_to_all | solution.py:246
  163.8 12.4 %all-to-all-start.3 = ((bf16[8,32,256]{2,1,0:T(8,128)(2,1)}), bf16[8,32,256]{2,1,0:T(8,128)(2,1)S(1)}, u32[]{:S(2)}, u32[]{:S(2)}) async-start(bf16[8,32,256]{2,1,0:T(8,128)(2,1)} %broadcast_in_dim.20), calls=%async_computation.3 | async-start | bytes 262144 | tf_op jit(solution)/shard_map/all_to_all | solution.py:246
  171.0 21.5 %collective-permute-start.9 = (f32[2,128,1024]{2,1,0:T(8,128)}, f32[2,128,1024]{2,1,0:T(8,128)S(1)}, u32[]{:S(2)}, u32[]{:S(2)}) collective-permute-start(f32[2,128,1024]{2,1,0:T(8,128)} %get-tuple-element.26), channel_id=1, source_target_pairs={{0,4},{4,0},{1,5},{5,1},{2,6},{6,2},{3,7},{7,3},{8,12},{12,8},{9,1... | collective-permute-start | bytes 3145736 | tf_op jit(solution)/shard_map/ppermute | solution.py:51
  186.7 1.9 collective-permute-start.19
  (26 other events, 261.5 us)
where the time goes:
time: 199 us; the launch traced here: 196 us
  waiting for transfers between devices  86.8 us (44%)
  starting transfers between devices  37.3 us (19%)
  Pallas kernels  37.1 us (19%)
  blocking collectives  25.7 us (13%)
  local copies, waits for them, and re-layouts  6.51 us (3%)
    ppermute x20, waiting for transfers between devices, shift(): lax.ppermute(value, axis, [(i, (i + by) % size) for i in range(size)])  65.1 us
    pallas_call x8, Pallas kernels, call(): pl.pallas_call(kernel, in_specs=[smem()] + vmem(len(args)), out_specs=vme...  37.1 us
    all_to_all x2, blocking collectives, exchange(): return lax.all_to_all(value, axis, split_axis=0, concat_axis=0, tiled=True)  25.7 us
    all_to_all x3, waiting for transfers between devices, exchange(): return lax.all_to_all(value, axis, split_axis=0, concat_axis=0, tiled=True)  21.7 us
    ppermute x20, starting transfers between devices, shift(): lax.ppermute(value, axis, [(i, (i + by) % size) for i in range(size)])  20.2 us
    all_to_all x3, starting transfers between devices, exchange(): return lax.all_to_all(value, axis, split_axis=0, concat_axis=0, tiled=True)  17.1 us
    unnamed x54, local copies, waits for them, and re-layouts  4.21 us
  transfers between devices with their start and end apart: 23, of which 13 were waited for; matrix products, arithmetic and copies ran while one was open for 1% of the time, Pallas kernels for 12%

commit v1 on v0

--- a/solution.py
+++ b/solution.py
@@ -21,13 +21,17 @@
     return pl.BlockSpec(memory_space=pltpu.SMEM)
 
 
-def call(kernel, ids, args, outs, scratch=()):
+def call(kernel, ids, args, outs, scratch=(), limit=12, last=False, near=True):
+    shape = jax.ShapeDtypeStruct if last else pltpu.VMEM
+    if near:
+        args = [pltpu.with_memory_space_constraint(a, pltpu.VMEM) for a in args]
     return pl.pallas_call(
         kernel,
         in_specs=[smem()] + vmem(len(args)),
         out_specs=vmem(len(outs)),
-        out_shape=[jax.ShapeDtypeStruct(s, d) for s, d in outs],
+        out_shape=[shape(s, d) for s, d in outs],
         scratch_shapes=list(scratch),
+        compiler_params=pltpu.CompilerParams(vmem_limit_bytes=limit << 20),
     )(ids, *args)
 
 
@@ -169,18 +173,17 @@
     return jnp.concatenate(one, axis=1), jnp.concatenate(two, axis=1)
 
 
-def outer_kernel(ids, columns, x0, r1, l1, r2, l2, r3, l3, r4, l4, keep, send, acc):
+def outer_kernel(ids, columns, x0, f1, b1, f2, b2, f3, b3, f4, keep, send, acc):
     core, place = ids[0], ids[2]
 
     def term(step, rows):
-        start = lax.rem(place + step, 8) * 256
+        start = lax.rem(place + jnp.where(core == 0, 8 - step, step), 8) * 256
         chunk = columns[pl.ds(pl.multiple_of(start, 256), 256), :]
         return dot(rows, chunk, ((0,), (0,)))
 
-    acc[...] = term(0, x0[...]) + term(7, r1[...]) + term(1, l1[...])
-    acc[...] += term(6, r2[...]) + term(2, l2[...])
-    acc[...] += term(5, r3[...]) + term(3, l3[...])
-    acc[...] += term(4, jnp.concatenate([r4[...], l4[...]], axis=0))
+    acc[...] = term(0, x0[...]) + term(1, f1[...]) + term(7, b1[...])
+    acc[...] += term(2, f2[...]) + term(6, b2[...])
+    acc[...] += term(3, f3[...]) + term(5, b3[...]) + term(4, f4[...])
     lane = lax.broadcasted_iota(jnp.int32, (32, 256), 1)
     mine = (lane < 192) == (core == 0)
     for part in range(4):
@@ -215,20 +218,19 @@
 
 
 def spread_kernel(ids, own, oth, gq, gk, gv, go):
-    core = ids[0]
+    core, place = ids[0], ids[3]
     mask = low_lanes((32, 128))
     scale = 32768**-0.5
-    for half in range(2):
-        for piece in range(4):
-            rows = slice(half * 128 + piece * 32, half * 128 + piece * 32 + 32)
-            for pair in range(4):
-                a, b = (
-                    jnp.where(core == half, own[piece, h], oth[piece, h]).astype(F32) * scale
-                    for h in (2 * pair, 2 * pair + 1)
-                )
-                lanes = slice(128 * pair, 128 * pair + 128)
-                for base, (low, high) in ((0, (gk, gv)), (128, (gq, go))):
-                    ta, tb = a[:, base : base + 128], b[:, base : base + 128]
+    for half, pieces in enumerate((own, oth)):
+        base = jnp.where(core == half, 0, 128)
+        for step in range(4):
+            start = base + lax.rem(place + step, 4) * 32
+            rows = pl.ds(pl.multiple_of(start, 32), 32)
+            for duo in range(4):
+                a, b = (pieces[step, h].astype(F32) * scale for h in (2 * duo, 2 * duo + 1))
+                lanes = slice(128 * duo, 128 * duo + 128)
+                for first, (low, high) in ((0, (gk, gv)), (128, (gq, go))):
+                    ta, tb = a[:, first : first + 128], b[:, first : first + 128]
                     low[rows, lanes] = jnp.where(mask, ta, pltpu.roll(tb, 64, 1))
                     high[rows, lanes] = jnp.where(mask, pltpu.roll(ta, 64, 1), tb)
 
@@ -242,13 +244,19 @@
     grad[...] = (up[...].astype(F32) + inverse * (gn - mean - normed_f * along)).astype(BF16)
 
 
+def turn(value, by):
+    perm = [(2 * i, 2 * ((i + by) % 8)) for i in range(8)]
+    perm += [(2 * i + 1, 2 * ((i - by) % 8) + 1) for i in range(8)]
+    return lax.ppermute(value, ("z", "core"), perm)
+
+
 def exchange(value, axis):
     return lax.all_to_all(value, axis, split_axis=0, concat_axis=0, tiled=True)
 
 
 def body(signal, w_query, w_key, w_value, w_output, upstream):
     core, place = lax.axis_index("core"), lax.axis_index("fsdp")
-    ids = jnp.stack([core, place, lax.axis_index("z")]).astype(jnp.int32)
+    ids = jnp.stack([core, place, lax.axis_index("z"), lax.axis_index("dp")]).astype(jnp.int32)
     sig, up = signal[0], upstream[0]
     w0 = jnp.concatenate(
         [jnp.where(core == 0, w_key, w_query), jnp.where(core == 0, w_value, w_output)], axis=1
@@ -267,10 +275,10 @@
         ],
         axis=0,
     )
-    r1, l1 = shift(x0, "z", 8, 1), shift(x0, "z", 8, -1)
-    r2, l2 = shift(r1, "z", 8, 1), shift(l1, "z", 8, -1)
-    r3, l3 = shift(r2, "z", 8, 1), shift(l2, "z", 8, -1)
-    r4, l4 = shift(r3[:128], "z", 8, 1), shift(l3[128:], "z", 8, -1)
+    f1, b1 = turn(x0, 1), turn(x0, -1)
+    f2, b2 = turn(f1, 1), turn(b1, -1)
+    f3, b3 = turn(f2, 1), turn(b2, -1)
+    f4 = turn(f3, 1)
     heads, _, _ = call(
         project_kernel,
         ids,
@@ -285,6 +293,7 @@
         [mine, other],
         [((3072, 128), BF16), ((2048, 128), F32)],
         [pltpu.VMEM((2048, 128), BF16), pltpu.VMEM((1024, 128), BF16), pltpu.VMEM((2048, 128), F32)],
+        24,
     )
     recv = pair(send)
     moved, columns = call(
@@ -292,6 +301,7 @@
         ids,
         [keep, send, recv],
         [((2048, 128), BF16), ((2048, 256), BF16)],
+        last=True,
     )
     grads = exchange(moved.reshape(8, 256, 128), "z")
     kept, sent = call(
@@ -306,20 +316,23 @@
         ids,
         [sig, up, kept, got],
         [((128, 1024), BF16), ((128, 1024), BF16)],
+        last=True,
     )
     share, foreign = call(
         outer_kernel,
         ids,
-        [columns, x0, r1, l1, r2, l2, r3, l3, r4, l4],
+        [columns, x0, f1, b1, f2, b2, f3, b3, f4],
         [((16, 32, 256), BF16), ((16, 32, 256), BF16)],
         [pltpu.VMEM((1024, 256), F32)],
+        near=False,
     )
     share = share + pair(foreign)
     total = jnp.sum(exchange(share, ("dp", "fsdp")).astype(F32), axis=0).astype(BF16)
     total = exchange(jnp.broadcast_to(total[None], (8, 32, 256)), "z")
-    total = exchange(jnp.broadcast_to(total[None], (4, 8, 32, 256)), "dp")
+    around = [total] + [shift(total, "dp", 4, -step) for step in (1, 3, 2)]
+    total = jnp.stack([around[0], around[1], around[3], around[2]])
     across = pair(total)
-    shares = call(spread_kernel, ids, [total, across], [((256, 512), F32)] * 4)
+    shares = call(spread_kernel, ids, [total, across], [((256, 512), F32)] * 4, last=True)
     return (out[None], grad[None], *shares)
 
 

time: 199 us -> 161 us (0.81)
  waiting for transfers between devices: 86.8 us -> 67.7 us
  Pallas kernels: 37.1 us -> 26 us
  blocking collectives: 25.7 us -> 15.8 us
  starting transfers between devices: 37.3 us -> 42.5 us
  local copies, waits for them, and re-layouts: 6.51 us -> 3.19 us
    ppermute x20 -> x15, waiting for transfers between devices: 65.1 us -> 23.5 us  [shift(): lax.ppermute(value, axis, [(i, (i + by) % size) for i in range(size)])]
    ppermute x0 -> x7, waiting for transfers between devices: none -> 24.9 us  [turn(): return lax.ppermute(value, ('z', 'core'), perm)]
    pallas_call x8, Pallas kernels: 37.1 us -> 26 us  [call(): pl.pallas_call(kernel, in_specs=[smem()] + vmem(len(args)), out_specs=vme...]
    ppermute x0 -> x7, starting transfers between devices: none -> 10.5 us  [turn(): return lax.ppermute(value, ('z', 'core'), perm)]
    all_to_all x2 -> x1, blocking collectives: 25.7 us -> 15.8 us  [exchange(): return lax.all_to_all(value, axis, split_axis=0, concat_axis=0, tiled=True)]
    ppermute x20 -> x15, starting transfers between devices: 20.2 us -> 10.8 us  [shift(): lax.ppermute(value, axis, [(i, (i + by) % size) for i in range(size)])]
    all_to_all x3, starting transfers between devices: 17.1 us -> 21.2 us  [exchange(): return lax.all_to_all(value, axis, split_axis=0, concat_axis=0, tiled=True)]
    all_to_all x3, waiting for transfers between devices: 21.7 us -> 19.3 us  [exchange(): return lax.all_to_all(value, axis, split_axis=0, concat_axis=0, tiled=True)]
  transfers between devices with their start and end apart: 23 -> 25, of which waited for: 13 -> 15; matrix products, arithmetic and copies ran while one was open for 1% -> 1% of each run, Pallas kernels for 12% -> 14%
where the time goes in v1:
time: 161 us; the launch traced here: 158 us
  waiting for transfers between devices  67.7 us (42%)
  starting transfers between devices  42.5 us (26%)
  Pallas kernels  26 us (16%)
  blocking collectives  15.8 us (10%)
  local copies, waits for them, and re-layouts  3.19 us (2%)
  other arithmetic  2.13 us (1%)
    pallas_call x8, Pallas kernels, call(): pl.pallas_call(kernel, in_specs=[smem()] + vmem(len(args)), out_specs=vme...  26 us
    ppermute x7, waiting for transfers between devices, turn(): return lax.ppermute(value, ('z', 'core'), perm)  24.9 us
    ppermute x15, waiting for transfers between devices, shift(): lax.ppermute(value, axis, [(i, (i + by) % size) for i in range(size)])  23.5 us
    all_to_all x3, starting transfers between devices, exchange(): return lax.all_to_all(value, axis, split_axis=0, concat_axis=0, tiled=True)  21.2 us
    all_to_all x3, waiting for transfers between devices, exchange(): return lax.all_to_all(value, axis, split_axis=0, concat_axis=0, tiled=True)  19.3 us
    all_to_all x1, blocking collectives, exchange(): return lax.all_to_all(value, axis, split_axis=0, concat_axis=0, tiled=True)  15.8 us
    ppermute x15, starting transfers between devices, shift(): lax.ppermute(value, axis, [(i, (i + by) % size) for i in range(size)])  10.8 us
    ppermute x7, starting transfers between devices, turn(): return lax.ppermute(value, ('z', 'core'), perm)  10.5 us
  transfers between devices with their start and end apart: 25, of which 15 were waited for; matrix products, arithmetic and copies ran while one was open for 1% of the time, Pallas kernels for 14%

profile of v1, /device:TPU:2, one launch (start us, length us, event | category | flops | bytes accessed | tf_op | source)
XLA Modules:
  0.0 158.1 jit_solution(17517341429141032937)
XLA Ops:
  3.9 2.3 %collective-permute-start.1 = (bf16[128,1024]{1,0:T(8,128)(2,1)S(1)}, bf16[128,1024]{1,0:T(8,128)(2,1)S(1)}, u32[]{:S(2)}, u32[]{:S(2)}) collective-permute-start(bf16[128,1024]{1,0:T(8,128)(2,1)S(1)} %get-tuple-element.39.w0t), channel_id=1, source_target_pairs={{0,3},{1,0},{2,1},{3,2},{4,7},{5,4},{6,5},{7,6},{8,11},{9,8},{10,9... | collective-permute-start | bytes 786440 | tf_op jit(solution)/shard_map/ppermute | solution.py:55
  8.3 4.9 %collective-permute-done.1.w1t = bf16[128,1024]{1,0:T(8,128)(2,1)S(1)} collective-permute-done((bf16[128,1024]{1,0:T(8,128)(2,1)S(1)}, bf16[128,1024]{1,0:T(8,128)(2,1)S(1)}, u32[]{:S(2)}, u32[]{:S(2)}) %collective-permute-start.1) | collective-permute-done | bytes 262176 | tf_op jit(solution)/shard_map/ppermute | solution.py:55
  13.2 2.2 %collective-permute-start.3 = (bf16[128,1024]{1,0:T(8,128)(2,1)S(1)}, bf16[128,1024]{1,0:T(8,128)(2,1)S(1)}, u32[]{:S(2)}, u32[]{:S(2)}) collective-permute-start(bf16[128,1024]{1,0:T(8,128)(2,1)S(1)} %collective-permute-done.1.w1t), channel_id=1, source_target_pairs={{0,3},{1,0},{2,1},{3,2},{4,7},{5,4},{6,5},{7,6},{8,11},{9,8},{10,9... | collective-permute-start | bytes 786440 | tf_op jit(solution)/shard_map/ppermute | solution.py:55
  15.4 3.4 %collective-permute-done.2.w1b = bf16[128,1024]{1,0:T(8,128)(2,1)S(1)} collective-permute-done((bf16[128,1024]{1,0:T(8,128)(2,1)S(1)}, bf16[128,1024]{1,0:T(8,128)(2,1)S(1)}, u32[]{:S(2)}, u32[]{:S(2)}) %collective-permute-start.2) | collective-permute-done | bytes 262176 | tf_op jit(solution)/shard_map/ppermute | solution.py:55
  18.8 2.2 %collective-permute-done.6.w3t = bf16[128,1024]{1,0:T(8,128)(2,1)S(1)} collective-permute-done((bf16[128,1024]{1,0:T(8,128)(2,1)S(1)}, bf16[128,1024]{1,0:T(8,128)(2,1)S(1)}, u32[]{:S(2)}, u32[]{:S(2)}) %collective-permute-start.6) | collective-permute-done | bytes 262176 | tf_op jit(solution)/shard_map/ppermute | solution.py:55
  21.0 2.6 %collective-permute-done.3.w2t = bf16[128,1024]{1,0:T(8,128)(2,1)S(1)} collective-permute-done((bf16[128,1024]{1,0:T(8,128)(2,1)S(1)}, bf16[128,1024]{1,0:T(8,128)(2,1)S(1)}, u32[]{:S(2)}, u32[]{:S(2)}) %collective-permute-start.3) | collective-permute-done | bytes 262176 | tf_op jit(solution)/shard_map/ppermute | solution.py:55
  25.7 2.2 %shard_map.110 = (bf16[8,256,128]{2,1,0:T(8,128)(2,1)}, bf16[256,1024]{1,0:T(8,128)(2,1)}, bf16[256,1024]{1,0:T(8,128)(2,1)}) custom-call(s32[4]{0:T(128)S(1)} %pad_add_fusion.ids, bf16[2,128,1024]{2,1,0:T(8,128)(2,1)S(1)} %shard_map.109.own, bf16[2,128,1024]{2,1,0:T(8,128)(2,1)S(1)} %collective-permute-done.oth, ...), custom_call_target="tpu_custom_call" | custom-call | tf_op jit(solution)/shard_map/pallas_call | solution.py:28
  27.9 7.8 %all-to-all-start = ((bf16[8,256,128]{2,1,0:T(8,128)(2,1)}), bf16[8,256,128]{2,1,0:T(8,128)(2,1)S(1)}, u32[]{:S(2)}, u32[]{:S(2)}) async-start(bf16[8,256,128]{2,1,0:T(8,128)(2,1)} %get-tuple-element.21), calls=%async_computation | async-start | bytes 1048576 | tf_op jit(solution)/shard_map/all_to_all | solution.py:254
  35.8 2.1 %collective-permute-start.10 = (bf16[256,1024]{1,0:T(8,128)(2,1)S(1)}, bf16[256,1024]{1,0:T(8,128)(2,1)S(1)}, u32[]{:S(2)}, u32[]{:S(2)}) collective-permute-start(bf16[256,1024]{1,0:T(8,128)(2,1)S(1)} %pad_maximum_fusion.x0), channel_id=1, source_target_pairs={{0,8},{8,16},{16,24},{24,32},{32,40},{40,48},{48,56},{56,0},{4,60}... | collective-permute-start | bytes 1572872 | tf_op jit(solution)/shard_map/ppermute | solution.py:250
  37.9 14.9 %all-to-all-done = bf16[8,256,128]{2,1,0:T(8,128)(2,1)S(1)} async-done(((bf16[8,256,128]{2,1,0:T(8,128)(2,1)}), bf16[8,256,128]{2,1,0:T(8,128)(2,1)S(1)}, u32[]{:S(2)}, u32[]{:S(2)}) %all-to-all-start) | async-done | bytes 524320 | tf_op jit(solution)/shard_map/all_to_all | solution.py:254
  55.7 11.9 %shard_map.111 = (bf16[3072,128]{1,0:T(8,128)(2,1)S(1)}, f32[2048,128]{1,0:T(8,128)S(1)}) custom-call(s32[4]{0:T(128)S(1)} %pad_add_fusion.ids, bf16[2048,128]{1,0:T(8,128)(2,1)S(1)} %bitcast.19, bf16[2048,128]{1,0:T(8,128)(2,1)S(1)} %collective-permute-done.7.other), custom_call_target="tpu_custom_call" | custom-call | tf_op jit(solution)/shard_map/pallas_call | solution.py:28
  68.0 3.0 %collective-permute-start.13 = (bf16[256,1024]{1,0:T(8,128)(2,1)}, bf16[256,1024]{1,0:T(8,128)(2,1)}, u32[]{:S(2)}, u32[]{:S(2)}) collective-permute-start(bf16[256,1024]{1,0:T(8,128)(2,1)} %collective-permute-done.11.b1), channel_id=1, source_target_pairs={{0,56},{8,0},{16,8},{24,16},{32,24},{40,32},{48,40},{56,48},{4,12}... | collective-permute-start | bytes 1572872 | tf_op jit(solution)/shard_map/ppermute | solution.py:250
  72.6 6.1 %all-to-all-start.1 = ((bf16[8,256,128]{2,1,0:T(8,128)(2,1)}), bf16[8,256,128]{2,1,0:T(8,128)(2,1)S(1)}, u32[]{:S(2)}, u32[]{:S(2)}) async-start(bf16[8,256,128]{2,1,0:T(8,128)(2,1)} %bitcast.7), calls=%async_computation.1 | async-start | bytes 1048576 | tf_op jit(solution)/shard_map/all_to_all | solution.py:254
  78.7 5.0 %collective-permute-done.13.b2 = bf16[256,1024]{1,0:T(8,128)(2,1)} collective-permute-done((bf16[256,1024]{1,0:T(8,128)(2,1)}, bf16[256,1024]{1,0:T(8,128)(2,1)}, u32[]{:S(2)}, u32[]{:S(2)}) %collective-permute-start.13) | collective-permute-done | bytes 524320 | tf_op jit(solution)/shard_map/ppermute | solution.py:250
  83.7 4.2 %collective-permute-start.15 = (bf16[256,1024]{1,0:T(8,128)(2,1)}, bf16[256,1024]{1,0:T(8,128)(2,1)S(1)}, u32[]{:S(2)}, u32[]{:S(2)}) collective-permute-start(bf16[256,1024]{1,0:T(8,128)(2,1)} %collective-permute-done.13.b2), channel_id=1, source_target_pairs={{0,56},{8,0},{16,8},{24,16},{32,24},{40,32},{48,40},{56,48},{4,12}... | collective-permute-start | bytes 1572872 | tf_op jit(solution)/shard_map/ppermute | solution.py:250
  87.8 17.8 %collective-permute-done.15.b3 = bf16[256,1024]{1,0:T(8,128)(2,1)S(1)} collective-permute-done((bf16[256,1024]{1,0:T(8,128)(2,1)}, bf16[256,1024]{1,0:T(8,128)(2,1)S(1)}, u32[]{:S(2)}, u32[]{:S(2)}) %collective-permute-start.15) | collective-permute-done | bytes 524320 | tf_op jit(solution)/shard_map/ppermute | solution.py:250
  106.2 3.1 %shard_map.115 = (bf16[16,32,256]{2,1,0:T(8,128)(2,1)S(1)}, bf16[16,32,256]{2,1,0:T(8,128)(2,1)S(1)}) custom-call(s32[4]{0:T(128)S(1)} %pad_add_fusion.ids, bf16[2048,256]{1,0:T(8,128)(2,1)S(1)} %get-tuple-element.29.columns, bf16[256,1024]{1,0:T(8,128)(2,1)S(1)} %pad_maximum_fusion.x0, bf16[256,1024]{1,0:T(8,128)(2,1)S(1)} %copy-done.15, ...), custom_call_target="tpu_custom_call" | custom-call | tf_op jit(solution)/shard_map/pallas_call | solution.py:28
  111.7 7.3 %all-to-all-start.2 = ((bf16[16,32,256]{2,1,0:T(8,128)(2,1)}), bf16[16,32,256]{2,1,0:T(8,128)(2,1)}, u32[]{:S(2)}, u32[]{:S(2)}) async-start(bf16[16,32,256]{2,1,0:T(8,128)(2,1)} %add.3), calls=%async_computation.2 | async-start | bytes 524288 | tf_op jit(solution)/shard_map/all_to_all | solution.py:254
  119.9 2.4 %shard_map.113 = (f32[2,128,1024]{2,1,0:T(8,128)S(1)}, f32[2,128,1024]{2,1,0:T(8,128)}) custom-call(s32[4]{0:T(128)S(1)} %pad_add_fusion.ids, bf16[8,256,128]{2,1,0:T(8,128)(2,1)S(1)} %all-to-all-done.1.heads, bf16[128,1024]{1,0:T(8,128)(2,1)S(1)} %get-tuple-element.39.w0t, bf16[128,1024]{1,0:T(8,128)(2,1)S(1)} %get-tuple-element.38.w0b, ...), custom_call_target="tpu_custom_call" | custom-call | tf_op jit(solution)/shard_map/pallas_call | solution.py:28
  122.3 4.3 %all-to-all-done.2 = bf16[16,32,256]{2,1,0:T(8,128)(2,1)} async-done(((bf16[16,32,256]{2,1,0:T(8,128)(2,1)}), bf16[16,32,256]{2,1,0:T(8,128)(2,1)}, u32[]{:S(2)}, u32[]{:S(2)}) %all-to-all-start.2) | async-done | bytes 262176 | tf_op jit(solution)/shard_map/all_to_all | solution.py:254
  127.7 15.8 %all_to_all.20 = bf16[8,32,256]{2,1,0:T(8,128)(2,1)S(1)} all-to-all(bf16[8,32,256]{2,1,0:T(8,128)(2,1)S(1)} %broadcast_in_dim.14), channel_id=1, replica_groups=mesh['dp'=4,'z'=8,'core'=2,'fsdp'=4] {'z'}, dimensions={0} | all-to-all | bytes 262144 | tf_op jit(solution)/shard_map/all_to_all | solution.py:254
  143.5 2.3 %collective-permute-start.19 = (bf16[8,32,256]{2,1,0:T(8,128)(2,1)S(1)}, bf16[8,32,256]{2,1,0:T(8,128)(2,1)S(1)}, u32[]{:S(2)}, u32[]{:S(2)}) collective-permute-start(bf16[8,32,256]{2,1,0:T(8,128)(2,1)S(1)} %all_to_all.20), channel_id=1, source_target_pairs={{0,128},{64,192},{128,0},{192,64},{1,129},{65,193},{129,1},{193,65... | collective-permute-start | bytes 393224 | tf_op jit(solution)/shard_map/ppermute | solution.py:55
  146.9 4.1 %collective-permute-done.20 = bf16[8,32,256]{2,1,0:T(8,128)(2,1)S(1)} collective-permute-done((bf16[8,32,256]{2,1,0:T(8,128)(2,1)S(1)}, bf16[8,32,256]{2,1,0:T(8,128)(2,1)S(1)}, u32[]{:S(2)}, u32[]{:S(2)}) %collective-permute-start.20) | collective-permute-done | bytes 131104 | tf_op jit(solution)/shard_map/ppermute | solution.py:55
  154.0 2.4 %shard_map.116 = (f32[256,512]{1,0:T(8,128)}, f32[256,512]{1,0:T(8,128)}, f32[256,512]{1,0:T(8,128)}, f32[256,512]{1,0:T(8,128)}) custom-call(s32[4]{0:T(128)S(1)} %pad_add_fusion.ids, bf16[4,8,32,256]{3,2,1,0:T(8,128)(2,1)S(1)} %pad_maximum_fusion.1.own, bf16[4,8,32,256]{3,2,1,0:T(8,128)(2,1)S(1)} %collective-permute-done.21.oth), custom_call_target="tpu_custom_call" | custom-call | tf_op jit(solution)/shard_map/pallas_call | solution.py:28
  (84 shorter events, 22.9 us)
Async XLA Ops:
  3.4 17.6 %collective-permute-start = (bf16[2,128,1024]{2,1,0:T(8,128)(2,1)S(1)}, bf16[2,128,1024]{2,1,0:T(8,128)(2,1)S(1)}, u32[]{:S(2)}, u32[]{:S(2)}) collective-permute-start(bf16[2,128,1024]{2,1,0:T(8,128)(2,1)S(1)} %shard_map.109.own), channel_id=1, source_target_pairs={{0,4},{4,0},{1,5},{5,1},{2,6},{6,2},{3,7},{7,3},{8,12},{12,8},{9,1... | collective-permute-start | bytes 1572872 | tf_op jit(solution)/shard_map/ppermute | solution.py:55
  3.9 9.3 %collective-permute-start.1 = (bf16[128,1024]{1,0:T(8,128)(2,1)S(1)}, bf16[128,1024]{1,0:T(8,128)(2,1)S(1)}, u32[]{:S(2)}, u32[]{:S(2)}) collective-permute-start(bf16[128,1024]{1,0:T(8,128)(2,1)S(1)} %get-tuple-element.39.w0t), channel_id=1, source_target_pairs={{0,3},{1,0},{2,1},{3,2},{4,7},{5,4},{6,5},{7,6},{8,11},{9,8},{10,9... | collective-permute-start | bytes 786440 | tf_op jit(solution)/shard_map/ppermute | solution.py:55
  6.2 9.2 %collective-permute-start.4 = (bf16[128,1024]{1,0:T(8,128)(2,1)S(1)}, bf16[128,1024]{1,0:T(8,128)(2,1)S(1)}, u32[]{:S(2)}, u32[]{:S(2)}) collective-permute-start(bf16[128,1024]{1,0:T(8,128)(2,1)S(1)} %get-tuple-element.38.w0b), channel_id=1, source_target_pairs={{0,1},{1,2},{2,3},{3,0},{4,5},{5,6},{6,7},{7,4},{8,9},{9,10},{10,1... | collective-permute-start | bytes 786440 | tf_op jit(solution)/shard_map/ppermute | solution.py:55
  6.3 12.5 %collective-permute-start.2 = (bf16[128,1024]{1,0:T(8,128)(2,1)S(1)}, bf16[128,1024]{1,0:T(8,128)(2,1)S(1)}, u32[]{:S(2)}, u32[]{:S(2)}) collective-permute-start(bf16[128,1024]{1,0:T(8,128)(2,1)S(1)} %get-tuple-element.38.w0b), channel_id=1, source_target_pairs={{0,3},{1,0},{2,1},{3,2},{4,7},{5,4},{6,5},{7,6},{8,11},{9,8},{10,9... | collective-permute-start | bytes 786440 | tf_op jit(solution)/shard_map/ppermute | solution.py:55
  8.3 12.8 %collective-permute-start.6 = (bf16[128,1024]{1,0:T(8,128)(2,1)S(1)}, bf16[128,1024]{1,0:T(8,128)(2,1)S(1)}, u32[]{:S(2)}, u32[]{:S(2)}) collective-permute-start(bf16[128,1024]{1,0:T(8,128)(2,1)S(1)} %get-tuple-element.39.w0t), channel_id=1, source_target_pairs={{0,1},{1,2},{2,3},{3,0},{4,5},{5,6},{6,7},{7,4},{8,9},{9,10},{10,1... | collective-permute-start | bytes 786440 | tf_op jit(solution)/shard_map/ppermute | solution.py:55
  13.2 10.5 %collective-permute-start.3 = (bf16[128,1024]{1,0:T(8,128)(2,1)S(1)}, bf16[128,1024]{1,0:T(8,128)(2,1)S(1)}, u32[]{:S(2)}, u32[]{:S(2)}) collective-permute-start(bf16[128,1024]{1,0:T(8,128)(2,1)S(1)} %collective-permute-done.1.w1t), channel_id=1, source_target_pairs={{0,3},{1,0},{2,1},{3,2},{4,7},{5,4},{6,5},{7,6},{8,11},{9,8},{10,9... | collective-permute-start | bytes 786440 | tf_op jit(solution)/shard_map/ppermute | solution.py:55
  15.4 10.2 %collective-permute-start.5 = (bf16[128,1024]{1,0:T(8,128)(2,1)S(1)}, bf16[128,1024]{1,0:T(8,128)(2,1)S(1)}, u32[]{:S(2)}, u32[]{:S(2)}) collective-permute-start(bf16[128,1024]{1,0:T(8,128)(2,1)S(1)} %collective-permute-done.4.w3b), channel_id=1, source_target_pairs={{0,1},{1,2},{2,3},{3,0},{4,5},{5,6},{6,7},{7,4},{8,9},{9,10},{10,1... | collective-permute-start | bytes 786440 | tf_op jit(solution)/shard_map/ppermute | solution.py:55
  27.9 24.9 %all-to-all-start = ((bf16[8,256,128]{2,1,0:T(8,128)(2,1)}), bf16[8,256,128]{2,1,0:T(8,128)(2,1)S(1)}, u32[]{:S(2)}, u32[]{:S(2)}) async-start(bf16[8,256,128]{2,1,0:T(8,128)(2,1)} %get-tuple-element.21), calls=%async_computation | async-start | bytes 1048576 | tf_op jit(solution)/shard_map/all_to_all | solution.py:254
  35.8 19.9 %collective-permute-start.10 = (bf16[256,1024]{1,0:T(8,128)(2,1)S(1)}, bf16[256,1024]{1,0:T(8,128)(2,1)S(1)}, u32[]{:S(2)}, u32[]{:S(2)}) collective-permute-start(bf16[256,1024]{1,0:T(8,128)(2,1)S(1)} %pad_maximum_fusion.x0), channel_id=1, source_target_pairs={{0,8},{8,16},{16,24},{24,32},{32,40},{40,48},{48,56},{56,0},{4,60}... | collective-permute-start | bytes 1572872 | tf_op jit(solution)/shard_map/ppermute | solution.py:250
  52.8 2.8 %collective-permute-start.7 = (bf16[2048,128]{1,0:T(8,128)(2,1)S(1)}, bf16[2048,128]{1,0:T(8,128)(2,1)S(1)}, u32[]{:S(2)}, u32[]{:S(2)}) collective-permute-start(bf16[2048,128]{1,0:T(8,128)(2,1)S(1)} %bitcast.18), channel_id=1, source_target_pairs={{0,4},{4,0},{1,5},{5,1},{2,6},{6,2},{3,7},{7,3},{8,12},{12,8},{9,1... | collective-permute-start | bytes 1572872 | tf_op jit(solution)/shard_map/ppermute | solution.py:55
  52.8 15.2 %collective-permute-start.11 = (bf16[256,1024]{1,0:T(8,128)(2,1)S(1)}, bf16[256,1024]{1,0:T(8,128)(2,1)}, u32[]{:S(2)}, u32[]{:S(2)}) collective-permute-start(bf16[256,1024]{1,0:T(8,128)(2,1)S(1)} %pad_maximum_fusion.x0), channel_id=1, source_target_pairs={{0,56},{8,0},{16,8},{24,16},{32,24},{40,32},{48,40},{56,48},{4,12}... | collective-permute-start | bytes 1572872 | tf_op jit(solution)/shard_map/ppermute | solution.py:250
  55.7 15.3 %collective-permute-start.12 = (bf16[256,1024]{1,0:T(8,128)(2,1)S(1)}, bf16[256,1024]{1,0:T(8,128)(2,1)}, u32[]{:S(2)}, u32[]{:S(2)}) collective-permute-start(bf16[256,1024]{1,0:T(8,128)(2,1)S(1)} %collective-permute-done.10.f1), channel_id=1, source_target_pairs={{0,8},{8,16},{16,24},{24,32},{32,40},{40,48},{48,56},{56,0},{4,60}... | collective-permute-start | bytes 1572872 | tf_op jit(solution)/shard_map/ppermute | solution.py:250
  67.6 3.4 %collective-permute-start.8 = (bf16[3072,128]{1,0:T(8,128)(2,1)S(1)}, bf16[3072,128]{1,0:T(8,128)(2,1)S(1)}, u32[]{:S(2)}, u32[]{:S(2)}) collective-permute-start(bf16[3072,128]{1,0:T(8,128)(2,1)S(1)} %get-tuple-element.23.send), channel_id=1, source_target_pairs={{0,4},{4,0},{1,5},{5,1},{2,6},{6,2},{3,7},{7,3},{8,12},{12,8},{9,1... | collective-permute-start | bytes 2359304 | tf_op jit(solution)/shard_map/ppermute | solution.py:55
  68.0 15.7 %collective-permute-start.13 = (bf16[256,1024]{1,0:T(8,128)(2,1)}, bf16[256,1024]{1,0:T(8,128)(2,1)}, u32[]{:S(2)}, u32[]{:S(2)}) collective-permute-start(bf16[256,1024]{1,0:T(8,128)(2,1)} %collective-permute-done.11.b1), channel_id=1, source_target_pairs={{0,56},{8,0},{16,8},{24,16},{32,24},{40,32},{48,40},{56,48},{4,12}... | collective-permute-start | bytes 1572872 | tf_op jit(solution)/shard_map/ppermute | solution.py:250
  71.0 16.9 %collective-permute-start.14 = (bf16[256,1024]{1,0:T(8,128)(2,1)}, bf16[256,1024]{1,0:T(8,128)(2,1)}, u32[]{:S(2)}, u32[]{:S(2)}) collective-permute-start(bf16[256,1024]{1,0:T(8,128)(2,1)} %collective-permute-done.12.f2), channel_id=1, source_target_pairs={{0,8},{8,16},{16,24},{24,32},{32,40},{40,48},{48,56},{56,0},{4,60}... | collective-permute-start | bytes 1572872 | tf_op jit(solution)/shard_map/ppermute | solution.py:250
  72.6 39.1 %all-to-all-start.1 = ((bf16[8,256,128]{2,1,0:T(8,128)(2,1)}), bf16[8,256,128]{2,1,0:T(8,128)(2,1)S(1)}, u32[]{:S(2)}, u32[]{:S(2)}) async-start(bf16[8,256,128]{2,1,0:T(8,128)(2,1)} %bitcast.7), calls=%async_computation.1 | async-start | bytes 1048576 | tf_op jit(solution)/shard_map/all_to_all | solution.py:254
  83.7 21.9 %collective-permute-start.15 = (bf16[256,1024]{1,0:T(8,128)(2,1)}, bf16[256,1024]{1,0:T(8,128)(2,1)S(1)}, u32[]{:S(2)}, u32[]{:S(2)}) collective-permute-start(bf16[256,1024]{1,0:T(8,128)(2,1)} %collective-permute-done.13.b2), channel_id=1, source_target_pairs={{0,56},{8,0},{16,8},{24,16},{32,24},{40,32},{48,40},{56,48},{4,12}... | collective-permute-start | bytes 1572872 | tf_op jit(solution)/shard_map/ppermute | solution.py:250
  87.8 18.3 %collective-permute-start.16 = (bf16[256,1024]{1,0:T(8,128)(2,1)}, bf16[256,1024]{1,0:T(8,128)(2,1)S(1)}, u32[]{:S(2)}, u32[]{:S(2)}) collective-permute-start(bf16[256,1024]{1,0:T(8,128)(2,1)} %collective-permute-done.14.f3), channel_id=1, source_target_pairs={{0,8},{8,16},{16,24},{24,32},{32,40},{40,48},{48,56},{56,0},{4,60}... | collective-permute-start | bytes 1572872 | tf_op jit(solution)/shard_map/ppermute | solution.py:250
  111.7 15.0 %all-to-all-start.2 = ((bf16[16,32,256]{2,1,0:T(8,128)(2,1)}), bf16[16,32,256]{2,1,0:T(8,128)(2,1)}, u32[]{:S(2)}, u32[]{:S(2)}) async-start(bf16[16,32,256]{2,1,0:T(8,128)(2,1)} %add.3), calls=%async_computation.2 | async-start | bytes 524288 | tf_op jit(solution)/shard_map/all_to_all | solution.py:254
  122.3 34.1 %collective-permute-start.9 = (f32[2,128,1024]{2,1,0:T(8,128)}, f32[2,128,1024]{2,1,0:T(8,128)S(1)}, u32[]{:S(2)}, u32[]{:S(2)}) collective-permute-start(f32[2,128,1024]{2,1,0:T(8,128)} %get-tuple-element.26), channel_id=1, source_target_pairs={{0,4},{4,0},{1,5},{5,1},{2,6},{6,2},{3,7},{7,3},{8,12},{12,8},{9,1... | collective-permute-start | bytes 3145736 | tf_op jit(solution)/shard_map/ppermute | solution.py:55
  143.4 7.6 %collective-permute-start.20 = (bf16[8,32,256]{2,1,0:T(8,128)(2,1)S(1)}, bf16[8,32,256]{2,1,0:T(8,128)(2,1)S(1)}, u32[]{:S(2)}, u32[]{:S(2)}) collective-permute-start(bf16[8,32,256]{2,1,0:T(8,128)(2,1)S(1)} %all_to_all.20), channel_id=1, source_target_pairs={{0,64},{64,128},{128,192},{192,0},{1,65},{65,129},{129,193},{193,1... | collective-permute-start | bytes 393224 | tf_op jit(solution)/shard_map/ppermute | solution.py:55
  143.5 7.6 %collective-permute-start.19 = (bf16[8,32,256]{2,1,0:T(8,128)(2,1)S(1)}, bf16[8,32,256]{2,1,0:T(8,128)(2,1)S(1)}, u32[]{:S(2)}, u32[]{:S(2)}) collective-permute-start(bf16[8,32,256]{2,1,0:T(8,128)(2,1)S(1)} %all_to_all.20), channel_id=1, source_target_pairs={{0,128},{64,192},{128,0},{192,64},{1,129},{65,193},{129,1},{193,65... | collective-permute-start | bytes 393224 | tf_op jit(solution)/shard_map/ppermute | solution.py:55
  145.8 6.2 %collective-permute-start.18 = (bf16[8,32,256]{2,1,0:T(8,128)(2,1)S(1)}, bf16[8,32,256]{2,1,0:T(8,128)(2,1)S(1)}, u32[]{:S(2)}, u32[]{:S(2)}) collective-permute-start(bf16[8,32,256]{2,1,0:T(8,128)(2,1)S(1)} %all_to_all.20), channel_id=1, source_target_pairs={{0,192},{64,0},{128,64},{192,128},{1,193},{65,1},{129,65},{193,129... | collective-permute-start | bytes 393224 | tf_op jit(solution)/shard_map/ppermute | solution.py:55
  152.0 2.0 %collective-permute-start.21 = (bf16[4,8,32,256]{3,2,1,0:T(8,128)(2,1)S(1)}, bf16[4,8,32,256]{3,2,1,0:T(8,128)(2,1)S(1)}, u32[]{:S(2)}, u32[]{:S(2)}) collective-permute-start(bf16[4,8,32,256]{3,2,1,0:T(8,128)(2,1)S(1)} %pad_maximum_fusion.1.own), channel_id=1, source_target_pairs={{0,4},{4,0},{1,5},{5,1},{2,6},{6,2},{3,7},{7,3},{8,12},{12,8},{9,1... | collective-permute-start | bytes 1572872 | tf_op jit(solution)/shard_map/ppermute | solution.py:55
  (21 other events, 128.8 us)

commit v2 on v1

v2 whole, which is shorter than its diff:
```python
import jax
import jax.numpy as jnp
from jax import lax
from jax.experimental import pallas as pl
from jax.experimental.pallas import tpu as pltpu
from jax.sharding import Mesh
from jax.sharding import PartitionSpec as P


HSIZE = 64
LOG2E = 1.4426950408889634
F32 = jnp.float32
BF16 = jnp.bfloat16


def vmem(count):
    return [pl.BlockSpec(memory_space=pltpu.VMEM) for _ in range(count)]


def smem():
    return pl.BlockSpec(memory_space=pltpu.SMEM)


def call(kernel, ids, args, outs, scratch=(), limit=12, shape=pltpu.VMEM, far=()):
    spaces = [pltpu.VMEM] * len(args) + [pltpu.HBM] * len(far)
    args = [pltpu.with_memory_space_constraint(a, m) for a, m in zip([*args, *far], spaces)]
    return pl.pallas_call(
        kernel,
        in_specs=[smem()] + vmem(len(args)),
        out_specs=vmem(len(outs)),
        out_shape=[shape(s, d) for s, d in outs],
        scratch_shapes=list(scratch),
        compiler_params=pltpu.CompilerParams(vmem_limit_bytes=limit << 20),
    )(ids, *args)


def normalize(rows):
    wide = rows.astype(F32)
    centre = wide - jnp.mean(wide, axis=-1, keepdims=True)
    variance = jnp.mean(centre * centre, axis=-1, keepdims=True)
    inverse = lax.rsqrt(variance + 1e-05)
    return centre * inverse, inverse


def dot(a, b, dims):
    return lax.dot_general(a, b, (dims, ((), ())), preferred_element_type=F32)


def low_lanes(shape):
    return lax.broadcasted_iota(jnp.int32, shape, len(shape) - 1) < HSIZE


def shift(value, axis, size, by):
    return lax.ppermute(value, axis, [(i, (i + by) % size) for i in range(size)])


def pair(value):
    return shift(value, "core", 2, 1)


def block_of(ids, step):
    return pl.multiple_of(lax.rem(ids[1] + step, 4) * 256, 256)


def stack_kernel(ids, sig, up, both):
    both[0] = normalize(sig[...])[0].astype(BF16)
    both[1] = up[...]


def whole_weights(ids, pieces, whole):
    upper = pl.multiple_of(lax.rem(ids[3], 2) * 128, 128)
    lower = pl.multiple_of(128 - upper, 128)
    for step in range(4):
        whole[step, pl.ds(upper, 128), :] = pieces[2 * step][...]
        whole[step, pl.ds(lower, 128), :] = pieces[2 * step + 1][...]


def project_kernel(ids, own, oth, *refs):
    pieces, (heads, first, second, whole) = refs[:8], refs[8:]
    core = ids[0]
    whole_weights(ids, pieces, whole)
    for half, both in enumerate((own, oth)):
        at = core if half == 0 else 1 - core
        rows = pl.ds(pl.multiple_of(at * 128, 128), 128)
        first[rows, :] = both[0]
        second[rows, :] = jnp.where(core == 0, both[0], both[1])
    one = two = None
    for step in range(4):
        cols = pl.ds(block_of(ids, step), 256)
        a = dot(first[:, cols], whole[step, :, :512], ((1,), (0,)))
        b = dot(second[:, cols], whole[step, :, 512:], ((1,), (0,)))
        one = a if one is None else one + a
        two = b if two is None else two + b
    mask = low_lanes((256, 128))
    for pair in range(4):
        lanes = slice(128 * pair, 128 * pair + 128)
        t1, t2 = one[:, lanes], two[:, lanes]
        heads[2 * pair] = jnp.where(mask, t1, pltpu.roll(t2, 64, 1)).astype(BF16)
        heads[2 * pair + 1] = jnp.where(mask, pltpu.roll(t1, 64, 1), t2).astype(BF16)


def attend(kv, qg, turned_kv, acc, part, blocks):
    keys, block = kv.shape[0], 256
    low = low_lanes((keys, 128))
    zero = jnp.zeros((), BF16)
    pairs = kv[...]
    key_rows = jnp.where(low, pairs, zero)
    value_rows = jnp.where(low, zero, pairs)
    upper = lax.broadcasted_iota(jnp.int32, (128, keys), 0) < HSIZE
    columns = turned_kv[...]
    key_cols = jnp.where(upper, columns, zero)
    value_cols = jnp.where(upper, zero, columns)
    low_q = low_lanes((block, 128))
    scale = jnp.where(low_lanes((1, 128)), HSIZE**-0.5, 1.0).astype(F32)

    def step(i, carry):
        start = pl.multiple_of(i * block, block)
        qb = qg[pl.ds(start, block), :]
        s = dot(key_rows, qb, ((1,), (1,)))
        top = jnp.max(s, axis=0, keepdims=True)
        e = jnp.exp2((s - top) * (HSIZE**-0.5 * LOG2E))
        inv = 1.0 / jnp.sum(e, axis=0, keepdims=True)
        att = e * inv
        grad = dot(value_rows, qb, ((1,), (1,)))
        delta = jnp.sum(att * grad, axis=0, keepdims=True)
        weights = att.astype(BF16)
        gs = (att * (grad - delta)).astype(BF16)
        qk = jnp.where(low_q, qb, zero)
        qv = jnp.where(low_q, zero, qb)
        acc[...] += dot(gs, qk, ((1,), (0,))) + dot(weights, qv, ((1,), (0,)))
        turned = dot(key_cols, gs, ((1,), (0,))) + dot(value_cols, weights, ((1,), (0,)))
        part[pl.ds(start, block), :] = (turned.T * scale).astype(BF16)
        return carry

    lax.fori_loop(*blocks, step, 0)
    return scale


def attention_kernel(ids, own, other, send, keep, kv, qg, turned_kv, part):
    core, keys = ids[0], kv.shape[0]

    @pl.when(core == 0)
    def _():
        kv[...] = own[...]
        qg[...] = other[0:1024, :]

    @pl.when(core != 0)
    def _():
        kv[...] = other[...]
        qg[...] = own[1024:2048, :]

    turned_kv[...] = kv[...].astype(F32).T.astype(BF16)
    keep[...] = jnp.zeros_like(keep)
    scale = attend(kv, qg, turned_kv, keep, part, (0, 4))
    total = keep[...] * scale
    keep[...] = total
    send[0:keys, :] = total.astype(BF16)
    send[keys:, :] = part[...]


def merge_kernel(ids, keep, send, recv, moved, columns):
    core = ids[0]
    keys = keep.shape[0]
    half = keys // 2
    kv = (keep[...] + recv[0:keys, :].astype(F32)).astype(BF16)
    own, oth = send[keys:, :], recv[keys:, :]
    low = jnp.where(core == 0, own, oth)
    high = jnp.where(core == 0, oth, own)
    columns[:, 0:128] = kv
    columns[0:half, 128:256] = low
    columns[half:keys, 128:256] = high
    moved[0:half, :] = jnp.where(core == 0, kv[0:half], low)
    moved[half:keys, :] = jnp.where(core == 0, kv[half:keys], high)


def unpack(heads):
    mask = low_lanes((256, 128))
    one, two = [], []
    for pair in range(4):
        a, b = heads[2 * pair].astype(F32), heads[2 * pair + 1].astype(F32)
        one.append(jnp.where(mask, a, pltpu.roll(b, 64, 1)).astype(BF16))
        two.append(jnp.where(mask, pltpu.roll(a, 64, 1), b).astype(BF16))
    return jnp.concatenate(one, axis=1), jnp.concatenate(two, axis=1)


def outer_kernel(ids, columns, x0, f1, b1, f2, b2, f3, b3, f4, keep, send, acc_n, acc_u):
    core, place = ids[0], ids[2]

    def chunk(step):
        block = lax.rem(place + jnp.where(core == 0, 8 - step, step), 8)
        start = block * 256 + core * 128
        return columns[pl.ds(pl.multiple_of(start, 128), 128), :]

    for index, (low, high, a, b) in enumerate(
        ((0, 4, x0, f4), (1, 7, f1, b1), (2, 6, f2, b2), (3, 5, f3, b3))
    ):
        rows = jnp.concatenate([chunk(low), chunk(high)], axis=0)
        normed = jnp.concatenate([a[0], b[0]], axis=0)
        frames = jnp.concatenate([a[1], b[1]], axis=0)
        n, u = dot(normed, rows, ((0,), (0,))), dot(frames, rows[:, 128:], ((0,), (0,)))
        acc_n[...] = n if index == 0 else acc_n[...] + n
        acc_u[...] = u if index == 0 else acc_u[...] + u
    mask = low_lanes((128, 128))
    for step in range(4):
        base = block_of(ids, step)
        for half in range(2):
            rows = pl.ds(pl.multiple_of(base + half * 128, 128), 128)
            upper = jnp.where(mask, acc_n[rows, 128:], acc_u[rows, :])
            value = jnp.concatenate([acc_n[rows, :128], upper], axis=1)

            @pl.when(core == half)
            def _():
                keep[step] = value

            @pl.when(core != half)
            def _():
                send[step] = value.astype(BF16)


def back_kernel(ids, heads, *refs):
    pieces, (keep, send, whole) = refs[:8], refs[8:]
    core = ids[0]
    one, two = unpack(heads)
    whole_weights(ids, pieces, whole)
    for step in range(4):
        cols = pl.ds(block_of(ids, step), 256)
        a = dot(one, whole[step, :, :512], ((1,), (1,)))
        b = dot(two, whole[step, :, 512:], ((1,), (1,)))
        total = jnp.where(core == 0, a + b, a)
        extra = jnp.where(core == 0, 0.0, b)
        keep[0, :, cols] = jnp.where(core == 0, total[:128], total[128:])
        keep[1, :, cols] = jnp.where(core == 0, extra[:128], extra[128:])
        send[0, :, cols] = jnp.where(core == 0, total[128:], total[:128])
        send[1, :, cols] = jnp.where(core == 0, extra[128:], extra[:128])


def spread_kernel(ids, own, oth, gq, gk, gv, go):
    core = ids[0]
    mask = low_lanes((128, 128))
    scale = 32768**-0.5
    for half, pieces in enumerate((own, oth)):
        start = jnp.where(core == half, 0, 128)
        rows = pl.ds(pl.multiple_of(start, 128), 128)
        for duo in range(4):
            a, b = (pieces[h].astype(F32) * scale for h in (2 * duo, 2 * duo + 1))
            lanes = slice(128 * duo, 128 * duo + 128)
            for first, (low, high) in ((0, (gk, gv)), (128, (gq, go))):
                ta, tb = a[:, first : first + 128], b[:, first : first + 128]
                low[rows, lanes] = jnp.where(mask, ta, pltpu.roll(tb, 64, 1))
                high[rows, lanes] = jnp.where(mask, pltpu.roll(ta, 64, 1), tb)


def finish_kernel(ids, sig, up, keep, recv, out, grad):
    normed_f, inverse = normalize(sig[...])
    out[...] = (sig[...].astype(F32) + keep[1] + recv[1]).astype(BF16)
    gn = keep[0] + recv[0]
    mean = jnp.mean(gn, axis=-1, keepdims=True)
    along = jnp.mean(gn * normed_f, axis=-1, keepdims=True)
    grad[...] = (up[...].astype(F32) + inverse * (gn - mean - normed_f * along)).astype(BF16)


def turn(value, by):
    perm = [(2 * i, 2 * ((i + by) % 8)) for i in range(8)]
    perm += [(2 * i + 1, 2 * ((i - by) % 8) + 1) for i in range(8)]
    return lax.ppermute(value, ("z", "core"), perm)


def exchange(value, axis):
    return lax.all_to_all(value, axis, split_axis=0, concat_axis=0, tiled=True)


def body(signal, w_query, w_key, w_value, w_output, upstream):
    core, place = lax.axis_index("core"), lax.axis_index("fsdp")
    ids = jnp.stack([core, place, lax.axis_index("z"), lax.axis_index("dp")]).astype(jnp.int32)
    sig, up = signal[0], upstream[0]
    w0 = jnp.concatenate(
        [jnp.where(core == 0, w_key, w_query), jnp.where(core == 0, w_value, w_output)], axis=1
    )
    even = lax.rem(lax.axis_index("dp"), 2) == 0
    w0a = jnp.where(even, w0[:128], w0[128:])
    w0b = jnp.where(even, w0[128:], w0[:128])
    w1a, w3b = shift(w0a, "fsdp", 4, -1), shift(w0b, "fsdp", 4, 1)
    (own,) = call(stack_kernel, ids, [sig, up], [((2, 128, 1024), BF16)])
    oth = pair(own)
    w2a, w1b = shift(w1a, "fsdp", 4, -1), shift(w1a, "dp", 4, -1)
    w2b, w3a = shift(w3b, "fsdp", 4, 1), shift(w3b, "dp", 4, 1)
    weights = [w0a, w0b, w1a, w1b, w2a, w2b, w3a, w3b]
    f1, b1 = turn(own, 1), turn(own, -1)
    f2, b2 = turn(f1, 1), turn(b1, -1)
    f3, b3 = turn(f2, 1), turn(b2, -1)
    f4 = turn(f3, 1)
    heads, _, _ = call(
        project_kernel,
        ids,
        [own, oth] + weights,
        [((8, 256, 128), BF16), ((256, 1024), BF16), ((256, 1024), BF16)],
        [pltpu.VMEM((4, 256, 1024), BF16)],
    )
    mine = exchange(heads, "z").reshape(2048, 128)
    other = pair(mine)
    send, keep = call(
        attention_kernel,
        ids,
        [mine, other],
        [((3072, 128), BF16), ((2048, 128), F32)],
        [
            pltpu.VMEM((2048, 128), BF16),
            pltpu.VMEM((1024, 128), BF16),
            pltpu.VMEM((128, 2048), BF16),
            pltpu.VMEM((1024, 128), BF16),
        ],
        24,
    )
    recv = pair(send)
    moved, columns = call(
        merge_kernel,
        ids,
        [keep, send, recv],
        [((2048, 128), BF16), ((2048, 256), BF16)],
        shape=pltpu.HBM,
    )
    grads = exchange(moved.reshape(8, 256, 128), "z")
    kept, sent = call(
        back_kernel,
        ids,
        [grads],
        [((2, 128, 1024), F32), ((2, 128, 1024), F32)],
        [pltpu.VMEM((4, 256, 1024), BF16)],
        far=weights,
    )
    got = pair(sent)
    out, grad = call(
        finish_kernel,
        ids,
        [sig, up, kept, got],
        [((128, 1024), BF16), ((128, 1024), BF16)],
        shape=pltpu.HBM,
    )
    share, foreign = call(
        outer_kernel,
        ids,
        [],
        [((4, 128, 256), F32), ((4, 128, 256), BF16)],
        [pltpu.VMEM((1024, 256), F32), pltpu.VMEM((1024, 128), F32)],
        far=[columns, own, f1, b1, f2, b2, f3, b3, f4],
    )
    foreign = pair(foreign)
    share = [(share[i] + foreign[i].astype(F32)).astype(BF16) for i in range(4)]
    total = share[0].astype(F32)
    for step in (1, 3, 2):
        total += shift(share[step], "fsdp", 4, step).astype(F32)
    mine = total.astype(BF16)
    total = mine.astype(F32)
    for step in (1, 3, 2):
        total += shift(mine, "dp", 4, step).astype(F32)
    total = exchange(jnp.broadcast_to(total.astype(BF16)[None], (8, 128, 256)), "z")
    across = pair(total)
    shares = call(spread_kernel, ids, [total, across], [((256, 512), F32)] * 4, shape=pltpu.HBM)
    return (out[None], grad[None], *shares)


def solution(mesh):
    dp, seq, fsdp = mesh.devices.shape
    split = Mesh(mesh.devices.reshape(dp, seq // 2, 2, fsdp), ("dp", "z", "core", "fsdp"))
    frames = P(("dp", "fsdp"), ("z", "core"), None)
    rows = P("fsdp", None)

    return jax.shard_map(
        body,
        mesh=split,
        in_specs=(frames, rows, rows, rows, rows, frames),
        out_specs=(frames, frames, rows, rows, rows, rows),
        check_vma=False,
    )
```

time: 161 us -> 162 us (level)
  the two profiles are of different devices: /device:TPU:2 before, /device:TPU:1 now
where the time goes in v2:
time: 162 us; the launch traced here: 161 us
  starting transfers between devices  65.5 us (40%)
  waiting for transfers between devices  63.2 us (39%)
  Pallas kernels  28.7 us (18%)
  local copies, waits for them, and re-layouts  1.69 us (1%)
    ppermute x18, starting transfers between devices, shift(): lax.ppermute(value, axis, [(i, (i + by) % size) for i in range(size)])  41.2 us
    ppermute x7, waiting for transfers between devices, turn(): return lax.ppermute(value, ('z', 'core'), perm)  35.5 us
    pallas_call x8, Pallas kernels, call(): pl.pallas_call(kernel, in_specs=[smem()] + vmem(len(args)), out_specs=vme...  28.7 us
    ppermute x18, waiting for transfers between devices, shift(): lax.ppermute(value, axis, [(i, (i + by) % size) for i in range(size)])  18 us
    all_to_all x3, starting transfers between devices, exchange(): return lax.all_to_all(value, axis, split_axis=0, concat_axis=0, tiled=True)  16.9 us
    all_to_all x3, waiting for transfers between devices, exchange(): return lax.all_to_all(value, axis, split_axis=0, concat_axis=0, tiled=True)  9.74 us
    ppermute x7, starting transfers between devices, turn(): return lax.ppermute(value, ('z', 'core'), perm)  7.35 us
  transfers between devices with their start and end apart: 28, of which 17 were waited for; matrix products, arithmetic and copies ran while one was open for 0% of the time, Pallas kernels for 13%

profile of v2, /device:TPU:1, one launch (start us, length us, event | category | flops | bytes accessed | tf_op | source)
XLA Modules:
  0.0 161.4 jit_solution(10803411875423593836)
XLA Ops:
  1.9 3.4 %collective-permute-start.1 = (bf16[128,1024]{1,0:T(8,128)(2,1)S(1)}, bf16[128,1024]{1,0:T(8,128)(2,1)S(1)}, u32[]{:S(2)}, u32[]{:S(2)}) collective-permute-start(bf16[128,1024]{1,0:T(8,128)(2,1)S(1)} %get-tuple-element.40.refs_0_), channel_id=1, source_target_pairs={{0,3},{1,0},{2,1},{3,2},{4,7},{5,4},{6,5},{7,6},{8,11},{9,8},{10,9... | collective-permute-start | bytes 786440 | tf_op jit(solution)/shard_map/ppermute | solution.py:54
  10.3 2.7 %collective-permute-start.2 = (bf16[128,1024]{1,0:T(8,128)(2,1)S(1)}, bf16[128,1024]{1,0:T(8,128)(2,1)S(1)}, u32[]{:S(2)}, u32[]{:S(2)}) collective-permute-start(bf16[128,1024]{1,0:T(8,128)(2,1)S(1)} %collective-permute-done.1.refs_2_), channel_id=1, source_target_pairs={{0,192},{64,0},{128,64},{192,128},{1,193},{65,1},{129,65},{193,129... | collective-permute-start | bytes 786440 | tf_op jit(solution)/shard_map/ppermute | solution.py:54
  13.0 3.4 %collective-permute-start.3 = (bf16[128,1024]{1,0:T(8,128)(2,1)S(1)}, bf16[128,1024]{1,0:T(8,128)(2,1)S(1)}, u32[]{:S(2)}, u32[]{:S(2)}) collective-permute-start(bf16[128,1024]{1,0:T(8,128)(2,1)S(1)} %collective-permute-done.1.refs_2_), channel_id=1, source_target_pairs={{0,3},{1,0},{2,1},{3,2},{4,7},{5,4},{6,5},{7,6},{8,11},{9,8},{10,9... | collective-permute-start | bytes 786440 | tf_op jit(solution)/shard_map/ppermute | solution.py:54
  17.5 2.8 %collective-permute-done.3.refs_4_ = bf16[128,1024]{1,0:T(8,128)(2,1)S(1)} collective-permute-done((bf16[128,1024]{1,0:T(8,128)(2,1)S(1)}, bf16[128,1024]{1,0:T(8,128)(2,1)S(1)}, u32[]{:S(2)}, u32[]{:S(2)}) %collective-permute-start.3) | collective-permute-done | bytes 262176 | tf_op jit(solution)/shard_map/ppermute | solution.py:54
  20.3 3.1 %collective-permute-done.5.refs_5_ = bf16[128,1024]{1,0:T(8,128)(2,1)S(1)} collective-permute-done((bf16[128,1024]{1,0:T(8,128)(2,1)S(1)}, bf16[128,1024]{1,0:T(8,128)(2,1)S(1)}, u32[]{:S(2)}, u32[]{:S(2)}) %collective-permute-start.5) | collective-permute-done | bytes 262176 | tf_op jit(solution)/shard_map/ppermute | solution.py:54
  25.9 8.2 %all-to-all-start = ((bf16[8,256,128]{2,1,0:T(8,128)(2,1)}), bf16[8,256,128]{2,1,0:T(8,128)(2,1)S(1)}, u32[]{:S(2)}, u32[]{:S(2)}) async-start(bf16[8,256,128]{2,1,0:T(8,128)(2,1)} %get-tuple-element.21), calls=%async_computation | async-start | bytes 1048576 | tf_op jit(solution)/shard_map/all_to_all | solution.py:269
  34.1 2.7 %collective-permute-start.10 = (bf16[2,128,1024]{2,1,0:T(8,128)(2,1)S(1)}, bf16[2,128,1024]{2,1,0:T(8,128)(2,1)S(1)}, u32[]{:S(2)}, u32[]{:S(2)}) collective-permute-start(bf16[2,128,1024]{2,1,0:T(8,128)(2,1)S(1)} %shard_map.109.own.x0), channel_id=1, source_target_pairs={{0,8},{8,16},{16,24},{24,32},{32,40},{40,48},{48,56},{56,0},{4,60}... | collective-permute-start | bytes 1572872 | tf_op jit(solution)/shard_map/ppermute | solution.py:265
  36.8 20.3 %collective-permute-done.10.f1 = bf16[2,128,1024]{2,1,0:T(8,128)(2,1)S(1)} collective-permute-done((bf16[2,128,1024]{2,1,0:T(8,128)(2,1)S(1)}, bf16[2,128,1024]{2,1,0:T(8,128)(2,1)S(1)}, u32[]{:S(2)}, u32[]{:S(2)}) %collective-permute-start.10) | collective-permute-done | bytes 524320 | tf_op jit(solution)/shard_map/ppermute | solution.py:265
  58.3 2.9 %collective-permute-start.7 = (bf16[2048,128]{1,0:T(8,128)(2,1)S(1)}, bf16[2048,128]{1,0:T(8,128)(2,1)S(1)}, u32[]{:S(2)}, u32[]{:S(2)}) collective-permute-start(bf16[2048,128]{1,0:T(8,128)(2,1)S(1)} %bitcast.21), channel_id=1, source_target_pairs={{0,4},{4,0},{1,5},{5,1},{2,6},{6,2},{3,7},{7,3},{8,12},{12,8},{9,1... | collective-permute-start | bytes 1572872 | tf_op jit(solution)/shard_map/ppermute | solution.py:54
  61.4 5.9 %collective-permute-done.12.f2 = bf16[2,128,1024]{2,1,0:T(8,128)(2,1)S(1)} collective-permute-done((bf16[2,128,1024]{2,1,0:T(8,128)(2,1)S(1)}, bf16[2,128,1024]{2,1,0:T(8,128)(2,1)S(1)}, u32[]{:S(2)}, u32[]{:S(2)}) %collective-permute-start.12) | collective-permute-done | bytes 524320 | tf_op jit(solution)/shard_map/ppermute | solution.py:265
  67.6 12.0 %shard_map.111 = (bf16[3072,128]{1,0:T(8,128)(2,1)S(1)}, f32[2048,128]{1,0:T(8,128)S(1)}) custom-call(s32[4]{0:T(128)S(1)} %pad_add_fusion.ids, bf16[2048,128]{1,0:T(8,128)(2,1)S(1)} %bitcast.22, bf16[2048,128]{1,0:T(8,128)(2,1)S(1)} %collective-permute-done.7.other), custom_call_target="tpu_custom_call" | custom-call | tf_op jit(solution)/shard_map/pallas_call | solution.py:27
  79.6 9.5 %collective-permute-start.8 = (bf16[3072,128]{1,0:T(8,128)(2,1)S(1)}, bf16[3072,128]{1,0:T(8,128)(2,1)S(1)}, u32[]{:S(2)}, u32[]{:S(2)}) collective-permute-start(bf16[3072,128]{1,0:T(8,128)(2,1)S(1)} %get-tuple-element.23.send), channel_id=1, source_target_pairs={{0,4},{4,0},{1,5},{5,1},{2,6},{6,2},{3,7},{7,3},{8,12},{12,8},{9,1... | collective-permute-start | bytes 2359304 | tf_op jit(solution)/shard_map/ppermute | solution.py:54
  89.1 3.0 %collective-permute-start.16 = (bf16[2,128,1024]{2,1,0:T(8,128)(2,1)S(1)}, bf16[2,128,1024]{2,1,0:T(8,128)(2,1)S(1)}, u32[]{:S(2)}, u32[]{:S(2)}) collective-permute-start(bf16[2,128,1024]{2,1,0:T(8,128)(2,1)S(1)} %collective-permute-done.14.f3), channel_id=1, source_target_pairs={{0,8},{8,16},{16,24},{24,32},{32,40},{40,48},{48,56},{56,0},{4,60}... | collective-permute-start | bytes 1572872 | tf_op jit(solution)/shard_map/ppermute | solution.py:265
  94.2 6.9 %collective-permute-done.15.b3 = bf16[2,128,1024]{2,1,0:T(8,128)(2,1)S(1)} collective-permute-done((bf16[2,128,1024]{2,1,0:T(8,128)(2,1)S(1)}, bf16[2,128,1024]{2,1,0:T(8,128)(2,1)S(1)}, u32[]{:S(2)}, u32[]{:S(2)}) %collective-permute-start.15) | collective-permute-done | bytes 524320 | tf_op jit(solution)/shard_map/ppermute | solution.py:265
  101.0 2.4 %collective-permute-done.16.f4 = bf16[2,128,1024]{2,1,0:T(8,128)(2,1)S(1)} collective-permute-done((bf16[2,128,1024]{2,1,0:T(8,128)(2,1)S(1)}, bf16[2,128,1024]{2,1,0:T(8,128)(2,1)S(1)}, u32[]{:S(2)}, u32[]{:S(2)}) %collective-permute-start.16) | collective-permute-done | bytes 524320 | tf_op jit(solution)/shard_map/ppermute | solution.py:265
  104.2 3.9 %shard_map.115 = (f32[4,128,256]{2,1,0:T(8,128)S(1)}, bf16[4,128,256]{2,1,0:T(8,128)(2,1)S(1)}) custom-call(s32[4]{0:T(128)S(1)} %pad_add_fusion.ids, bf16[2048,256]{1,0:T(8,128)(2,1)} %get-tuple-element.29.columns, bf16[2,128,1024]{2,1,0:T(8,128)(2,1)} %copy-done, bf16[2,128,1024]{2,1,0:T(8,128)(2,1)} %copy-done.12, bf16[2,128,1024]{2,1,0:T(8,128)(2,1)} %copy-done.13, ...), custom_call_target="tpu_custom_call" | custom-call | tf_op jit(solution)/shard_map/pallas_call | solution.py:27
  109.7 4.3 %all-to-all-start.1 = ((bf16[8,256,128]{2,1,0:T(8,128)(2,1)}), bf16[8,256,128]{2,1,0:T(8,128)(2,1)S(1)}, u32[]{:S(2)}, u32[]{:S(2)}) async-start(bf16[8,256,128]{2,1,0:T(8,128)(2,1)} %bitcast.7), calls=%async_computation.1 | async-start | bytes 1048576 | tf_op jit(solution)/shard_map/all_to_all | solution.py:269
  121.2 2.9 %collective-permute-start.23 = (bf16[128,256]{1,0:T(8,128)(2,1)S(1)}, bf16[128,256]{1,0:T(8,128)(2,1)S(1)}, u32[]{:S(2)}, u32[]{:S(2)}) collective-permute-start(bf16[128,256]{1,0:T(8,128)(2,1)S(1)} %fusion.3), channel_id=1, source_target_pairs={{0,128},{64,192},{128,0},{192,64},{1,129},{65,193},{129,1},{193,65... | collective-permute-start | bytes 196616 | tf_op jit(solution)/shard_map/ppermute | solution.py:54
  129.6 2.5 %all-to-all-done.1.heads = bf16[8,256,128]{2,1,0:T(8,128)(2,1)S(1)} async-done(((bf16[8,256,128]{2,1,0:T(8,128)(2,1)}), bf16[8,256,128]{2,1,0:T(8,128)(2,1)S(1)}, u32[]{:S(2)}, u32[]{:S(2)}) %all-to-all-start.1) | async-done | bytes 524320 | tf_op jit(solution)/shard_map/all_to_all | solution.py:269
  132.8 4.5 %all-to-all-start.2 = ((bf16[8,128,256]{2,1,0:T(8,128)(2,1)}), bf16[8,128,256]{2,1,0:T(8,128)(2,1)S(1)}, u32[]{:S(2)}, u32[]{:S(2)}) async-start(bf16[8,128,256]{2,1,0:T(8,128)(2,1)} %broadcast_in_dim.14), calls=%async_computation.2 | async-start | bytes 1048576 | tf_op jit(solution)/shard_map/all_to_all | solution.py:269
  137.3 3.6 %shard_map.113 = (f32[2,128,1024]{2,1,0:T(8,128)S(1)}, f32[2,128,1024]{2,1,0:T(8,128)}) custom-call(s32[4]{0:T(128)S(1)} %pad_add_fusion.ids, bf16[8,256,128]{2,1,0:T(8,128)(2,1)S(1)} %all-to-all-done.1.heads, bf16[128,1024]{1,0:T(8,128)(2,1)} %copy-done.2, bf16[128,1024]{1,0:T(8,128)(2,1)} %copy-done.1, bf16[128,1024]{1,0:T(8,128)(2,1)} %copy-done.6, ...), custom_call_target="tpu_custom_call" | custom-call | tf_op jit(solution)/shard_map/pallas_call | solution.py:27
  140.9 3.4 %collective-permute-start.9 = (f32[2,128,1024]{2,1,0:T(8,128)}, f32[2,128,1024]{2,1,0:T(8,128)S(1)}, u32[]{:S(2)}, u32[]{:S(2)}) collective-permute-start(f32[2,128,1024]{2,1,0:T(8,128)} %get-tuple-element.26), channel_id=1, source_target_pairs={{0,4},{4,0},{1,5},{5,1},{2,6},{6,2},{3,7},{7,3},{8,12},{12,8},{9,1... | collective-permute-start | bytes 3145736 | tf_op jit(solution)/shard_map/ppermute | solution.py:54
  144.3 7.3 %all-to-all-done.2.own = bf16[8,128,256]{2,1,0:T(8,128)(2,1)S(1)} async-done(((bf16[8,128,256]{2,1,0:T(8,128)(2,1)}), bf16[8,128,256]{2,1,0:T(8,128)(2,1)S(1)}, u32[]{:S(2)}, u32[]{:S(2)}) %all-to-all-start.2) | async-done | bytes 524320 | tf_op jit(solution)/shard_map/all_to_all | solution.py:269
  151.6 4.2 %collective-permute-start.24 = (bf16[8,128,256]{2,1,0:T(8,128)(2,1)S(1)}, bf16[8,128,256]{2,1,0:T(8,128)(2,1)S(1)}, u32[]{:S(2)}, u32[]{:S(2)}) collective-permute-start(bf16[8,128,256]{2,1,0:T(8,128)(2,1)S(1)} %all-to-all-done.2.own), channel_id=1, source_target_pairs={{0,4},{4,0},{1,5},{5,1},{2,6},{6,2},{3,7},{7,3},{8,12},{12,8},{9,1... | collective-permute-start | bytes 1572872 | tf_op jit(solution)/shard_map/ppermute | solution.py:54
  (85 shorter events, 34.9 us)
Async XLA Ops:
  1.9 8.4 %collective-permute-start.1 = (bf16[128,1024]{1,0:T(8,128)(2,1)S(1)}, bf16[128,1024]{1,0:T(8,128)(2,1)S(1)}, u32[]{:S(2)}, u32[]{:S(2)}) collective-permute-start(bf16[128,1024]{1,0:T(8,128)(2,1)S(1)} %get-tuple-element.40.refs_0_), channel_id=1, source_target_pairs={{0,3},{1,0},{2,1},{3,2},{4,7},{5,4},{6,5},{7,6},{8,11},{9,8},{10,9... | collective-permute-start | bytes 786440 | tf_op jit(solution)/shard_map/ppermute | solution.py:54
  6.2 11.3 %collective-permute-start = (bf16[2,128,1024]{2,1,0:T(8,128)(2,1)S(1)}, bf16[2,128,1024]{2,1,0:T(8,128)(2,1)S(1)}, u32[]{:S(2)}, u32[]{:S(2)}) collective-permute-start(bf16[2,128,1024]{2,1,0:T(8,128)(2,1)S(1)} %shard_map.109.own.x0), channel_id=1, source_target_pairs={{0,4},{4,0},{1,5},{5,1},{2,6},{6,2},{3,7},{7,3},{8,12},{12,8},{9,1... | collective-permute-start | bytes 1572872 | tf_op jit(solution)/shard_map/ppermute | solution.py:54
  7.2 9.2 %collective-permute-start.4 = (bf16[128,1024]{1,0:T(8,128)(2,1)S(1)}, bf16[128,1024]{1,0:T(8,128)(2,1)S(1)}, u32[]{:S(2)}, u32[]{:S(2)}) collective-permute-start(bf16[128,1024]{1,0:T(8,128)(2,1)S(1)} %get-tuple-element.39.refs_1_), channel_id=1, source_target_pairs={{0,1},{1,2},{2,3},{3,0},{4,5},{5,6},{6,7},{7,4},{8,9},{9,10},{10,1... | collective-permute-start | bytes 786440 | tf_op jit(solution)/shard_map/ppermute | solution.py:54
  10.3 7.2 %collective-permute-start.2 = (bf16[128,1024]{1,0:T(8,128)(2,1)S(1)}, bf16[128,1024]{1,0:T(8,128)(2,1)S(1)}, u32[]{:S(2)}, u32[]{:S(2)}) collective-permute-start(bf16[128,1024]{1,0:T(8,128)(2,1)S(1)} %collective-permute-done.1.refs_2_), channel_id=1, source_target_pairs={{0,192},{64,0},{128,64},{192,128},{1,193},{65,1},{129,65},{193,129... | collective-permute-start | bytes 786440 | tf_op jit(solution)/shard_map/ppermute | solution.py:54
  13.0 7.3 %collective-permute-start.3 = (bf16[128,1024]{1,0:T(8,128)(2,1)S(1)}, bf16[128,1024]{1,0:T(8,128)(2,1)S(1)}, u32[]{:S(2)}, u32[]{:S(2)}) collective-permute-start(bf16[128,1024]{1,0:T(8,128)(2,1)S(1)} %collective-permute-done.1.refs_2_), channel_id=1, source_target_pairs={{0,3},{1,0},{2,1},{3,2},{4,7},{5,4},{6,5},{7,6},{8,11},{9,8},{10,9... | collective-permute-start | bytes 786440 | tf_op jit(solution)/shard_map/ppermute | solution.py:54
  16.4 7.0 %collective-permute-start.5 = (bf16[128,1024]{1,0:T(8,128)(2,1)S(1)}, bf16[128,1024]{1,0:T(8,128)(2,1)S(1)}, u32[]{:S(2)}, u32[]{:S(2)}) collective-permute-start(bf16[128,1024]{1,0:T(8,128)(2,1)S(1)} %collective-permute-done.4.refs_7_), channel_id=1, source_target_pairs={{0,1},{1,2},{2,3},{3,0},{4,5},{5,6},{6,7},{7,4},{8,9},{9,10},{10,1... | collective-permute-start | bytes 786440 | tf_op jit(solution)/shard_map/ppermute | solution.py:54
  16.4 7.1 %collective-permute-start.6 = (bf16[128,1024]{1,0:T(8,128)(2,1)S(1)}, bf16[128,1024]{1,0:T(8,128)(2,1)S(1)}, u32[]{:S(2)}, u32[]{:S(2)}) collective-permute-start(bf16[128,1024]{1,0:T(8,128)(2,1)S(1)} %collective-permute-done.4.refs_7_), channel_id=1, source_target_pairs={{0,64},{64,128},{128,192},{192,0},{1,65},{65,129},{129,193},{193,1... | collective-permute-start | bytes 786440 | tf_op jit(solution)/shard_map/ppermute | solution.py:54
  25.9 32.4 %all-to-all-start = ((bf16[8,256,128]{2,1,0:T(8,128)(2,1)}), bf16[8,256,128]{2,1,0:T(8,128)(2,1)S(1)}, u32[]{:S(2)}, u32[]{:S(2)}) async-start(bf16[8,256,128]{2,1,0:T(8,128)(2,1)} %get-tuple-element.21), calls=%async_computation | async-start | bytes 1048576 | tf_op jit(solution)/shard_map/all_to_all | solution.py:269
  34.1 23.0 %collective-permute-start.10 = (bf16[2,128,1024]{2,1,0:T(8,128)(2,1)S(1)}, bf16[2,128,1024]{2,1,0:T(8,128)(2,1)S(1)}, u32[]{:S(2)}, u32[]{:S(2)}) collective-permute-start(bf16[2,128,1024]{2,1,0:T(8,128)(2,1)S(1)} %shard_map.109.own.x0), channel_id=1, source_target_pairs={{0,8},{8,16},{16,24},{24,32},{32,40},{40,48},{48,56},{56,0},{4,60}... | collective-permute-start | bytes 1572872 | tf_op jit(solution)/shard_map/ppermute | solution.py:265
  36.8 24.4 %collective-permute-start.11 = (bf16[2,128,1024]{2,1,0:T(8,128)(2,1)S(1)}, bf16[2,128,1024]{2,1,0:T(8,128)(2,1)S(1)}, u32[]{:S(2)}, u32[]{:S(2)}) collective-permute-start(bf16[2,128,1024]{2,1,0:T(8,128)(2,1)S(1)} %shard_map.109.own.x0), channel_id=1, source_target_pairs={{0,56},{8,0},{16,8},{24,16},{32,24},{40,32},{48,40},{56,48},{4,12}... | collective-permute-start | bytes 1572872 | tf_op jit(solution)/shard_map/ppermute | solution.py:265
  57.1 10.2 %collective-permute-start.12 = (bf16[2,128,1024]{2,1,0:T(8,128)(2,1)S(1)}, bf16[2,128,1024]{2,1,0:T(8,128)(2,1)S(1)}, u32[]{:S(2)}, u32[]{:S(2)}) collective-permute-start(bf16[2,128,1024]{2,1,0:T(8,128)(2,1)S(1)} %collective-permute-done.10.f1), channel_id=1, source_target_pairs={{0,8},{8,16},{16,24},{24,32},{32,40},{40,48},{48,56},{56,0},{4,60}... | collective-permute-start | bytes 1572872 | tf_op jit(solution)/shard_map/ppermute | solution.py:265
  58.3 9.2 %collective-permute-start.7 = (bf16[2048,128]{1,0:T(8,128)(2,1)S(1)}, bf16[2048,128]{1,0:T(8,128)(2,1)S(1)}, u32[]{:S(2)}, u32[]{:S(2)}) collective-permute-start(bf16[2048,128]{1,0:T(8,128)(2,1)S(1)} %bitcast.21), channel_id=1, source_target_pairs={{0,4},{4,0},{1,5},{5,1},{2,6},{6,2},{3,7},{7,3},{8,12},{12,8},{9,1... | collective-permute-start | bytes 1572872 | tf_op jit(solution)/shard_map/ppermute | solution.py:54
  61.2 27.9 %collective-permute-start.13 = (bf16[2,128,1024]{2,1,0:T(8,128)(2,1)S(1)}, bf16[2,128,1024]{2,1,0:T(8,128)(2,1)S(1)}, u32[]{:S(2)}, u32[]{:S(2)}) collective-permute-start(bf16[2,128,1024]{2,1,0:T(8,128)(2,1)S(1)} %collective-permute-done.11.b1), channel_id=1, source_target_pairs={{0,56},{8,0},{16,8},{24,16},{32,24},{40,32},{48,40},{56,48},{4,12}... | collective-permute-start | bytes 1572872 | tf_op jit(solution)/shard_map/ppermute | solution.py:265
  67.3 21.8 %collective-permute-start.14 = (bf16[2,128,1024]{2,1,0:T(8,128)(2,1)S(1)}, bf16[2,128,1024]{2,1,0:T(8,128)(2,1)S(1)}, u32[]{:S(2)}, u32[]{:S(2)}) collective-permute-start(bf16[2,128,1024]{2,1,0:T(8,128)(2,1)S(1)} %collective-permute-done.12.f2), channel_id=1, source_target_pairs={{0,8},{8,16},{16,24},{24,32},{32,40},{40,48},{48,56},{56,0},{4,60}... | collective-permute-start | bytes 1572872 | tf_op jit(solution)/shard_map/ppermute | solution.py:265
  79.6 12.6 %collective-permute-start.8 = (bf16[3072,128]{1,0:T(8,128)(2,1)S(1)}, bf16[3072,128]{1,0:T(8,128)(2,1)S(1)}, u32[]{:S(2)}, u32[]{:S(2)}) collective-permute-start(bf16[3072,128]{1,0:T(8,128)(2,1)S(1)} %get-tuple-element.23.send), channel_id=1, source_target_pairs={{0,4},{4,0},{1,5},{5,1},{2,6},{6,2},{3,7},{7,3},{8,12},{12,8},{9,1... | collective-permute-start | bytes 2359304 | tf_op jit(solution)/shard_map/ppermute | solution.py:54
  89.1 11.9 %collective-permute-start.15 = (bf16[2,128,1024]{2,1,0:T(8,128)(2,1)S(1)}, bf16[2,128,1024]{2,1,0:T(8,128)(2,1)S(1)}, u32[]{:S(2)}, u32[]{:S(2)}) collective-permute-start(bf16[2,128,1024]{2,1,0:T(8,128)(2,1)S(1)} %collective-permute-done.13.b2), channel_id=1, source_target_pairs={{0,56},{8,0},{16,8},{24,16},{32,24},{40,32},{48,40},{56,48},{4,12}... | collective-permute-start | bytes 1572872 | tf_op jit(solution)/shard_map/ppermute | solution.py:265
  89.1 14.3 %collective-permute-start.16 = (bf16[2,128,1024]{2,1,0:T(8,128)(2,1)S(1)}, bf16[2,128,1024]{2,1,0:T(8,128)(2,1)S(1)}, u32[]{:S(2)}, u32[]{:S(2)}) collective-permute-start(bf16[2,128,1024]{2,1,0:T(8,128)(2,1)S(1)} %collective-permute-done.14.f3), channel_id=1, source_target_pairs={{0,8},{8,16},{16,24},{24,32},{32,40},{40,48},{48,56},{56,0},{4,60}... | collective-permute-start | bytes 1572872 | tf_op jit(solution)/shard_map/ppermute | solution.py:265
  108.1 5.9 %collective-permute-start.17 = (bf16[4,128,256]{2,1,0:T(8,128)(2,1)S(1)}, bf16[4,128,256]{2,1,0:T(8,128)(2,1)S(1)}, u32[]{:S(2)}, u32[]{:S(2)}) collective-permute-start(bf16[4,128,256]{2,1,0:T(8,128)(2,1)S(1)} %get-tuple-element.31), channel_id=1, source_target_pairs={{0,4},{4,0},{1,5},{5,1},{2,6},{6,2},{3,7},{7,3},{8,12},{12,8},{9,1... | collective-permute-start | bytes 786440 | tf_op jit(solution)/shard_map/ppermute | solution.py:54
  109.7 22.3 %all-to-all-start.1 = ((bf16[8,256,128]{2,1,0:T(8,128)(2,1)}), bf16[8,256,128]{2,1,0:T(8,128)(2,1)S(1)}, u32[]{:S(2)}, u32[]{:S(2)}) async-start(bf16[8,256,128]{2,1,0:T(8,128)(2,1)} %bitcast.7), calls=%async_computation.1 | async-start | bytes 1048576 | tf_op jit(solution)/shard_map/all_to_all | solution.py:269
  115.3 4.7 %collective-permute-start.19 = (bf16[128,256]{1,0:T(8,128)(2,1)S(1)}, bf16[128,256]{1,0:T(8,128)(2,1)S(1)}, u32[]{:S(2)}, u32[]{:S(2)}) collective-permute-start(bf16[128,256]{1,0:T(8,128)(2,1)S(1)} %get-tuple-element.38), channel_id=1, source_target_pairs={{0,3},{1,0},{2,1},{3,2},{4,7},{5,4},{6,5},{7,6},{8,11},{9,8},{10,9... | collective-permute-start | bytes 196616 | tf_op jit(solution)/shard_map/ppermute | solution.py:54
  121.2 5.0 %collective-permute-start.23 = (bf16[128,256]{1,0:T(8,128)(2,1)S(1)}, bf16[128,256]{1,0:T(8,128)(2,1)S(1)}, u32[]{:S(2)}, u32[]{:S(2)}) collective-permute-start(bf16[128,256]{1,0:T(8,128)(2,1)S(1)} %fusion.3), channel_id=1, source_target_pairs={{0,128},{64,192},{128,0},{192,64},{1,129},{65,193},{129,1},{193,65... | collective-permute-start | bytes 196616 | tf_op jit(solution)/shard_map/ppermute | solution.py:54
  132.8 18.7 %all-to-all-start.2 = ((bf16[8,128,256]{2,1,0:T(8,128)(2,1)}), bf16[8,128,256]{2,1,0:T(8,128)(2,1)S(1)}, u32[]{:S(2)}, u32[]{:S(2)}) async-start(bf16[8,128,256]{2,1,0:T(8,128)(2,1)} %broadcast_in_dim.14), calls=%async_computation.2 | async-start | bytes 1048576 | tf_op jit(solution)/shard_map/all_to_all | solution.py:269
  140.9 18.8 %collective-permute-start.9 = (f32[2,128,1024]{2,1,0:T(8,128)}, f32[2,128,1024]{2,1,0:T(8,128)S(1)}, u32[]{:S(2)}, u32[]{:S(2)}) collective-permute-start(f32[2,128,1024]{2,1,0:T(8,128)} %get-tuple-element.26), channel_id=1, source_target_pairs={{0,4},{4,0},{1,5},{5,1},{2,6},{6,2},{3,7},{7,3},{8,12},{12,8},{9,1... | collective-permute-start | bytes 3145736 | tf_op jit(solution)/shard_map/ppermute | solution.py:54
  151.6 5.7 %collective-permute-start.24 = (bf16[8,128,256]{2,1,0:T(8,128)(2,1)S(1)}, bf16[8,128,256]{2,1,0:T(8,128)(2,1)S(1)}, u32[]{:S(2)}, u32[]{:S(2)}) collective-permute-start(bf16[8,128,256]{2,1,0:T(8,128)(2,1)S(1)} %all-to-all-done.2.own), channel_id=1, source_target_pairs={{0,4},{4,0},{1,5},{5,1},{2,6},{6,2},{3,7},{7,3},{8,12},{12,8},{9,1... | collective-permute-start | bytes 1572872 | tf_op jit(solution)/shard_map/ppermute | solution.py:54
  (23 other events, 242.3 us)

commit v3 on v2

--- a/solution.py
+++ b/solution.py
@@ -100,7 +100,7 @@
 
 
 def attend(kv, qg, turned_kv, acc, part, blocks):
-    keys, block = kv.shape[0], 256
+    keys, block = kv.shape[0], 512
     low = low_lanes((keys, 128))
     zero = jnp.zeros((), BF16)
     pairs = kv[...]
@@ -127,7 +127,8 @@
         gs = (att * (grad - delta)).astype(BF16)
         qk = jnp.where(low_q, qb, zero)
         qv = jnp.where(low_q, zero, qb)
-        acc[...] += dot(gs, qk, ((1,), (0,))) + dot(weights, qv, ((1,), (0,)))
+        both, queries = jnp.concatenate([gs, weights], axis=1), jnp.concatenate([qk, qv], axis=0)
+        acc[...] += dot(both, queries, ((1,), (0,)))
         turned = dot(key_cols, gs, ((1,), (0,))) + dot(value_cols, weights, ((1,), (0,)))
         part[pl.ds(start, block), :] = (turned.T * scale).astype(BF16)
         return carry
@@ -151,7 +152,7 @@
 
     turned_kv[...] = kv[...].astype(F32).T.astype(BF16)
     keep[...] = jnp.zeros_like(keep)
-    scale = attend(kv, qg, turned_kv, keep, part, (0, 4))
+    scale = attend(kv, qg, turned_kv, keep, part, (0, 2))
     total = keep[...] * scale
     keep[...] = total
     send[0:keys, :] = total.astype(BF16)
@@ -234,15 +235,24 @@
         send[1, :, cols] = jnp.where(core == 0, extra[128:], extra[:128])
 
 
-def spread_kernel(ids, own, oth, gq, gk, gv, go):
-    core = ids[0]
+NEAR, FAR = (0, 1, 7, 2, 6), (3, 4, 5)
+
+
+def spread_kernel(ids, *refs):
+    own, (near, far), (gq, gk, gv, go, heads) = refs[:8], refs[8:10], refs[10:]
+    oth = {step: near.at[i] for i, step in enumerate(NEAR)}
+    oth.update({step: far.at[i] for i, step in enumerate(FAR)})
+    core, place = ids[0], ids[2]
     mask = low_lanes((128, 128))
     scale = 32768**-0.5
     for half, pieces in enumerate((own, oth)):
+        for step in range(8):
+            back = core if half == 1 else 1 - core
+            heads[lax.rem(place + jnp.where(back == 1, 8 - step, step), 8)] = pieces[step][...]
         start = jnp.where(core == half, 0, 128)
         rows = pl.ds(pl.multiple_of(start, 128), 128)
         for duo in range(4):
-            a, b = (pieces[h].astype(F32) * scale for h in (2 * duo, 2 * duo + 1))
+            a, b = (heads[h].astype(F32) * scale for h in (2 * duo, 2 * duo + 1))
             lanes = slice(128 * duo, 128 * duo + 128)
             for first, (low, high) in ((0, (gk, gv)), (128, (gq, go))):
                 ta, tb = a[:, first : first + 128], b[:, first : first + 128]
@@ -309,7 +319,7 @@
             pltpu.VMEM((128, 2048), BF16),
             pltpu.VMEM((1024, 128), BF16),
         ],
-        24,
+        30,
     )
     recv = pair(send)
     moved, columns = call(
@@ -353,9 +363,20 @@
     total = mine.astype(F32)
     for step in (1, 3, 2):
         total += shift(mine, "dp", 4, step).astype(F32)
-    total = exchange(jnp.broadcast_to(total.astype(BF16)[None], (8, 128, 256)), "z")
-    across = pair(total)
-    shares = call(spread_kernel, ids, [total, across], [((256, 512), F32)] * 4, shape=pltpu.HBM)
+    total = total.astype(BF16)
+    p2, p6 = turn(total, 2), turn(total, -2)
+    p1, p7 = turn(total, 1), turn(total, -1)
+    p3, p4, p5 = turn(p2, 1), turn(p2, 2), turn(p6, -1)
+    pieces = [total, p1, p2, p3, p4, p5, p6, p7]
+    across = [pair(jnp.stack([pieces[i] for i in NEAR])), pair(jnp.stack([pieces[i] for i in FAR]))]
+    shares = call(
+        spread_kernel,
+        ids,
+        pieces + across,
+        [((256, 512), F32)] * 4,
+        [pltpu.VMEM((8, 128, 256), BF16)],
+        shape=pltpu.HBM,
+    )
     return (out[None], grad[None], *shares)
 
 

time: 162 us -> 154 us (0.951)
  waiting for transfers between devices: 63.2 us -> 54.8 us
  starting transfers between devices: 65.5 us -> 69.9 us
  Pallas kernels: 28.7 us -> 26.2 us
    ppermute x7 -> x14, starting transfers between devices: 7.35 us -> 17.6 us  [turn(): return lax.ppermute(value, ('z', 'core'), perm)]
    all_to_all x3 -> x2, waiting for transfers between devices: 9.74 us -> 0.01 us  [exchange(): return lax.all_to_all(value, axis, split_axis=0, concat_axis=0, tiled=True)]
    all_to_all x3 -> x2, starting transfers between devices: 16.9 us -> 12.5 us  [exchange(): return lax.all_to_all(value, axis, split_axis=0, concat_axis=0, tiled=True)]
    pallas_call x8, Pallas kernels: 28.7 us -> 26.2 us  [call(): pl.pallas_call(kernel, in_specs=[smem()] + vmem(len(args)), out_specs=vme...]
    ppermute x18 -> x19, starting transfers between devices: 41.2 us -> 39.9 us  [shift(): lax.ppermute(value, axis, [(i, (i + by) % size) for i in range(size)])]
    ppermute x7 -> x14, waiting for transfers between devices: 35.5 us -> 36.6 us  [turn(): return lax.ppermute(value, ('z', 'core'), perm)]
    ppermute x18 -> x19, waiting for transfers between devices: 18 us -> 18.2 us  [shift(): lax.ppermute(value, axis, [(i, (i + by) % size) for i in range(size)])]
  transfers between devices with their start and end apart: 28 -> 35, of which waited for: 17 -> 16; matrix products, arithmetic and copies ran while one was open for 0% -> 0% of each run, Pallas kernels for 13% -> 12%
where the time goes in v3:
time: 154 us
  starting transfers between devices  69.9 us (45%)
  waiting for transfers between devices  54.8 us (36%)
  Pallas kernels  26.2 us (17%)
    ppermute x19, starting transfers between devices, shift(): lax.ppermute(value, axis, [(i, (i + by) % size) for i in range(size)])  39.9 us
    ppermute x14, waiting for transfers between devices, turn(): return lax.ppermute(value, ('z', 'core'), perm)  36.6 us
    pallas_call x8, Pallas kernels, call(): pl.pallas_call(kernel, in_specs=[smem()] + vmem(len(args)), out_specs=vme...  26.2 us
    ppermute x19, waiting for transfers between devices, shift(): lax.ppermute(value, axis, [(i, (i + by) % size) for i in range(size)])  18.2 us
    ppermute x14, starting transfers between devices, turn(): return lax.ppermute(value, ('z', 'core'), perm)  17.6 us
    all_to_all x2, starting transfers between devices, exchange(): return lax.all_to_all(value, axis, split_axis=0, concat_axis=0, tiled=True)  12.5 us
  transfers between devices with their start and end apart: 35, of which 16 were waited for; matrix products, arithmetic and copies ran while one was open for 0% of the time, Pallas kernels for 12%

profile of v3, /device:TPU:1, one launch (start us, length us, event | category | flops | bytes accessed | tf_op | source)
XLA Modules:
  0.0 154.2 jit_solution(16968550147280280535)
XLA Ops:
  1.9 3.4 %collective-permute-start.1 = (bf16[128,1024]{1,0:T(8,128)(2,1)S(1)}, bf16[128,1024]{1,0:T(8,128)(2,1)S(1)}, u32[]{:S(2)}, u32[]{:S(2)}) collective-permute-start(bf16[128,1024]{1,0:T(8,128)(2,1)S(1)} %get-tuple-element.42.refs_0_), channel_id=1, source_target_pairs={{0,3},{1,0},{2,1},{3,2},{4,7},{5,4},{6,5},{7,6},{8,11},{9,8},{10,9... | collective-permute-start | bytes 786440 | tf_op jit(solution)/shard_map/ppermute | solution.py:54
  10.3 2.7 %collective-permute-start.2 = (bf16[128,1024]{1,0:T(8,128)(2,1)S(1)}, bf16[128,1024]{1,0:T(8,128)(2,1)S(1)}, u32[]{:S(2)}, u32[]{:S(2)}) collective-permute-start(bf16[128,1024]{1,0:T(8,128)(2,1)S(1)} %collective-permute-done.1.refs_2_), channel_id=1, source_target_pairs={{0,192},{64,0},{128,64},{192,128},{1,193},{65,1},{129,65},{193,129... | collective-permute-start | bytes 786440 | tf_op jit(solution)/shard_map/ppermute | solution.py:54
  13.0 3.4 %collective-permute-start.3 = (bf16[128,1024]{1,0:T(8,128)(2,1)S(1)}, bf16[128,1024]{1,0:T(8,128)(2,1)S(1)}, u32[]{:S(2)}, u32[]{:S(2)}) collective-permute-start(bf16[128,1024]{1,0:T(8,128)(2,1)S(1)} %collective-permute-done.1.refs_2_), channel_id=1, source_target_pairs={{0,3},{1,0},{2,1},{3,2},{4,7},{5,4},{6,5},{7,6},{8,11},{9,8},{10,9... | collective-permute-start | bytes 786440 | tf_op jit(solution)/shard_map/ppermute | solution.py:54
  17.5 2.8 %collective-permute-done.3.refs_4_ = bf16[128,1024]{1,0:T(8,128)(2,1)S(1)} collective-permute-done((bf16[128,1024]{1,0:T(8,128)(2,1)S(1)}, bf16[128,1024]{1,0:T(8,128)(2,1)S(1)}, u32[]{:S(2)}, u32[]{:S(2)}) %collective-permute-start.3) | collective-permute-done | bytes 262176 | tf_op jit(solution)/shard_map/ppermute | solution.py:54
  20.3 3.1 %collective-permute-done.5.refs_5_ = bf16[128,1024]{1,0:T(8,128)(2,1)S(1)} collective-permute-done((bf16[128,1024]{1,0:T(8,128)(2,1)S(1)}, bf16[128,1024]{1,0:T(8,128)(2,1)S(1)}, u32[]{:S(2)}, u32[]{:S(2)}) %collective-permute-start.5) | collective-permute-done | bytes 262176 | tf_op jit(solution)/shard_map/ppermute | solution.py:54
  25.9 8.2 %all-to-all-start = ((bf16[8,256,128]{2,1,0:T(8,128)(2,1)}), bf16[8,256,128]{2,1,0:T(8,128)(2,1)S(1)}, u32[]{:S(2)}, u32[]{:S(2)}) async-start(bf16[8,256,128]{2,1,0:T(8,128)(2,1)} %get-tuple-element.21), calls=%async_computation | async-start | bytes 1048576 | tf_op jit(solution)/shard_map/all_to_all | solution.py:279
  34.1 2.7 %collective-permute-start.10 = (bf16[2,128,1024]{2,1,0:T(8,128)(2,1)S(1)}, bf16[2,128,1024]{2,1,0:T(8,128)(2,1)S(1)}, u32[]{:S(2)}, u32[]{:S(2)}) collective-permute-start(bf16[2,128,1024]{2,1,0:T(8,128)(2,1)S(1)} %shard_map.109.own.x0), channel_id=1, source_target_pairs={{0,8},{8,16},{16,24},{24,32},{32,40},{40,48},{48,56},{56,0},{4,60}... | collective-permute-start | bytes 1572872 | tf_op jit(solution)/shard_map/ppermute | solution.py:275
  36.8 20.3 %collective-permute-done.10.f1 = bf16[2,128,1024]{2,1,0:T(8,128)(2,1)S(1)} collective-permute-done((bf16[2,128,1024]{2,1,0:T(8,128)(2,1)S(1)}, bf16[2,128,1024]{2,1,0:T(8,128)(2,1)S(1)}, u32[]{:S(2)}, u32[]{:S(2)}) %collective-permute-start.10) | collective-permute-done | bytes 524320 | tf_op jit(solution)/shard_map/ppermute | solution.py:275
  58.3 2.9 %collective-permute-start.7 = (bf16[2048,128]{1,0:T(8,128)(2,1)S(1)}, bf16[2048,128]{1,0:T(8,128)(2,1)S(1)}, u32[]{:S(2)}, u32[]{:S(2)}) collective-permute-start(bf16[2048,128]{1,0:T(8,128)(2,1)S(1)} %bitcast.34), channel_id=1, source_target_pairs={{0,4},{4,0},{1,5},{5,1},{2,6},{6,2},{3,7},{7,3},{8,12},{12,8},{9,1... | collective-permute-start | bytes 1572872 | tf_op jit(solution)/shard_map/ppermute | solution.py:54
  61.4 5.9 %collective-permute-done.12.f2 = bf16[2,128,1024]{2,1,0:T(8,128)(2,1)S(1)} collective-permute-done((bf16[2,128,1024]{2,1,0:T(8,128)(2,1)S(1)}, bf16[2,128,1024]{2,1,0:T(8,128)(2,1)S(1)}, u32[]{:S(2)}, u32[]{:S(2)}) %collective-permute-start.12) | collective-permute-done | bytes 524320 | tf_op jit(solution)/shard_map/ppermute | solution.py:275
  67.6 10.5 %shard_map.111 = (bf16[3072,128]{1,0:T(8,128)(2,1)S(1)}, f32[2048,128]{1,0:T(8,128)S(1)}) custom-call(s32[4]{0:T(128)S(1)} %pad_add_fusion.ids, bf16[2048,128]{1,0:T(8,128)(2,1)S(1)} %bitcast.35, bf16[2048,128]{1,0:T(8,128)(2,1)S(1)} %collective-permute-done.7.other), custom_call_target="tpu_custom_call" | custom-call | tf_op jit(solution)/shard_map/pallas_call | solution.py:27
  78.1 9.5 %collective-permute-start.8 = (bf16[3072,128]{1,0:T(8,128)(2,1)S(1)}, bf16[3072,128]{1,0:T(8,128)(2,1)S(1)}, u32[]{:S(2)}, u32[]{:S(2)}) collective-permute-start(bf16[3072,128]{1,0:T(8,128)(2,1)S(1)} %get-tuple-element.23.send), channel_id=1, source_target_pairs={{0,4},{4,0},{1,5},{5,1},{2,6},{6,2},{3,7},{7,3},{8,12},{12,8},{9,1... | collective-permute-start | bytes 2359304 | tf_op jit(solution)/shard_map/ppermute | solution.py:54
  87.6 3.0 %collective-permute-start.16 = (bf16[2,128,1024]{2,1,0:T(8,128)(2,1)S(1)}, bf16[2,128,1024]{2,1,0:T(8,128)(2,1)S(1)}, u32[]{:S(2)}, u32[]{:S(2)}) collective-permute-start(bf16[2,128,1024]{2,1,0:T(8,128)(2,1)S(1)} %collective-permute-done.14.f3), channel_id=1, source_target_pairs={{0,8},{8,16},{16,24},{24,32},{32,40},{40,48},{48,56},{56,0},{4,60}... | collective-permute-start | bytes 1572872 | tf_op jit(solution)/shard_map/ppermute | solution.py:275
  92.6 6.9 %collective-permute-done.15.b3 = bf16[2,128,1024]{2,1,0:T(8,128)(2,1)S(1)} collective-permute-done((bf16[2,128,1024]{2,1,0:T(8,128)(2,1)S(1)}, bf16[2,128,1024]{2,1,0:T(8,128)(2,1)S(1)}, u32[]{:S(2)}, u32[]{:S(2)}) %collective-permute-start.15) | collective-permute-done | bytes 524320 | tf_op jit(solution)/shard_map/ppermute | solution.py:275
  99.5 2.4 %collective-permute-done.16.f4 = bf16[2,128,1024]{2,1,0:T(8,128)(2,1)S(1)} collective-permute-done((bf16[2,128,1024]{2,1,0:T(8,128)(2,1)S(1)}, bf16[2,128,1024]{2,1,0:T(8,128)(2,1)S(1)}, u32[]{:S(2)}, u32[]{:S(2)}) %collective-permute-start.16) | collective-permute-done | bytes 524320 | tf_op jit(solution)/shard_map/ppermute | solution.py:275
  102.7 3.9 %shard_map.115 = (f32[4,128,256]{2,1,0:T(8,128)S(1)}, bf16[4,128,256]{2,1,0:T(8,128)(2,1)S(1)}) custom-call(s32[4]{0:T(128)S(1)} %pad_add_fusion.ids, bf16[2048,256]{1,0:T(8,128)(2,1)} %get-tuple-element.29.columns, bf16[2,128,1024]{2,1,0:T(8,128)(2,1)} %copy-done, bf16[2,128,1024]{2,1,0:T(8,128)(2,1)} %copy-done.11, bf16[2,128,1024]{2,1,0:T(8,128)(2,1)} %copy-done.12, ...), custom_call_target="tpu_custom_call" | custom-call | tf_op jit(solution)/shard_map/pallas_call | solution.py:27
  108.2 4.3 %all-to-all-start.1 = ((bf16[8,256,128]{2,1,0:T(8,128)(2,1)}), bf16[8,256,128]{2,1,0:T(8,128)(2,1)S(1)}, u32[]{:S(2)}, u32[]{:S(2)}) async-start(bf16[8,256,128]{2,1,0:T(8,128)(2,1)} %bitcast.7), calls=%async_computation.1 | async-start | bytes 1048576 | tf_op jit(solution)/shard_map/all_to_all | solution.py:279
  119.7 3.1 %collective-permute-start.23 = (bf16[128,256]{1,0:T(8,128)(2,1)S(1)}, bf16[128,256]{1,0:T(8,128)(2,1)S(1)}, u32[]{:S(2)}, u32[]{:S(2)}) collective-permute-start(bf16[128,256]{1,0:T(8,128)(2,1)S(1)} %fusion.3), channel_id=1, source_target_pairs={{0,128},{64,192},{128,0},{192,64},{1,129},{65,193},{129,1},{193,65... | collective-permute-start | bytes 196616 | tf_op jit(solution)/shard_map/ppermute | solution.py:54
  128.3 3.9 %collective-permute-start.25 = (bf16[128,256]{1,0:T(8,128)(2,1)S(1)}, bf16[128,256]{1,0:T(8,128)(2,1)S(1)}, u32[]{:S(2)}, u32[]{:S(2)}) collective-permute-start(bf16[128,256]{1,0:T(8,128)(2,1)S(1)} %get-tuple-element.37.refs_0_), channel_id=1, source_target_pairs={{0,16},{8,24},{16,32},{24,40},{32,48},{40,56},{48,0},{56,8},{4,52}... | collective-permute-start | bytes 196616 | tf_op jit(solution)/shard_map/ppermute | solution.py:275
  132.2 2.7 %collective-permute-start.24 = (bf16[128,256]{1,0:T(8,128)(2,1)S(1)}, bf16[128,256]{1,0:T(8,128)(2,1)S(1)}, u32[]{:S(2)}, u32[]{:S(2)}) collective-permute-start(bf16[128,256]{1,0:T(8,128)(2,1)S(1)} %get-tuple-element.37.refs_0_), channel_id=1, source_target_pairs={{0,8},{8,16},{16,24},{24,32},{32,40},{40,48},{48,56},{56,0},{4,60}... | collective-permute-start | bytes 196616 | tf_op jit(solution)/shard_map/ppermute | solution.py:275
  134.9 2.7 %collective-permute-start.26 = (bf16[128,256]{1,0:T(8,128)(2,1)S(1)}, bf16[128,256]{1,0:T(8,128)(2,1)S(1)}, u32[]{:S(2)}, u32[]{:S(2)}) collective-permute-start(bf16[128,256]{1,0:T(8,128)(2,1)S(1)} %collective-permute-done.25.refs_2_), channel_id=1, source_target_pairs={{0,8},{8,16},{16,24},{24,32},{32,40},{40,48},{48,56},{56,0},{4,60}... | collective-permute-start | bytes 196616 | tf_op jit(solution)/shard_map/ppermute | solution.py:275
  139.6 2.6 %shard_map.113 = (f32[2,128,1024]{2,1,0:T(8,128)S(1)}, f32[2,128,1024]{2,1,0:T(8,128)S(1)}) custom-call(s32[4]{0:T(128)S(1)} %pad_add_fusion.ids, bf16[8,256,128]{2,1,0:T(8,128)(2,1)S(1)} %all-to-all-done.1.heads, bf16[128,1024]{1,0:T(8,128)(2,1)} %copy-done.2, bf16[128,1024]{1,0:T(8,128)(2,1)} %copy-done.1, bf16[128,1024]{1,0:T(8,128)(2,1)} %copy-done.5, ...), custom_call_target="tpu_custom_call" | custom-call | tf_op jit(solution)/shard_map/pallas_call | solution.py:27
  142.2 4.8 %collective-permute-start.9 = (f32[2,128,1024]{2,1,0:T(8,128)S(1)}, f32[2,128,1024]{2,1,0:T(8,128)S(1)}, u32[]{:S(2)}, u32[]{:S(2)}) collective-permute-start(f32[2,128,1024]{2,1,0:T(8,128)S(1)} %get-tuple-element.26), channel_id=1, source_target_pairs={{0,4},{4,0},{1,5},{5,1},{2,6},{6,2},{3,7},{7,3},{8,12},{12,8},{9,1... | collective-permute-start | bytes 3145736 | tf_op jit(solution)/shard_map/ppermute | solution.py:54
  150.1 2.5 %shard_map.116 = (f32[256,512]{1,0:T(8,128)}, f32[256,512]{1,0:T(8,128)}, f32[256,512]{1,0:T(8,128)}, f32[256,512]{1,0:T(8,128)}) custom-call(s32[4]{0:T(128)S(1)} %pad_add_fusion.ids, bf16[128,256]{1,0:T(8,128)(2,1)S(1)} %get-tuple-element.37.refs_0_, bf16[128,256]{1,0:T(8,128)(2,1)S(1)} %collective-permute-done.24.refs_1_, ...), custom_call_target="tpu_custom_call" | custom-call | tf_op jit(solution)/shard_map/pallas_call | solution.py:27
  (101 shorter events, 35.1 us)
Async XLA Ops:
  1.9 8.4 %collective-permute-start.1 = (bf16[128,1024]{1,0:T(8,128)(2,1)S(1)}, bf16[128,1024]{1,0:T(8,128)(2,1)S(1)}, u32[]{:S(2)}, u32[]{:S(2)}) collective-permute-start(bf16[128,1024]{1,0:T(8,128)(2,1)S(1)} %get-tuple-element.42.refs_0_), channel_id=1, source_target_pairs={{0,3},{1,0},{2,1},{3,2},{4,7},{5,4},{6,5},{7,6},{8,11},{9,8},{10,9... | collective-permute-start | bytes 786440 | tf_op jit(solution)/shard_map/ppermute | solution.py:54
  6.2 11.3 %collective-permute-start = (bf16[2,128,1024]{2,1,0:T(8,128)(2,1)S(1)}, bf16[2,128,1024]{2,1,0:T(8,128)(2,1)S(1)}, u32[]{:S(2)}, u32[]{:S(2)}) collective-permute-start(bf16[2,128,1024]{2,1,0:T(8,128)(2,1)S(1)} %shard_map.109.own.x0), channel_id=1, source_target_pairs={{0,4},{4,0},{1,5},{5,1},{2,6},{6,2},{3,7},{7,3},{8,12},{12,8},{9,1... | collective-permute-start | bytes 1572872 | tf_op jit(solution)/shard_map/ppermute | solution.py:54
  7.2 9.2 %collective-permute-start.4 = (bf16[128,1024]{1,0:T(8,128)(2,1)S(1)}, bf16[128,1024]{1,0:T(8,128)(2,1)S(1)}, u32[]{:S(2)}, u32[]{:S(2)}) collective-permute-start(bf16[128,1024]{1,0:T(8,128)(2,1)S(1)} %get-tuple-element.41.refs_1_), channel_id=1, source_target_pairs={{0,1},{1,2},{2,3},{3,0},{4,5},{5,6},{6,7},{7,4},{8,9},{9,10},{10,1... | collective-permute-start | bytes 786440 | tf_op jit(solution)/shard_map/ppermute | solution.py:54
  10.3 7.2 %collective-permute-start.2 = (bf16[128,1024]{1,0:T(8,128)(2,1)S(1)}, bf16[128,1024]{1,0:T(8,128)(2,1)S(1)}, u32[]{:S(2)}, u32[]{:S(2)}) collective-permute-start(bf16[128,1024]{1,0:T(8,128)(2,1)S(1)} %collective-permute-done.1.refs_2_), channel_id=1, source_target_pairs={{0,192},{64,0},{128,64},{192,128},{1,193},{65,1},{129,65},{193,129... | collective-permute-start | bytes 786440 | tf_op jit(solution)/shard_map/ppermute | solution.py:54
  13.0 7.3 %collective-permute-start.3 = (bf16[128,1024]{1,0:T(8,128)(2,1)S(1)}, bf16[128,1024]{1,0:T(8,128)(2,1)S(1)}, u32[]{:S(2)}, u32[]{:S(2)}) collective-permute-start(bf16[128,1024]{1,0:T(8,128)(2,1)S(1)} %collective-permute-done.1.refs_2_), channel_id=1, source_target_pairs={{0,3},{1,0},{2,1},{3,2},{4,7},{5,4},{6,5},{7,6},{8,11},{9,8},{10,9... | collective-permute-start | bytes 786440 | tf_op jit(solution)/shard_map/ppermute | solution.py:54
  16.4 7.1 %collective-permute-start.6 = (bf16[128,1024]{1,0:T(8,128)(2,1)S(1)}, bf16[128,1024]{1,0:T(8,128)(2,1)S(1)}, u32[]{:S(2)}, u32[]{:S(2)}) collective-permute-start(bf16[128,1024]{1,0:T(8,128)(2,1)S(1)} %collective-permute-done.4.refs_7_), channel_id=1, source_target_pairs={{0,64},{64,128},{128,192},{192,0},{1,65},{65,129},{129,193},{193,1... | collective-permute-start | bytes 786440 | tf_op jit(solution)/shard_map/ppermute | solution.py:54
  25.9 32.4 %all-to-all-start = ((bf16[8,256,128]{2,1,0:T(8,128)(2,1)}), bf16[8,256,128]{2,1,0:T(8,128)(2,1)S(1)}, u32[]{:S(2)}, u32[]{:S(2)}) async-start(bf16[8,256,128]{2,1,0:T(8,128)(2,1)} %get-tuple-element.21), calls=%async_computation | async-start | bytes 1048576 | tf_op jit(solution)/shard_map/all_to_all | solution.py:279
  34.1 23.0 %collective-permute-start.10 = (bf16[2,128,1024]{2,1,0:T(8,128)(2,1)S(1)}, bf16[2,128,1024]{2,1,0:T(8,128)(2,1)S(1)}, u32[]{:S(2)}, u32[]{:S(2)}) collective-permute-start(bf16[2,128,1024]{2,1,0:T(8,128)(2,1)S(1)} %shard_map.109.own.x0), channel_id=1, source_target_pairs={{0,8},{8,16},{16,24},{24,32},{32,40},{40,48},{48,56},{56,0},{4,60}... | collective-permute-start | bytes 1572872 | tf_op jit(solution)/shard_map/ppermute | solution.py:275
  36.8 24.4 %collective-permute-start.11 = (bf16[2,128,1024]{2,1,0:T(8,128)(2,1)S(1)}, bf16[2,128,1024]{2,1,0:T(8,128)(2,1)S(1)}, u32[]{:S(2)}, u32[]{:S(2)}) collective-permute-start(bf16[2,128,1024]{2,1,0:T(8,128)(2,1)S(1)} %shard_map.109.own.x0), channel_id=1, source_target_pairs={{0,56},{8,0},{16,8},{24,16},{32,24},{40,32},{48,40},{56,48},{4,12}... | collective-permute-start | bytes 1572872 | tf_op jit(solution)/shard_map/ppermute | solution.py:275
  57.1 10.2 %collective-permute-start.12 = (bf16[2,128,1024]{2,1,0:T(8,128)(2,1)S(1)}, bf16[2,128,1024]{2,1,0:T(8,128)(2,1)S(1)}, u32[]{:S(2)}, u32[]{:S(2)}) collective-permute-start(bf16[2,128,1024]{2,1,0:T(8,128)(2,1)S(1)} %collective-permute-done.10.f1), channel_id=1, source_target_pairs={{0,8},{8,16},{16,24},{24,32},{32,40},{40,48},{48,56},{56,0},{4,60}... | collective-permute-start | bytes 1572872 | tf_op jit(solution)/shard_map/ppermute | solution.py:275
  58.3 9.2 %collective-permute-start.7 = (bf16[2048,128]{1,0:T(8,128)(2,1)S(1)}, bf16[2048,128]{1,0:T(8,128)(2,1)S(1)}, u32[]{:S(2)}, u32[]{:S(2)}) collective-permute-start(bf16[2048,128]{1,0:T(8,128)(2,1)S(1)} %bitcast.34), channel_id=1, source_target_pairs={{0,4},{4,0},{1,5},{5,1},{2,6},{6,2},{3,7},{7,3},{8,12},{12,8},{9,1... | collective-permute-start | bytes 1572872 | tf_op jit(solution)/shard_map/ppermute | solution.py:54
  61.2 26.4 %collective-permute-start.13 = (bf16[2,128,1024]{2,1,0:T(8,128)(2,1)S(1)}, bf16[2,128,1024]{2,1,0:T(8,128)(2,1)S(1)}, u32[]{:S(2)}, u32[]{:S(2)}) collective-permute-start(bf16[2,128,1024]{2,1,0:T(8,128)(2,1)S(1)} %collective-permute-done.11.b1), channel_id=1, source_target_pairs={{0,56},{8,0},{16,8},{24,16},{32,24},{40,32},{48,40},{56,48},{4,12}... | collective-permute-start | bytes 1572872 | tf_op jit(solution)/shard_map/ppermute | solution.py:275
  67.3 20.3 %collective-permute-start.14 = (bf16[2,128,1024]{2,1,0:T(8,128)(2,1)S(1)}, bf16[2,128,1024]{2,1,0:T(8,128)(2,1)S(1)}, u32[]{:S(2)}, u32[]{:S(2)}) collective-permute-start(bf16[2,128,1024]{2,1,0:T(8,128)(2,1)S(1)} %collective-permute-done.12.f2), channel_id=1, source_target_pairs={{0,8},{8,16},{16,24},{24,32},{32,40},{40,48},{48,56},{56,0},{4,60}... | collective-permute-start | bytes 1572872 | tf_op jit(solution)/shard_map/ppermute | solution.py:275
  78.1 12.6 %collective-permute-start.8 = (bf16[3072,128]{1,0:T(8,128)(2,1)S(1)}, bf16[3072,128]{1,0:T(8,128)(2,1)S(1)}, u32[]{:S(2)}, u32[]{:S(2)}) collective-permute-start(bf16[3072,128]{1,0:T(8,128)(2,1)S(1)} %get-tuple-element.23.send), channel_id=1, source_target_pairs={{0,4},{4,0},{1,5},{5,1},{2,6},{6,2},{3,7},{7,3},{8,12},{12,8},{9,1... | collective-permute-start | bytes 2359304 | tf_op jit(solution)/shard_map/ppermute | solution.py:54
  87.6 11.9 %collective-permute-start.15 = (bf16[2,128,1024]{2,1,0:T(8,128)(2,1)S(1)}, bf16[2,128,1024]{2,1,0:T(8,128)(2,1)S(1)}, u32[]{:S(2)}, u32[]{:S(2)}) collective-permute-start(bf16[2,128,1024]{2,1,0:T(8,128)(2,1)S(1)} %collective-permute-done.13.b2), channel_id=1, source_target_pairs={{0,56},{8,0},{16,8},{24,16},{32,24},{40,32},{48,40},{56,48},{4,12}... | collective-permute-start | bytes 1572872 | tf_op jit(solution)/shard_map/ppermute | solution.py:275
  87.6 14.3 %collective-permute-start.16 = (bf16[2,128,1024]{2,1,0:T(8,128)(2,1)S(1)}, bf16[2,128,1024]{2,1,0:T(8,128)(2,1)S(1)}, u32[]{:S(2)}, u32[]{:S(2)}) collective-permute-start(bf16[2,128,1024]{2,1,0:T(8,128)(2,1)S(1)} %collective-permute-done.14.f3), channel_id=1, source_target_pairs={{0,8},{8,16},{16,24},{24,32},{32,40},{40,48},{48,56},{56,0},{4,60}... | collective-permute-start | bytes 1572872 | tf_op jit(solution)/shard_map/ppermute | solution.py:275
  108.2 31.4 %all-to-all-start.1 = ((bf16[8,256,128]{2,1,0:T(8,128)(2,1)}), bf16[8,256,128]{2,1,0:T(8,128)(2,1)S(1)}, u32[]{:S(2)}, u32[]{:S(2)}) async-start(bf16[8,256,128]{2,1,0:T(8,128)(2,1)} %bitcast.7), calls=%async_computation.1 | async-start | bytes 1048576 | tf_op jit(solution)/shard_map/all_to_all | solution.py:279
  132.2 7.0 %collective-permute-start.28 = (bf16[128,256]{1,0:T(8,128)(2,1)S(1)}, bf16[128,256]{1,0:T(8,128)(2,1)S(1)}, u32[]{:S(2)}, u32[]{:S(2)}) collective-permute-start(bf16[128,256]{1,0:T(8,128)(2,1)S(1)} %get-tuple-element.37.refs_0_), channel_id=1, source_target_pairs={{0,48},{8,56},{16,0},{24,8},{32,16},{40,24},{48,32},{56,40},{4,20}... | collective-permute-start | bytes 196616 | tf_op jit(solution)/shard_map/ppermute | solution.py:275
  132.2 10.0 %collective-permute-start.24 = (bf16[128,256]{1,0:T(8,128)(2,1)S(1)}, bf16[128,256]{1,0:T(8,128)(2,1)S(1)}, u32[]{:S(2)}, u32[]{:S(2)}) collective-permute-start(bf16[128,256]{1,0:T(8,128)(2,1)S(1)} %get-tuple-element.37.refs_0_), channel_id=1, source_target_pairs={{0,8},{8,16},{16,24},{24,32},{32,40},{40,48},{48,56},{56,0},{4,60}... | collective-permute-start | bytes 196616 | tf_op jit(solution)/shard_map/ppermute | solution.py:275
  134.9 12.1 %collective-permute-start.30 = (bf16[128,256]{1,0:T(8,128)(2,1)S(1)}, bf16[128,256]{1,0:T(8,128)(2,1)S(1)}, u32[]{:S(2)}, u32[]{:S(2)}) collective-permute-start(bf16[128,256]{1,0:T(8,128)(2,1)S(1)} %get-tuple-element.37.refs_0_), channel_id=1, source_target_pairs={{0,56},{8,0},{16,8},{24,16},{32,24},{40,32},{48,40},{56,48},{4,12}... | collective-permute-start | bytes 196616 | tf_op jit(solution)/shard_map/ppermute | solution.py:275
  134.9 12.3 %collective-permute-start.26 = (bf16[128,256]{1,0:T(8,128)(2,1)S(1)}, bf16[128,256]{1,0:T(8,128)(2,1)S(1)}, u32[]{:S(2)}, u32[]{:S(2)}) collective-permute-start(bf16[128,256]{1,0:T(8,128)(2,1)S(1)} %collective-permute-done.25.refs_2_), channel_id=1, source_target_pairs={{0,8},{8,16},{16,24},{24,32},{32,40},{40,48},{48,56},{56,0},{4,60}... | collective-permute-start | bytes 196616 | tf_op jit(solution)/shard_map/ppermute | solution.py:275
  137.6 9.6 %collective-permute-start.27 = (bf16[128,256]{1,0:T(8,128)(2,1)S(1)}, bf16[128,256]{1,0:T(8,128)(2,1)S(1)}, u32[]{:S(2)}, u32[]{:S(2)}) collective-permute-start(bf16[128,256]{1,0:T(8,128)(2,1)S(1)} %collective-permute-done.25.refs_2_), channel_id=1, source_target_pairs={{0,16},{8,24},{16,32},{24,40},{32,48},{40,56},{48,0},{56,8},{4,52}... | collective-permute-start | bytes 196616 | tf_op jit(solution)/shard_map/ppermute | solution.py:275
  139.2 8.0 %collective-permute-start.29 = (bf16[128,256]{1,0:T(8,128)(2,1)S(1)}, bf16[128,256]{1,0:T(8,128)(2,1)S(1)}, u32[]{:S(2)}, u32[]{:S(2)}) collective-permute-start(bf16[128,256]{1,0:T(8,128)(2,1)S(1)} %collective-permute-done.28.refs_6_), channel_id=1, source_target_pairs={{0,56},{8,0},{16,8},{24,16},{32,24},{40,32},{48,40},{56,48},{4,12}... | collective-permute-start | bytes 196616 | tf_op jit(solution)/shard_map/ppermute | solution.py:275
  142.2 10.4 %collective-permute-start.9 = (f32[2,128,1024]{2,1,0:T(8,128)S(1)}, f32[2,128,1024]{2,1,0:T(8,128)S(1)}, u32[]{:S(2)}, u32[]{:S(2)}) collective-permute-start(f32[2,128,1024]{2,1,0:T(8,128)S(1)} %get-tuple-element.26), channel_id=1, source_target_pairs={{0,4},{4,0},{1,5},{5,1},{2,6},{6,2},{3,7},{7,3},{8,12},{12,8},{9,1... | collective-permute-start | bytes 3145736 | tf_op jit(solution)/shard_map/ppermute | solution.py:54
  (29 other events, 254.1 us)

commit v4 on v3

--- a/solution.py
+++ b/solution.py
@@ -184,7 +184,7 @@
     return jnp.concatenate(one, axis=1), jnp.concatenate(two, axis=1)
 
 
-def outer_kernel(ids, columns, x0, f1, b1, f2, b2, f3, b3, f4, keep, send, acc_n, acc_u):
+def outer_kernel(ids, b3, f4, columns, x0, f1, b1, f2, b2, f3, keep, send, acc_n, acc_u):
     core, place = ids[0], ids[2]
 
     def chunk(step):
@@ -349,10 +349,10 @@
     share, foreign = call(
         outer_kernel,
         ids,
-        [],
+        [b3, f4],
         [((4, 128, 256), F32), ((4, 128, 256), BF16)],
         [pltpu.VMEM((1024, 256), F32), pltpu.VMEM((1024, 128), F32)],
-        far=[columns, own, f1, b1, f2, b2, f3, b3, f4],
+        far=[columns, own, f1, b1, f2, b2, f3],
     )
     foreign = pair(foreign)
     share = [(share[i] + foreign[i].astype(F32)).astype(BF16) for i in range(4)]

time: 154 us -> 153 us (level)
  no operation moved by 1% of the time
where the time goes in v4:
time: 153 us
  starting transfers between devices  69.9 us (46%)
  waiting for transfers between devices  54.8 us (36%)
  Pallas kernels  25.9 us (17%)
    ppermute x19, starting transfers between devices, shift(): lax.ppermute(value, axis, [(i, (i + by) % size) for i in range(size)])  39.9 us
    ppermute x14, waiting for transfers between devices, turn(): return lax.ppermute(value, ('z', 'core'), perm)  36.6 us
    pallas_call x8, Pallas kernels, call(): pl.pallas_call(kernel, in_specs=[smem()] + vmem(len(args)), out_specs=vme...  25.9 us
    ppermute x19, waiting for transfers between devices, shift(): lax.ppermute(value, axis, [(i, (i + by) % size) for i in range(size)])  18.2 us
    ppermute x14, starting transfers between devices, turn(): return lax.ppermute(value, ('z', 'core'), perm)  17.6 us
    all_to_all x2, starting transfers between devices, exchange(): return lax.all_to_all(value, axis, split_axis=0, concat_axis=0, tiled=True)  12.5 us
  transfers between devices with their start and end apart: 35, of which 16 were waited for; matrix products, arithmetic and copies ran while one was open for 0% of the time, Pallas kernels for 12%

profile of v4, /device:TPU:1, one launch (start us, length us, event | category | flops | bytes accessed | tf_op | source)
XLA Modules:
  0.0 153.1 jit_solution(63347485104257485)
XLA Ops:
  1.9 3.4 %collective-permute-start.1 = (bf16[128,1024]{1,0:T(8,128)(2,1)S(1)}, bf16[128,1024]{1,0:T(8,128)(2,1)S(1)}, u32[]{:S(2)}, u32[]{:S(2)}) collective-permute-start(bf16[128,1024]{1,0:T(8,128)(2,1)S(1)} %get-tuple-element.42.refs_0_), channel_id=1, source_target_pairs={{0,3},{1,0},{2,1},{3,2},{4,7},{5,4},{6,5},{7,6},{8,11},{9,8},{10,9... | collective-permute-start | bytes 786440 | tf_op jit(solution)/shard_map/ppermute | solution.py:54
  10.3 2.7 %collective-permute-start.2 = (bf16[128,1024]{1,0:T(8,128)(2,1)S(1)}, bf16[128,1024]{1,0:T(8,128)(2,1)S(1)}, u32[]{:S(2)}, u32[]{:S(2)}) collective-permute-start(bf16[128,1024]{1,0:T(8,128)(2,1)S(1)} %collective-permute-done.1.refs_2_), channel_id=1, source_target_pairs={{0,192},{64,0},{128,64},{192,128},{1,193},{65,1},{129,65},{193,129... | collective-permute-start | bytes 786440 | tf_op jit(solution)/shard_map/ppermute | solution.py:54
  13.0 3.4 %collective-permute-start.3 = (bf16[128,1024]{1,0:T(8,128)(2,1)S(1)}, bf16[128,1024]{1,0:T(8,128)(2,1)S(1)}, u32[]{:S(2)}, u32[]{:S(2)}) collective-permute-start(bf16[128,1024]{1,0:T(8,128)(2,1)S(1)} %collective-permute-done.1.refs_2_), channel_id=1, source_target_pairs={{0,3},{1,0},{2,1},{3,2},{4,7},{5,4},{6,5},{7,6},{8,11},{9,8},{10,9... | collective-permute-start | bytes 786440 | tf_op jit(solution)/shard_map/ppermute | solution.py:54
  17.5 2.8 %collective-permute-done.3.refs_4_ = bf16[128,1024]{1,0:T(8,128)(2,1)S(1)} collective-permute-done((bf16[128,1024]{1,0:T(8,128)(2,1)S(1)}, bf16[128,1024]{1,0:T(8,128)(2,1)S(1)}, u32[]{:S(2)}, u32[]{:S(2)}) %collective-permute-start.3) | collective-permute-done | bytes 262176 | tf_op jit(solution)/shard_map/ppermute | solution.py:54
  20.3 3.1 %collective-permute-done.5.refs_5_ = bf16[128,1024]{1,0:T(8,128)(2,1)S(1)} collective-permute-done((bf16[128,1024]{1,0:T(8,128)(2,1)S(1)}, bf16[128,1024]{1,0:T(8,128)(2,1)S(1)}, u32[]{:S(2)}, u32[]{:S(2)}) %collective-permute-start.5) | collective-permute-done | bytes 262176 | tf_op jit(solution)/shard_map/ppermute | solution.py:54
  25.9 8.2 %all-to-all-start = ((bf16[8,256,128]{2,1,0:T(8,128)(2,1)}), bf16[8,256,128]{2,1,0:T(8,128)(2,1)S(1)}, u32[]{:S(2)}, u32[]{:S(2)}) async-start(bf16[8,256,128]{2,1,0:T(8,128)(2,1)} %get-tuple-element.21), calls=%async_computation | async-start | bytes 1048576 | tf_op jit(solution)/shard_map/all_to_all | solution.py:279
  34.1 2.7 %collective-permute-start.13 = (bf16[2,128,1024]{2,1,0:T(8,128)(2,1)S(1)}, bf16[2,128,1024]{2,1,0:T(8,128)(2,1)S(1)}, u32[]{:S(2)}, u32[]{:S(2)}) collective-permute-start(bf16[2,128,1024]{2,1,0:T(8,128)(2,1)S(1)} %shard_map.109.own.x0), channel_id=1, source_target_pairs={{0,8},{8,16},{16,24},{24,32},{32,40},{40,48},{48,56},{56,0},{4,60}... | collective-permute-start | bytes 1572872 | tf_op jit(solution)/shard_map/ppermute | solution.py:275
  36.8 20.3 %collective-permute-done.13.f1 = bf16[2,128,1024]{2,1,0:T(8,128)(2,1)S(1)} collective-permute-done((bf16[2,128,1024]{2,1,0:T(8,128)(2,1)S(1)}, bf16[2,128,1024]{2,1,0:T(8,128)(2,1)S(1)}, u32[]{:S(2)}, u32[]{:S(2)}) %collective-permute-start.13) | collective-permute-done | bytes 524320 | tf_op jit(solution)/shard_map/ppermute | solution.py:275
  58.3 2.9 %collective-permute-start.7 = (bf16[2048,128]{1,0:T(8,128)(2,1)S(1)}, bf16[2048,128]{1,0:T(8,128)(2,1)S(1)}, u32[]{:S(2)}, u32[]{:S(2)}) collective-permute-start(bf16[2048,128]{1,0:T(8,128)(2,1)S(1)} %bitcast.34), channel_id=1, source_target_pairs={{0,4},{4,0},{1,5},{5,1},{2,6},{6,2},{3,7},{7,3},{8,12},{12,8},{9,1... | collective-permute-start | bytes 1572872 | tf_op jit(solution)/shard_map/ppermute | solution.py:54
  61.4 5.9 %collective-permute-done.14.f2 = bf16[2,128,1024]{2,1,0:T(8,128)(2,1)S(1)} collective-permute-done((bf16[2,128,1024]{2,1,0:T(8,128)(2,1)S(1)}, bf16[2,128,1024]{2,1,0:T(8,128)(2,1)S(1)}, u32[]{:S(2)}, u32[]{:S(2)}) %collective-permute-start.14) | collective-permute-done | bytes 524320 | tf_op jit(solution)/shard_map/ppermute | solution.py:275
  67.6 10.5 %shard_map.111 = (bf16[3072,128]{1,0:T(8,128)(2,1)S(1)}, f32[2048,128]{1,0:T(8,128)S(1)}) custom-call(s32[4]{0:T(128)S(1)} %pad_add_fusion.ids, bf16[2048,128]{1,0:T(8,128)(2,1)S(1)} %bitcast.35, bf16[2048,128]{1,0:T(8,128)(2,1)S(1)} %collective-permute-done.7.other), custom_call_target="tpu_custom_call" | custom-call | tf_op jit(solution)/shard_map/pallas_call | solution.py:27
  78.1 9.5 %collective-permute-start.8 = (bf16[3072,128]{1,0:T(8,128)(2,1)S(1)}, bf16[3072,128]{1,0:T(8,128)(2,1)S(1)}, u32[]{:S(2)}, u32[]{:S(2)}) collective-permute-start(bf16[3072,128]{1,0:T(8,128)(2,1)S(1)} %get-tuple-element.23.send), channel_id=1, source_target_pairs={{0,4},{4,0},{1,5},{5,1},{2,6},{6,2},{3,7},{7,3},{8,12},{12,8},{9,1... | collective-permute-start | bytes 2359304 | tf_op jit(solution)/shard_map/ppermute | solution.py:54
  87.6 3.0 %collective-permute-start.16 = (bf16[2,128,1024]{2,1,0:T(8,128)(2,1)S(1)}, bf16[2,128,1024]{2,1,0:T(8,128)(2,1)S(1)}, u32[]{:S(2)}, u32[]{:S(2)}) collective-permute-start(bf16[2,128,1024]{2,1,0:T(8,128)(2,1)S(1)} %collective-permute-done.15.f3), channel_id=1, source_target_pairs={{0,8},{8,16},{16,24},{24,32},{32,40},{40,48},{48,56},{56,0},{4,60}... | collective-permute-start | bytes 1572872 | tf_op jit(solution)/shard_map/ppermute | solution.py:275
  92.6 6.9 %collective-permute-done.12.b3 = bf16[2,128,1024]{2,1,0:T(8,128)(2,1)S(1)} collective-permute-done((bf16[2,128,1024]{2,1,0:T(8,128)(2,1)S(1)}, bf16[2,128,1024]{2,1,0:T(8,128)(2,1)S(1)}, u32[]{:S(2)}, u32[]{:S(2)}) %collective-permute-start.12) | collective-permute-done | bytes 524320 | tf_op jit(solution)/shard_map/ppermute | solution.py:275
  99.5 2.4 %collective-permute-done.16.f4 = bf16[2,128,1024]{2,1,0:T(8,128)(2,1)S(1)} collective-permute-done((bf16[2,128,1024]{2,1,0:T(8,128)(2,1)S(1)}, bf16[2,128,1024]{2,1,0:T(8,128)(2,1)S(1)}, u32[]{:S(2)}, u32[]{:S(2)}) %collective-permute-start.16) | collective-permute-done | bytes 524320 | tf_op jit(solution)/shard_map/ppermute | solution.py:275
  101.9 3.6 %shard_map.115 = (f32[4,128,256]{2,1,0:T(8,128)S(1)}, bf16[4,128,256]{2,1,0:T(8,128)(2,1)S(1)}) custom-call(s32[4]{0:T(128)S(1)} %pad_add_fusion.ids, bf16[2,128,1024]{2,1,0:T(8,128)(2,1)S(1)} %collective-permute-done.12.b3, bf16[2,128,1024]{2,1,0:T(8,128)(2,1)S(1)} %collective-permute-done.16.f4, bf16[2048,256]{1,0:T(8,128)(2,1)} %get-tuple-element.29.columns, ...), custom_call_target="tpu_custom_call" | custom-call | tf_op jit(solution)/shard_map/pallas_call | solution.py:27
  107.1 4.3 %all-to-all-start.1 = ((bf16[8,256,128]{2,1,0:T(8,128)(2,1)}), bf16[8,256,128]{2,1,0:T(8,128)(2,1)S(1)}, u32[]{:S(2)}, u32[]{:S(2)}) async-start(bf16[8,256,128]{2,1,0:T(8,128)(2,1)} %bitcast.7), calls=%async_computation.1 | async-start | bytes 1048576 | tf_op jit(solution)/shard_map/all_to_all | solution.py:279
  118.6 3.1 %collective-permute-start.23 = (bf16[128,256]{1,0:T(8,128)(2,1)S(1)}, bf16[128,256]{1,0:T(8,128)(2,1)S(1)}, u32[]{:S(2)}, u32[]{:S(2)}) collective-permute-start(bf16[128,256]{1,0:T(8,128)(2,1)S(1)} %fusion.3), channel_id=1, source_target_pairs={{0,128},{64,192},{128,0},{192,64},{1,129},{65,193},{129,1},{193,65... | collective-permute-start | bytes 196616 | tf_op jit(solution)/shard_map/ppermute | solution.py:54
  127.2 3.9 %collective-permute-start.25 = (bf16[128,256]{1,0:T(8,128)(2,1)S(1)}, bf16[128,256]{1,0:T(8,128)(2,1)S(1)}, u32[]{:S(2)}, u32[]{:S(2)}) collective-permute-start(bf16[128,256]{1,0:T(8,128)(2,1)S(1)} %get-tuple-element.37.refs_0_), channel_id=1, source_target_pairs={{0,16},{8,24},{16,32},{24,40},{32,48},{40,56},{48,0},{56,8},{4,52}... | collective-permute-start | bytes 196616 | tf_op jit(solution)/shard_map/ppermute | solution.py:275
  131.1 2.7 %collective-permute-start.24 = (bf16[128,256]{1,0:T(8,128)(2,1)S(1)}, bf16[128,256]{1,0:T(8,128)(2,1)S(1)}, u32[]{:S(2)}, u32[]{:S(2)}) collective-permute-start(bf16[128,256]{1,0:T(8,128)(2,1)S(1)} %get-tuple-element.37.refs_0_), channel_id=1, source_target_pairs={{0,8},{8,16},{16,24},{24,32},{32,40},{40,48},{48,56},{56,0},{4,60}... | collective-permute-start | bytes 196616 | tf_op jit(solution)/shard_map/ppermute | solution.py:275
  133.8 2.7 %collective-permute-start.26 = (bf16[128,256]{1,0:T(8,128)(2,1)S(1)}, bf16[128,256]{1,0:T(8,128)(2,1)S(1)}, u32[]{:S(2)}, u32[]{:S(2)}) collective-permute-start(bf16[128,256]{1,0:T(8,128)(2,1)S(1)} %collective-permute-done.25.refs_2_), channel_id=1, source_target_pairs={{0,8},{8,16},{16,24},{24,32},{32,40},{40,48},{48,56},{56,0},{4,60}... | collective-permute-start | bytes 196616 | tf_op jit(solution)/shard_map/ppermute | solution.py:275
  138.5 2.6 %shard_map.113 = (f32[2,128,1024]{2,1,0:T(8,128)S(1)}, f32[2,128,1024]{2,1,0:T(8,128)S(1)}) custom-call(s32[4]{0:T(128)S(1)} %pad_add_fusion.ids, bf16[8,256,128]{2,1,0:T(8,128)(2,1)S(1)} %all-to-all-done.1.heads, bf16[128,1024]{1,0:T(8,128)(2,1)} %copy-done.2, bf16[128,1024]{1,0:T(8,128)(2,1)} %copy-done.1, bf16[128,1024]{1,0:T(8,128)(2,1)} %copy-done.5, ...), custom_call_target="tpu_custom_call" | custom-call | tf_op jit(solution)/shard_map/pallas_call | solution.py:27
  141.1 4.8 %collective-permute-start.9 = (f32[2,128,1024]{2,1,0:T(8,128)S(1)}, f32[2,128,1024]{2,1,0:T(8,128)S(1)}, u32[]{:S(2)}, u32[]{:S(2)}) collective-permute-start(f32[2,128,1024]{2,1,0:T(8,128)S(1)} %get-tuple-element.26), channel_id=1, source_target_pairs={{0,4},{4,0},{1,5},{5,1},{2,6},{6,2},{3,7},{7,3},{8,12},{12,8},{9,1... | collective-permute-start | bytes 3145736 | tf_op jit(solution)/shard_map/ppermute | solution.py:54
  149.0 2.5 %shard_map.116 = (f32[256,512]{1,0:T(8,128)}, f32[256,512]{1,0:T(8,128)}, f32[256,512]{1,0:T(8,128)}, f32[256,512]{1,0:T(8,128)}) custom-call(s32[4]{0:T(128)S(1)} %pad_add_fusion.ids, bf16[128,256]{1,0:T(8,128)(2,1)S(1)} %get-tuple-element.37.refs_0_, bf16[128,256]{1,0:T(8,128)(2,1)S(1)} %collective-permute-done.24.refs_1_, ...), custom_call_target="tpu_custom_call" | custom-call | tf_op jit(solution)/shard_map/pallas_call | solution.py:27
  (97 shorter events, 34.4 us)
Async XLA Ops:
  1.9 8.4 %collective-permute-start.1 = (bf16[128,1024]{1,0:T(8,128)(2,1)S(1)}, bf16[128,1024]{1,0:T(8,128)(2,1)S(1)}, u32[]{:S(2)}, u32[]{:S(2)}) collective-permute-start(bf16[128,1024]{1,0:T(8,128)(2,1)S(1)} %get-tuple-element.42.refs_0_), channel_id=1, source_target_pairs={{0,3},{1,0},{2,1},{3,2},{4,7},{5,4},{6,5},{7,6},{8,11},{9,8},{10,9... | collective-permute-start | bytes 786440 | tf_op jit(solution)/shard_map/ppermute | solution.py:54
  6.2 11.3 %collective-permute-start = (bf16[2,128,1024]{2,1,0:T(8,128)(2,1)S(1)}, bf16[2,128,1024]{2,1,0:T(8,128)(2,1)S(1)}, u32[]{:S(2)}, u32[]{:S(2)}) collective-permute-start(bf16[2,128,1024]{2,1,0:T(8,128)(2,1)S(1)} %shard_map.109.own.x0), channel_id=1, source_target_pairs={{0,4},{4,0},{1,5},{5,1},{2,6},{6,2},{3,7},{7,3},{8,12},{12,8},{9,1... | collective-permute-start | bytes 1572872 | tf_op jit(solution)/shard_map/ppermute | solution.py:54
  7.2 9.2 %collective-permute-start.4 = (bf16[128,1024]{1,0:T(8,128)(2,1)S(1)}, bf16[128,1024]{1,0:T(8,128)(2,1)S(1)}, u32[]{:S(2)}, u32[]{:S(2)}) collective-permute-start(bf16[128,1024]{1,0:T(8,128)(2,1)S(1)} %get-tuple-element.41.refs_1_), channel_id=1, source_target_pairs={{0,1},{1,2},{2,3},{3,0},{4,5},{5,6},{6,7},{7,4},{8,9},{9,10},{10,1... | collective-permute-start | bytes 786440 | tf_op jit(solution)/shard_map/ppermute | solution.py:54
  10.3 7.2 %collective-permute-start.2 = (bf16[128,1024]{1,0:T(8,128)(2,1)S(1)}, bf16[128,1024]{1,0:T(8,128)(2,1)S(1)}, u32[]{:S(2)}, u32[]{:S(2)}) collective-permute-start(bf16[128,1024]{1,0:T(8,128)(2,1)S(1)} %collective-permute-done.1.refs_2_), channel_id=1, source_target_pairs={{0,192},{64,0},{128,64},{192,128},{1,193},{65,1},{129,65},{193,129... | collective-permute-start | bytes 786440 | tf_op jit(solution)/shard_map/ppermute | solution.py:54
  13.0 7.3 %collective-permute-start.3 = (bf16[128,1024]{1,0:T(8,128)(2,1)S(1)}, bf16[128,1024]{1,0:T(8,128)(2,1)S(1)}, u32[]{:S(2)}, u32[]{:S(2)}) collective-permute-start(bf16[128,1024]{1,0:T(8,128)(2,1)S(1)} %collective-permute-done.1.refs_2_), channel_id=1, source_target_pairs={{0,3},{1,0},{2,1},{3,2},{4,7},{5,4},{6,5},{7,6},{8,11},{9,8},{10,9... | collective-permute-start | bytes 786440 | tf_op jit(solution)/shard_map/ppermute | solution.py:54
  16.4 7.1 %collective-permute-start.6 = (bf16[128,1024]{1,0:T(8,128)(2,1)S(1)}, bf16[128,1024]{1,0:T(8,128)(2,1)S(1)}, u32[]{:S(2)}, u32[]{:S(2)}) collective-permute-start(bf16[128,1024]{1,0:T(8,128)(2,1)S(1)} %collective-permute-done.4.refs_7_), channel_id=1, source_target_pairs={{0,64},{64,128},{128,192},{192,0},{1,65},{65,129},{129,193},{193,1... | collective-permute-start | bytes 786440 | tf_op jit(solution)/shard_map/ppermute | solution.py:54
  25.9 32.4 %all-to-all-start = ((bf16[8,256,128]{2,1,0:T(8,128)(2,1)}), bf16[8,256,128]{2,1,0:T(8,128)(2,1)S(1)}, u32[]{:S(2)}, u32[]{:S(2)}) async-start(bf16[8,256,128]{2,1,0:T(8,128)(2,1)} %get-tuple-element.21), calls=%async_computation | async-start | bytes 1048576 | tf_op jit(solution)/shard_map/all_to_all | solution.py:279
  34.1 23.0 %collective-permute-start.13 = (bf16[2,128,1024]{2,1,0:T(8,128)(2,1)S(1)}, bf16[2,128,1024]{2,1,0:T(8,128)(2,1)S(1)}, u32[]{:S(2)}, u32[]{:S(2)}) collective-permute-start(bf16[2,128,1024]{2,1,0:T(8,128)(2,1)S(1)} %shard_map.109.own.x0), channel_id=1, source_target_pairs={{0,8},{8,16},{16,24},{24,32},{32,40},{40,48},{48,56},{56,0},{4,60}... | collective-permute-start | bytes 1572872 | tf_op jit(solution)/shard_map/ppermute | solution.py:275
  36.8 24.4 %collective-permute-start.10 = (bf16[2,128,1024]{2,1,0:T(8,128)(2,1)S(1)}, bf16[2,128,1024]{2,1,0:T(8,128)(2,1)S(1)}, u32[]{:S(2)}, u32[]{:S(2)}) collective-permute-start(bf16[2,128,1024]{2,1,0:T(8,128)(2,1)S(1)} %shard_map.109.own.x0), channel_id=1, source_target_pairs={{0,56},{8,0},{16,8},{24,16},{32,24},{40,32},{48,40},{56,48},{4,12}... | collective-permute-start | bytes 1572872 | tf_op jit(solution)/shard_map/ppermute | solution.py:275
  57.1 10.2 %collective-permute-start.14 = (bf16[2,128,1024]{2,1,0:T(8,128)(2,1)S(1)}, bf16[2,128,1024]{2,1,0:T(8,128)(2,1)S(1)}, u32[]{:S(2)}, u32[]{:S(2)}) collective-permute-start(bf16[2,128,1024]{2,1,0:T(8,128)(2,1)S(1)} %collective-permute-done.13.f1), channel_id=1, source_target_pairs={{0,8},{8,16},{16,24},{24,32},{32,40},{40,48},{48,56},{56,0},{4,60}... | collective-permute-start | bytes 1572872 | tf_op jit(solution)/shard_map/ppermute | solution.py:275
  58.3 9.2 %collective-permute-start.7 = (bf16[2048,128]{1,0:T(8,128)(2,1)S(1)}, bf16[2048,128]{1,0:T(8,128)(2,1)S(1)}, u32[]{:S(2)}, u32[]{:S(2)}) collective-permute-start(bf16[2048,128]{1,0:T(8,128)(2,1)S(1)} %bitcast.34), channel_id=1, source_target_pairs={{0,4},{4,0},{1,5},{5,1},{2,6},{6,2},{3,7},{7,3},{8,12},{12,8},{9,1... | collective-permute-start | bytes 1572872 | tf_op jit(solution)/shard_map/ppermute | solution.py:54
  61.2 26.4 %collective-permute-start.11 = (bf16[2,128,1024]{2,1,0:T(8,128)(2,1)S(1)}, bf16[2,128,1024]{2,1,0:T(8,128)(2,1)S(1)}, u32[]{:S(2)}, u32[]{:S(2)}) collective-permute-start(bf16[2,128,1024]{2,1,0:T(8,128)(2,1)S(1)} %collective-permute-done.10.b1), channel_id=1, source_target_pairs={{0,56},{8,0},{16,8},{24,16},{32,24},{40,32},{48,40},{56,48},{4,12}... | collective-permute-start | bytes 1572872 | tf_op jit(solution)/shard_map/ppermute | solution.py:275
  67.3 20.3 %collective-permute-start.15 = (bf16[2,128,1024]{2,1,0:T(8,128)(2,1)S(1)}, bf16[2,128,1024]{2,1,0:T(8,128)(2,1)S(1)}, u32[]{:S(2)}, u32[]{:S(2)}) collective-permute-start(bf16[2,128,1024]{2,1,0:T(8,128)(2,1)S(1)} %collective-permute-done.14.f2), channel_id=1, source_target_pairs={{0,8},{8,16},{16,24},{24,32},{32,40},{40,48},{48,56},{56,0},{4,60}... | collective-permute-start | bytes 1572872 | tf_op jit(solution)/shard_map/ppermute | solution.py:275
  78.1 12.6 %collective-permute-start.8 = (bf16[3072,128]{1,0:T(8,128)(2,1)S(1)}, bf16[3072,128]{1,0:T(8,128)(2,1)S(1)}, u32[]{:S(2)}, u32[]{:S(2)}) collective-permute-start(bf16[3072,128]{1,0:T(8,128)(2,1)S(1)} %get-tuple-element.23.send), channel_id=1, source_target_pairs={{0,4},{4,0},{1,5},{5,1},{2,6},{6,2},{3,7},{7,3},{8,12},{12,8},{9,1... | collective-permute-start | bytes 2359304 | tf_op jit(solution)/shard_map/ppermute | solution.py:54
  87.6 11.9 %collective-permute-start.12 = (bf16[2,128,1024]{2,1,0:T(8,128)(2,1)S(1)}, bf16[2,128,1024]{2,1,0:T(8,128)(2,1)S(1)}, u32[]{:S(2)}, u32[]{:S(2)}) collective-permute-start(bf16[2,128,1024]{2,1,0:T(8,128)(2,1)S(1)} %collective-permute-done.11.b2), channel_id=1, source_target_pairs={{0,56},{8,0},{16,8},{24,16},{32,24},{40,32},{48,40},{56,48},{4,12}... | collective-permute-start | bytes 1572872 | tf_op jit(solution)/shard_map/ppermute | solution.py:275
  87.6 14.3 %collective-permute-start.16 = (bf16[2,128,1024]{2,1,0:T(8,128)(2,1)S(1)}, bf16[2,128,1024]{2,1,0:T(8,128)(2,1)S(1)}, u32[]{:S(2)}, u32[]{:S(2)}) collective-permute-start(bf16[2,128,1024]{2,1,0:T(8,128)(2,1)S(1)} %collective-permute-done.15.f3), channel_id=1, source_target_pairs={{0,8},{8,16},{16,24},{24,32},{32,40},{40,48},{48,56},{56,0},{4,60}... | collective-permute-start | bytes 1572872 | tf_op jit(solution)/shard_map/ppermute | solution.py:275
  107.1 31.4 %all-to-all-start.1 = ((bf16[8,256,128]{2,1,0:T(8,128)(2,1)}), bf16[8,256,128]{2,1,0:T(8,128)(2,1)S(1)}, u32[]{:S(2)}, u32[]{:S(2)}) async-start(bf16[8,256,128]{2,1,0:T(8,128)(2,1)} %bitcast.7), calls=%async_computation.1 | async-start | bytes 1048576 | tf_op jit(solution)/shard_map/all_to_all | solution.py:279
  131.1 7.0 %collective-permute-start.28 = (bf16[128,256]{1,0:T(8,128)(2,1)S(1)}, bf16[128,256]{1,0:T(8,128)(2,1)S(1)}, u32[]{:S(2)}, u32[]{:S(2)}) collective-permute-start(bf16[128,256]{1,0:T(8,128)(2,1)S(1)} %get-tuple-element.37.refs_0_), channel_id=1, source_target_pairs={{0,48},{8,56},{16,0},{24,8},{32,16},{40,24},{48,32},{56,40},{4,20}... | collective-permute-start | bytes 196616 | tf_op jit(solution)/shard_map/ppermute | solution.py:275
  131.1 10.0 %collective-permute-start.24 = (bf16[128,256]{1,0:T(8,128)(2,1)S(1)}, bf16[128,256]{1,0:T(8,128)(2,1)S(1)}, u32[]{:S(2)}, u32[]{:S(2)}) collective-permute-start(bf16[128,256]{1,0:T(8,128)(2,1)S(1)} %get-tuple-element.37.refs_0_), channel_id=1, source_target_pairs={{0,8},{8,16},{16,24},{24,32},{32,40},{40,48},{48,56},{56,0},{4,60}... | collective-permute-start | bytes 196616 | tf_op jit(solution)/shard_map/ppermute | solution.py:275
  133.8 12.1 %collective-permute-start.30 = (bf16[128,256]{1,0:T(8,128)(2,1)S(1)}, bf16[128,256]{1,0:T(8,128)(2,1)S(1)}, u32[]{:S(2)}, u32[]{:S(2)}) collective-permute-start(bf16[128,256]{1,0:T(8,128)(2,1)S(1)} %get-tuple-element.37.refs_0_), channel_id=1, source_target_pairs={{0,56},{8,0},{16,8},{24,16},{32,24},{40,32},{48,40},{56,48},{4,12}... | collective-permute-start | bytes 196616 | tf_op jit(solution)/shard_map/ppermute | solution.py:275
  133.8 12.3 %collective-permute-start.26 = (bf16[128,256]{1,0:T(8,128)(2,1)S(1)}, bf16[128,256]{1,0:T(8,128)(2,1)S(1)}, u32[]{:S(2)}, u32[]{:S(2)}) collective-permute-start(bf16[128,256]{1,0:T(8,128)(2,1)S(1)} %collective-permute-done.25.refs_2_), channel_id=1, source_target_pairs={{0,8},{8,16},{16,24},{24,32},{32,40},{40,48},{48,56},{56,0},{4,60}... | collective-permute-start | bytes 196616 | tf_op jit(solution)/shard_map/ppermute | solution.py:275
  136.5 9.6 %collective-permute-start.27 = (bf16[128,256]{1,0:T(8,128)(2,1)S(1)}, bf16[128,256]{1,0:T(8,128)(2,1)S(1)}, u32[]{:S(2)}, u32[]{:S(2)}) collective-permute-start(bf16[128,256]{1,0:T(8,128)(2,1)S(1)} %collective-permute-done.25.refs_2_), channel_id=1, source_target_pairs={{0,16},{8,24},{16,32},{24,40},{32,48},{40,56},{48,0},{56,8},{4,52}... | collective-permute-start | bytes 196616 | tf_op jit(solution)/shard_map/ppermute | solution.py:275
  138.1 8.0 %collective-permute-start.29 = (bf16[128,256]{1,0:T(8,128)(2,1)S(1)}, bf16[128,256]{1,0:T(8,128)(2,1)S(1)}, u32[]{:S(2)}, u32[]{:S(2)}) collective-permute-start(bf16[128,256]{1,0:T(8,128)(2,1)S(1)} %collective-permute-done.28.refs_6_), channel_id=1, source_target_pairs={{0,56},{8,0},{16,8},{24,16},{32,24},{40,32},{48,40},{56,48},{4,12}... | collective-permute-start | bytes 196616 | tf_op jit(solution)/shard_map/ppermute | solution.py:275
  141.1 10.4 %collective-permute-start.9 = (f32[2,128,1024]{2,1,0:T(8,128)S(1)}, f32[2,128,1024]{2,1,0:T(8,128)S(1)}, u32[]{:S(2)}, u32[]{:S(2)}) collective-permute-start(f32[2,128,1024]{2,1,0:T(8,128)S(1)} %get-tuple-element.26), channel_id=1, source_target_pairs={{0,4},{4,0},{1,5},{5,1},{2,6},{6,2},{3,7},{7,3},{8,12},{12,8},{9,1... | collective-permute-start | bytes 3145736 | tf_op jit(solution)/shard_map/ppermute | solution.py:54
  (27 other events, 250.8 us)

commit v5 on v4

--- a/solution.py
+++ b/solution.py
@@ -21,14 +21,14 @@
     return pl.BlockSpec(memory_space=pltpu.SMEM)
 
 
-def call(kernel, ids, args, outs, scratch=(), limit=12, shape=pltpu.VMEM, far=()):
+def call(kernel, ids, args, outs, scratch=(), limit=12, shape=(pltpu.VMEM,) * 4, far=()):
     spaces = [pltpu.VMEM] * len(args) + [pltpu.HBM] * len(far)
     args = [pltpu.with_memory_space_constraint(a, m) for a, m in zip([*args, *far], spaces)]
     return pl.pallas_call(
         kernel,
         in_specs=[smem()] + vmem(len(args)),
         out_specs=vmem(len(outs)),
-        out_shape=[shape(s, d) for s, d in outs],
+        out_shape=[m(s, d) for m, (s, d) in zip(shape, outs)],
         scratch_shapes=list(scratch),
         compiler_params=pltpu.CompilerParams(vmem_limit_bytes=limit << 20),
     )(ids, *args)
@@ -184,7 +184,7 @@
     return jnp.concatenate(one, axis=1), jnp.concatenate(two, axis=1)
 
 
-def outer_kernel(ids, b3, f4, columns, x0, f1, b1, f2, b2, f3, keep, send, acc_n, acc_u):
+def outer_kernel(ids, columns, b3, f4, x0, f1, b1, f2, b2, f3, keep, send, acc_n, acc_u):
     core, place = ids[0], ids[2]
 
     def chunk(step):
@@ -327,7 +327,7 @@
         ids,
         [keep, send, recv],
         [((2048, 128), BF16), ((2048, 256), BF16)],
-        shape=pltpu.HBM,
+        shape=(pltpu.HBM, pltpu.VMEM),
     )
     grads = exchange(moved.reshape(8, 256, 128), "z")
     kept, sent = call(
@@ -344,15 +344,15 @@
         ids,
         [sig, up, kept, got],
         [((128, 1024), BF16), ((128, 1024), BF16)],
-        shape=pltpu.HBM,
+        shape=(pltpu.HBM,) * 4,
     )
     share, foreign = call(
         outer_kernel,
         ids,
-        [b3, f4],
+        [columns, b3, f4],
         [((4, 128, 256), F32), ((4, 128, 256), BF16)],
         [pltpu.VMEM((1024, 256), F32), pltpu.VMEM((1024, 128), F32)],
-        far=[columns, own, f1, b1, f2, b2, f3],
+        far=[own, f1, b1, f2, b2, f3],
     )
     foreign = pair(foreign)
     share = [(share[i] + foreign[i].astype(F32)).astype(BF16) for i in range(4)]
@@ -375,7 +375,7 @@
         pieces + across,
         [((256, 512), F32)] * 4,
         [pltpu.VMEM((8, 128, 256), BF16)],
-        shape=pltpu.HBM,
+        shape=(pltpu.HBM,) * 4,
     )
     return (out[None], grad[None], *shares)
 

time: 153 us -> 153 us (level)
  no operation moved by 1% of the time
where the time goes in v5:
time: 153 us
  starting transfers between devices  69.7 us (46%)
  waiting for transfers between devices  55.2 us (36%)
  Pallas kernels  25.2 us (16%)
    ppermute x19, starting transfers between devices, shift(): lax.ppermute(value, axis, [(i, (i + by) % size) for i in range(size)])  39.7 us
    ppermute x14, waiting for transfers between devices, turn(): return lax.ppermute(value, ('z', 'core'), perm)  37 us
    pallas_call x8, Pallas kernels, call(): pl.pallas_call(kernel, in_specs=[smem()] + vmem(len(args)), out_specs=vme...  25.2 us
    ppermute x19, waiting for transfers between devices, shift(): lax.ppermute(value, axis, [(i, (i + by) % size) for i in range(size)])  18.2 us
    ppermute x14, starting transfers between devices, turn(): return lax.ppermute(value, ('z', 'core'), perm)  17.6 us
    all_to_all x2, starting transfers between devices, exchange(): return lax.all_to_all(value, axis, split_axis=0, concat_axis=0, tiled=True)  12.5 us
  transfers between devices with their start and end apart: 35, of which 16 were waited for; matrix products, arithmetic and copies ran while one was open for 0% of the time, Pallas kernels for 12%

profile of v5, /device:TPU:1, one launch (start us, length us, event | category | flops | bytes accessed | tf_op | source)
XLA Modules:
  0.0 152.5 jit_solution(690889734072593417)
XLA Ops:
  1.9 3.4 %collective-permute-start.1 = (bf16[128,1024]{1,0:T(8,128)(2,1)S(1)}, bf16[128,1024]{1,0:T(8,128)(2,1)S(1)}, u32[]{:S(2)}, u32[]{:S(2)}) collective-permute-start(bf16[128,1024]{1,0:T(8,128)(2,1)S(1)} %get-tuple-element.42.refs_0_), channel_id=1, source_target_pairs={{0,3},{1,0},{2,1},{3,2},{4,7},{5,4},{6,5},{7,6},{8,11},{9,8},{10,9... | collective-permute-start | bytes 786440 | tf_op jit(solution)/shard_map/ppermute | solution.py:54
  10.3 2.7 %collective-permute-start.2 = (bf16[128,1024]{1,0:T(8,128)(2,1)S(1)}, bf16[128,1024]{1,0:T(8,128)(2,1)S(1)}, u32[]{:S(2)}, u32[]{:S(2)}) collective-permute-start(bf16[128,1024]{1,0:T(8,128)(2,1)S(1)} %collective-permute-done.1.refs_2_), channel_id=1, source_target_pairs={{0,192},{64,0},{128,64},{192,128},{1,193},{65,1},{129,65},{193,129... | collective-permute-start | bytes 786440 | tf_op jit(solution)/shard_map/ppermute | solution.py:54
  13.0 3.4 %collective-permute-start.3 = (bf16[128,1024]{1,0:T(8,128)(2,1)S(1)}, bf16[128,1024]{1,0:T(8,128)(2,1)S(1)}, u32[]{:S(2)}, u32[]{:S(2)}) collective-permute-start(bf16[128,1024]{1,0:T(8,128)(2,1)S(1)} %collective-permute-done.1.refs_2_), channel_id=1, source_target_pairs={{0,3},{1,0},{2,1},{3,2},{4,7},{5,4},{6,5},{7,6},{8,11},{9,8},{10,9... | collective-permute-start | bytes 786440 | tf_op jit(solution)/shard_map/ppermute | solution.py:54
  17.5 2.8 %collective-permute-done.3.refs_4_ = bf16[128,1024]{1,0:T(8,128)(2,1)S(1)} collective-permute-done((bf16[128,1024]{1,0:T(8,128)(2,1)S(1)}, bf16[128,1024]{1,0:T(8,128)(2,1)S(1)}, u32[]{:S(2)}, u32[]{:S(2)}) %collective-permute-start.3) | collective-permute-done | bytes 262176 | tf_op jit(solution)/shard_map/ppermute | solution.py:54
  20.3 3.1 %collective-permute-done.5.refs_5_ = bf16[128,1024]{1,0:T(8,128)(2,1)S(1)} collective-permute-done((bf16[128,1024]{1,0:T(8,128)(2,1)S(1)}, bf16[128,1024]{1,0:T(8,128)(2,1)S(1)}, u32[]{:S(2)}, u32[]{:S(2)}) %collective-permute-start.5) | collective-permute-done | bytes 262176 | tf_op jit(solution)/shard_map/ppermute | solution.py:54
  25.9 8.2 %all-to-all-start = ((bf16[8,256,128]{2,1,0:T(8,128)(2,1)}), bf16[8,256,128]{2,1,0:T(8,128)(2,1)S(1)}, u32[]{:S(2)}, u32[]{:S(2)}) async-start(bf16[8,256,128]{2,1,0:T(8,128)(2,1)} %get-tuple-element.21), calls=%async_computation | async-start | bytes 1048576 | tf_op jit(solution)/shard_map/all_to_all | solution.py:279
  34.1 2.7 %collective-permute-start.13 = (bf16[2,128,1024]{2,1,0:T(8,128)(2,1)S(1)}, bf16[2,128,1024]{2,1,0:T(8,128)(2,1)S(1)}, u32[]{:S(2)}, u32[]{:S(2)}) collective-permute-start(bf16[2,128,1024]{2,1,0:T(8,128)(2,1)S(1)} %shard_map.109.own.x0), channel_id=1, source_target_pairs={{0,8},{8,16},{16,24},{24,32},{32,40},{40,48},{48,56},{56,0},{4,60}... | collective-permute-start | bytes 1572872 | tf_op jit(solution)/shard_map/ppermute | solution.py:275
  36.8 20.3 %collective-permute-done.13.f1 = bf16[2,128,1024]{2,1,0:T(8,128)(2,1)S(1)} collective-permute-done((bf16[2,128,1024]{2,1,0:T(8,128)(2,1)S(1)}, bf16[2,128,1024]{2,1,0:T(8,128)(2,1)S(1)}, u32[]{:S(2)}, u32[]{:S(2)}) %collective-permute-start.13) | collective-permute-done | bytes 524320 | tf_op jit(solution)/shard_map/ppermute | solution.py:275
  58.3 2.9 %collective-permute-start.7 = (bf16[2048,128]{1,0:T(8,128)(2,1)S(1)}, bf16[2048,128]{1,0:T(8,128)(2,1)S(1)}, u32[]{:S(2)}, u32[]{:S(2)}) collective-permute-start(bf16[2048,128]{1,0:T(8,128)(2,1)S(1)} %bitcast.34), channel_id=1, source_target_pairs={{0,4},{4,0},{1,5},{5,1},{2,6},{6,2},{3,7},{7,3},{8,12},{12,8},{9,1... | collective-permute-start | bytes 1572872 | tf_op jit(solution)/shard_map/ppermute | solution.py:54
  61.4 5.9 %collective-permute-done.14.f2 = bf16[2,128,1024]{2,1,0:T(8,128)(2,1)S(1)} collective-permute-done((bf16[2,128,1024]{2,1,0:T(8,128)(2,1)S(1)}, bf16[2,128,1024]{2,1,0:T(8,128)(2,1)S(1)}, u32[]{:S(2)}, u32[]{:S(2)}) %collective-permute-start.14) | collective-permute-done | bytes 524320 | tf_op jit(solution)/shard_map/ppermute | solution.py:275
  67.6 10.5 %shard_map.111 = (bf16[3072,128]{1,0:T(8,128)(2,1)S(1)}, f32[2048,128]{1,0:T(8,128)S(1)}) custom-call(s32[4]{0:T(128)S(1)} %pad_add_fusion.ids, bf16[2048,128]{1,0:T(8,128)(2,1)S(1)} %bitcast.35, bf16[2048,128]{1,0:T(8,128)(2,1)S(1)} %collective-permute-done.7.other), custom_call_target="tpu_custom_call" | custom-call | tf_op jit(solution)/shard_map/pallas_call | solution.py:27
  78.1 9.5 %collective-permute-start.8 = (bf16[3072,128]{1,0:T(8,128)(2,1)S(1)}, bf16[3072,128]{1,0:T(8,128)(2,1)S(1)}, u32[]{:S(2)}, u32[]{:S(2)}) collective-permute-start(bf16[3072,128]{1,0:T(8,128)(2,1)S(1)} %get-tuple-element.23.send), channel_id=1, source_target_pairs={{0,4},{4,0},{1,5},{5,1},{2,6},{6,2},{3,7},{7,3},{8,12},{12,8},{9,1... | collective-permute-start | bytes 2359304 | tf_op jit(solution)/shard_map/ppermute | solution.py:54
  87.6 3.0 %collective-permute-start.16 = (bf16[2,128,1024]{2,1,0:T(8,128)(2,1)S(1)}, bf16[2,128,1024]{2,1,0:T(8,128)(2,1)S(1)}, u32[]{:S(2)}, u32[]{:S(2)}) collective-permute-start(bf16[2,128,1024]{2,1,0:T(8,128)(2,1)S(1)} %collective-permute-done.15.f3), channel_id=1, source_target_pairs={{0,8},{8,16},{16,24},{24,32},{32,40},{40,48},{48,56},{56,0},{4,60}... | collective-permute-start | bytes 1572872 | tf_op jit(solution)/shard_map/ppermute | solution.py:275
  92.2 7.3 %collective-permute-done.12.b3 = bf16[2,128,1024]{2,1,0:T(8,128)(2,1)S(1)} collective-permute-done((bf16[2,128,1024]{2,1,0:T(8,128)(2,1)S(1)}, bf16[2,128,1024]{2,1,0:T(8,128)(2,1)S(1)}, u32[]{:S(2)}, u32[]{:S(2)}) %collective-permute-start.12) | collective-permute-done | bytes 524320 | tf_op jit(solution)/shard_map/ppermute | solution.py:275
  99.5 2.4 %collective-permute-done.16.f4 = bf16[2,128,1024]{2,1,0:T(8,128)(2,1)S(1)} collective-permute-done((bf16[2,128,1024]{2,1,0:T(8,128)(2,1)S(1)}, bf16[2,128,1024]{2,1,0:T(8,128)(2,1)S(1)}, u32[]{:S(2)}, u32[]{:S(2)}) %collective-permute-start.16) | collective-permute-done | bytes 524320 | tf_op jit(solution)/shard_map/ppermute | solution.py:275
  101.9 3.3 %shard_map.115 = (f32[4,128,256]{2,1,0:T(8,128)S(1)}, bf16[4,128,256]{2,1,0:T(8,128)(2,1)S(1)}) custom-call(s32[4]{0:T(128)S(1)} %pad_add_fusion.ids, bf16[2048,256]{1,0:T(8,128)(2,1)S(1)} %get-tuple-element.29.columns, bf16[2,128,1024]{2,1,0:T(8,128)(2,1)S(1)} %collective-permute-done.12.b3, bf16[2,128,1024]{2,1,0:T(8,128)(2,1)S(1)} %collective-permute-done.16.f4, ...), custom_call_target="tpu_custom_call" | custom-call | tf_op jit(solution)/shard_map/pallas_call | solution.py:27
  106.8 4.3 %all-to-all-start.1 = ((bf16[8,256,128]{2,1,0:T(8,128)(2,1)}), bf16[8,256,128]{2,1,0:T(8,128)(2,1)S(1)}, u32[]{:S(2)}, u32[]{:S(2)}) async-start(bf16[8,256,128]{2,1,0:T(8,128)(2,1)} %bitcast.7), calls=%async_computation.1 | async-start | bytes 1048576 | tf_op jit(solution)/shard_map/all_to_all | solution.py:279
  118.3 2.9 %collective-permute-start.23 = (bf16[128,256]{1,0:T(8,128)(2,1)S(1)}, bf16[128,256]{1,0:T(8,128)(2,1)S(1)}, u32[]{:S(2)}, u32[]{:S(2)}) collective-permute-start(bf16[128,256]{1,0:T(8,128)(2,1)S(1)} %fusion.3), channel_id=1, source_target_pairs={{0,128},{64,192},{128,0},{192,64},{1,129},{65,193},{129,1},{193,65... | collective-permute-start | bytes 196616 | tf_op jit(solution)/shard_map/ppermute | solution.py:54
  126.6 3.9 %collective-permute-start.25 = (bf16[128,256]{1,0:T(8,128)(2,1)S(1)}, bf16[128,256]{1,0:T(8,128)(2,1)S(1)}, u32[]{:S(2)}, u32[]{:S(2)}) collective-permute-start(bf16[128,256]{1,0:T(8,128)(2,1)S(1)} %get-tuple-element.37.refs_0_), channel_id=1, source_target_pairs={{0,16},{8,24},{16,32},{24,40},{32,48},{40,56},{48,0},{56,8},{4,52}... | collective-permute-start | bytes 196616 | tf_op jit(solution)/shard_map/ppermute | solution.py:275
  130.6 2.7 %collective-permute-start.24 = (bf16[128,256]{1,0:T(8,128)(2,1)S(1)}, bf16[128,256]{1,0:T(8,128)(2,1)S(1)}, u32[]{:S(2)}, u32[]{:S(2)}) collective-permute-start(bf16[128,256]{1,0:T(8,128)(2,1)S(1)} %get-tuple-element.37.refs_0_), channel_id=1, source_target_pairs={{0,8},{8,16},{16,24},{24,32},{32,40},{40,48},{48,56},{56,0},{4,60}... | collective-permute-start | bytes 196616 | tf_op jit(solution)/shard_map/ppermute | solution.py:275
  133.2 2.7 %collective-permute-start.26 = (bf16[128,256]{1,0:T(8,128)(2,1)S(1)}, bf16[128,256]{1,0:T(8,128)(2,1)S(1)}, u32[]{:S(2)}, u32[]{:S(2)}) collective-permute-start(bf16[128,256]{1,0:T(8,128)(2,1)S(1)} %collective-permute-done.25.refs_2_), channel_id=1, source_target_pairs={{0,8},{8,16},{16,24},{24,32},{32,40},{40,48},{48,56},{56,0},{4,60}... | collective-permute-start | bytes 196616 | tf_op jit(solution)/shard_map/ppermute | solution.py:275
  138.0 2.6 %shard_map.113 = (f32[2,128,1024]{2,1,0:T(8,128)S(1)}, f32[2,128,1024]{2,1,0:T(8,128)S(1)}) custom-call(s32[4]{0:T(128)S(1)} %pad_add_fusion.ids, bf16[8,256,128]{2,1,0:T(8,128)(2,1)S(1)} %all-to-all-done.1.heads, bf16[128,1024]{1,0:T(8,128)(2,1)} %copy-done.2, bf16[128,1024]{1,0:T(8,128)(2,1)} %copy-done.1, bf16[128,1024]{1,0:T(8,128)(2,1)} %copy-done.5, ...), custom_call_target="tpu_custom_call" | custom-call | tf_op jit(solution)/shard_map/pallas_call | solution.py:27
  140.5 4.8 %collective-permute-start.9 = (f32[2,128,1024]{2,1,0:T(8,128)S(1)}, f32[2,128,1024]{2,1,0:T(8,128)S(1)}, u32[]{:S(2)}, u32[]{:S(2)}) collective-permute-start(f32[2,128,1024]{2,1,0:T(8,128)S(1)} %get-tuple-element.26), channel_id=1, source_target_pairs={{0,4},{4,0},{1,5},{5,1},{2,6},{6,2},{3,7},{7,3},{8,12},{12,8},{9,1... | collective-permute-start | bytes 3145736 | tf_op jit(solution)/shard_map/ppermute | solution.py:54
  148.4 2.5 %shard_map.116 = (f32[256,512]{1,0:T(8,128)}, f32[256,512]{1,0:T(8,128)}, f32[256,512]{1,0:T(8,128)}, f32[256,512]{1,0:T(8,128)}) custom-call(s32[4]{0:T(128)S(1)} %pad_add_fusion.ids, bf16[128,256]{1,0:T(8,128)(2,1)S(1)} %get-tuple-element.37.refs_0_, bf16[128,256]{1,0:T(8,128)(2,1)S(1)} %collective-permute-done.24.refs_1_, ...), custom_call_target="tpu_custom_call" | custom-call | tf_op jit(solution)/shard_map/pallas_call | solution.py:27
  (97 shorter events, 34.0 us)
Async XLA Ops:
  1.9 8.4 %collective-permute-start.1 = (bf16[128,1024]{1,0:T(8,128)(2,1)S(1)}, bf16[128,1024]{1,0:T(8,128)(2,1)S(1)}, u32[]{:S(2)}, u32[]{:S(2)}) collective-permute-start(bf16[128,1024]{1,0:T(8,128)(2,1)S(1)} %get-tuple-element.42.refs_0_), channel_id=1, source_target_pairs={{0,3},{1,0},{2,1},{3,2},{4,7},{5,4},{6,5},{7,6},{8,11},{9,8},{10,9... | collective-permute-start | bytes 786440 | tf_op jit(solution)/shard_map/ppermute | solution.py:54
  6.2 11.3 %collective-permute-start = (bf16[2,128,1024]{2,1,0:T(8,128)(2,1)S(1)}, bf16[2,128,1024]{2,1,0:T(8,128)(2,1)S(1)}, u32[]{:S(2)}, u32[]{:S(2)}) collective-permute-start(bf16[2,128,1024]{2,1,0:T(8,128)(2,1)S(1)} %shard_map.109.own.x0), channel_id=1, source_target_pairs={{0,4},{4,0},{1,5},{5,1},{2,6},{6,2},{3,7},{7,3},{8,12},{12,8},{9,1... | collective-permute-start | bytes 1572872 | tf_op jit(solution)/shard_map/ppermute | solution.py:54
  7.2 9.2 %collective-permute-start.4 = (bf16[128,1024]{1,0:T(8,128)(2,1)S(1)}, bf16[128,1024]{1,0:T(8,128)(2,1)S(1)}, u32[]{:S(2)}, u32[]{:S(2)}) collective-permute-start(bf16[128,1024]{1,0:T(8,128)(2,1)S(1)} %get-tuple-element.41.refs_1_), channel_id=1, source_target_pairs={{0,1},{1,2},{2,3},{3,0},{4,5},{5,6},{6,7},{7,4},{8,9},{9,10},{10,1... | collective-permute-start | bytes 786440 | tf_op jit(solution)/shard_map/ppermute | solution.py:54
  10.3 7.2 %collective-permute-start.2 = (bf16[128,1024]{1,0:T(8,128)(2,1)S(1)}, bf16[128,1024]{1,0:T(8,128)(2,1)S(1)}, u32[]{:S(2)}, u32[]{:S(2)}) collective-permute-start(bf16[128,1024]{1,0:T(8,128)(2,1)S(1)} %collective-permute-done.1.refs_2_), channel_id=1, source_target_pairs={{0,192},{64,0},{128,64},{192,128},{1,193},{65,1},{129,65},{193,129... | collective-permute-start | bytes 786440 | tf_op jit(solution)/shard_map/ppermute | solution.py:54
  13.0 7.3 %collective-permute-start.3 = (bf16[128,1024]{1,0:T(8,128)(2,1)S(1)}, bf16[128,1024]{1,0:T(8,128)(2,1)S(1)}, u32[]{:S(2)}, u32[]{:S(2)}) collective-permute-start(bf16[128,1024]{1,0:T(8,128)(2,1)S(1)} %collective-permute-done.1.refs_2_), channel_id=1, source_target_pairs={{0,3},{1,0},{2,1},{3,2},{4,7},{5,4},{6,5},{7,6},{8,11},{9,8},{10,9... | collective-permute-start | bytes 786440 | tf_op jit(solution)/shard_map/ppermute | solution.py:54
  16.4 7.1 %collective-permute-start.6 = (bf16[128,1024]{1,0:T(8,128)(2,1)S(1)}, bf16[128,1024]{1,0:T(8,128)(2,1)S(1)}, u32[]{:S(2)}, u32[]{:S(2)}) collective-permute-start(bf16[128,1024]{1,0:T(8,128)(2,1)S(1)} %collective-permute-done.4.refs_7_), channel_id=1, source_target_pairs={{0,64},{64,128},{128,192},{192,0},{1,65},{65,129},{129,193},{193,1... | collective-permute-start | bytes 786440 | tf_op jit(solution)/shard_map/ppermute | solution.py:54
  25.9 32.4 %all-to-all-start = ((bf16[8,256,128]{2,1,0:T(8,128)(2,1)}), bf16[8,256,128]{2,1,0:T(8,128)(2,1)S(1)}, u32[]{:S(2)}, u32[]{:S(2)}) async-start(bf16[8,256,128]{2,1,0:T(8,128)(2,1)} %get-tuple-element.21), calls=%async_computation | async-start | bytes 1048576 | tf_op jit(solution)/shard_map/all_to_all | solution.py:279
  34.1 23.0 %collective-permute-start.13 = (bf16[2,128,1024]{2,1,0:T(8,128)(2,1)S(1)}, bf16[2,128,1024]{2,1,0:T(8,128)(2,1)S(1)}, u32[]{:S(2)}, u32[]{:S(2)}) collective-permute-start(bf16[2,128,1024]{2,1,0:T(8,128)(2,1)S(1)} %shard_map.109.own.x0), channel_id=1, source_target_pairs={{0,8},{8,16},{16,24},{24,32},{32,40},{40,48},{48,56},{56,0},{4,60}... | collective-permute-start | bytes 1572872 | tf_op jit(solution)/shard_map/ppermute | solution.py:275
  36.8 24.4 %collective-permute-start.10 = (bf16[2,128,1024]{2,1,0:T(8,128)(2,1)S(1)}, bf16[2,128,1024]{2,1,0:T(8,128)(2,1)S(1)}, u32[]{:S(2)}, u32[]{:S(2)}) collective-permute-start(bf16[2,128,1024]{2,1,0:T(8,128)(2,1)S(1)} %shard_map.109.own.x0), channel_id=1, source_target_pairs={{0,56},{8,0},{16,8},{24,16},{32,24},{40,32},{48,40},{56,48},{4,12}... | collective-permute-start | bytes 1572872 | tf_op jit(solution)/shard_map/ppermute | solution.py:275
  57.1 10.2 %collective-permute-start.14 = (bf16[2,128,1024]{2,1,0:T(8,128)(2,1)S(1)}, bf16[2,128,1024]{2,1,0:T(8,128)(2,1)S(1)}, u32[]{:S(2)}, u32[]{:S(2)}) collective-permute-start(bf16[2,128,1024]{2,1,0:T(8,128)(2,1)S(1)} %collective-permute-done.13.f1), channel_id=1, source_target_pairs={{0,8},{8,16},{16,24},{24,32},{32,40},{40,48},{48,56},{56,0},{4,60}... | collective-permute-start | bytes 1572872 | tf_op jit(solution)/shard_map/ppermute | solution.py:275
  58.3 9.2 %collective-permute-start.7 = (bf16[2048,128]{1,0:T(8,128)(2,1)S(1)}, bf16[2048,128]{1,0:T(8,128)(2,1)S(1)}, u32[]{:S(2)}, u32[]{:S(2)}) collective-permute-start(bf16[2048,128]{1,0:T(8,128)(2,1)S(1)} %bitcast.34), channel_id=1, source_target_pairs={{0,4},{4,0},{1,5},{5,1},{2,6},{6,2},{3,7},{7,3},{8,12},{12,8},{9,1... | collective-permute-start | bytes 1572872 | tf_op jit(solution)/shard_map/ppermute | solution.py:54
  61.2 26.4 %collective-permute-start.11 = (bf16[2,128,1024]{2,1,0:T(8,128)(2,1)S(1)}, bf16[2,128,1024]{2,1,0:T(8,128)(2,1)S(1)}, u32[]{:S(2)}, u32[]{:S(2)}) collective-permute-start(bf16[2,128,1024]{2,1,0:T(8,128)(2,1)S(1)} %collective-permute-done.10.b1), channel_id=1, source_target_pairs={{0,56},{8,0},{16,8},{24,16},{32,24},{40,32},{48,40},{56,48},{4,12}... | collective-permute-start | bytes 1572872 | tf_op jit(solution)/shard_map/ppermute | solution.py:275
  67.3 20.3 %collective-permute-start.15 = (bf16[2,128,1024]{2,1,0:T(8,128)(2,1)S(1)}, bf16[2,128,1024]{2,1,0:T(8,128)(2,1)S(1)}, u32[]{:S(2)}, u32[]{:S(2)}) collective-permute-start(bf16[2,128,1024]{2,1,0:T(8,128)(2,1)S(1)} %collective-permute-done.14.f2), channel_id=1, source_target_pairs={{0,8},{8,16},{16,24},{24,32},{32,40},{40,48},{48,56},{56,0},{4,60}... | collective-permute-start | bytes 1572872 | tf_op jit(solution)/shard_map/ppermute | solution.py:275
  78.1 12.6 %collective-permute-start.8 = (bf16[3072,128]{1,0:T(8,128)(2,1)S(1)}, bf16[3072,128]{1,0:T(8,128)(2,1)S(1)}, u32[]{:S(2)}, u32[]{:S(2)}) collective-permute-start(bf16[3072,128]{1,0:T(8,128)(2,1)S(1)} %get-tuple-element.23.send), channel_id=1, source_target_pairs={{0,4},{4,0},{1,5},{5,1},{2,6},{6,2},{3,7},{7,3},{8,12},{12,8},{9,1... | collective-permute-start | bytes 2359304 | tf_op jit(solution)/shard_map/ppermute | solution.py:54
  87.6 11.9 %collective-permute-start.12 = (bf16[2,128,1024]{2,1,0:T(8,128)(2,1)S(1)}, bf16[2,128,1024]{2,1,0:T(8,128)(2,1)S(1)}, u32[]{:S(2)}, u32[]{:S(2)}) collective-permute-start(bf16[2,128,1024]{2,1,0:T(8,128)(2,1)S(1)} %collective-permute-done.11.b2), channel_id=1, source_target_pairs={{0,56},{8,0},{16,8},{24,16},{32,24},{40,32},{48,40},{56,48},{4,12}... | collective-permute-start | bytes 1572872 | tf_op jit(solution)/shard_map/ppermute | solution.py:275
  87.6 14.3 %collective-permute-start.16 = (bf16[2,128,1024]{2,1,0:T(8,128)(2,1)S(1)}, bf16[2,128,1024]{2,1,0:T(8,128)(2,1)S(1)}, u32[]{:S(2)}, u32[]{:S(2)}) collective-permute-start(bf16[2,128,1024]{2,1,0:T(8,128)(2,1)S(1)} %collective-permute-done.15.f3), channel_id=1, source_target_pairs={{0,8},{8,16},{16,24},{24,32},{32,40},{40,48},{48,56},{56,0},{4,60}... | collective-permute-start | bytes 1572872 | tf_op jit(solution)/shard_map/ppermute | solution.py:275
  106.8 31.2 %all-to-all-start.1 = ((bf16[8,256,128]{2,1,0:T(8,128)(2,1)}), bf16[8,256,128]{2,1,0:T(8,128)(2,1)S(1)}, u32[]{:S(2)}, u32[]{:S(2)}) async-start(bf16[8,256,128]{2,1,0:T(8,128)(2,1)} %bitcast.7), calls=%async_computation.1 | async-start | bytes 1048576 | tf_op jit(solution)/shard_map/all_to_all | solution.py:279
  130.6 7.0 %collective-permute-start.28 = (bf16[128,256]{1,0:T(8,128)(2,1)S(1)}, bf16[128,256]{1,0:T(8,128)(2,1)S(1)}, u32[]{:S(2)}, u32[]{:S(2)}) collective-permute-start(bf16[128,256]{1,0:T(8,128)(2,1)S(1)} %get-tuple-element.37.refs_0_), channel_id=1, source_target_pairs={{0,48},{8,56},{16,0},{24,8},{32,16},{40,24},{48,32},{56,40},{4,20}... | collective-permute-start | bytes 196616 | tf_op jit(solution)/shard_map/ppermute | solution.py:275
  130.6 10.0 %collective-permute-start.24 = (bf16[128,256]{1,0:T(8,128)(2,1)S(1)}, bf16[128,256]{1,0:T(8,128)(2,1)S(1)}, u32[]{:S(2)}, u32[]{:S(2)}) collective-permute-start(bf16[128,256]{1,0:T(8,128)(2,1)S(1)} %get-tuple-element.37.refs_0_), channel_id=1, source_target_pairs={{0,8},{8,16},{16,24},{24,32},{32,40},{40,48},{48,56},{56,0},{4,60}... | collective-permute-start | bytes 196616 | tf_op jit(solution)/shard_map/ppermute | solution.py:275
  133.2 12.1 %collective-permute-start.30 = (bf16[128,256]{1,0:T(8,128)(2,1)S(1)}, bf16[128,256]{1,0:T(8,128)(2,1)S(1)}, u32[]{:S(2)}, u32[]{:S(2)}) collective-permute-start(bf16[128,256]{1,0:T(8,128)(2,1)S(1)} %get-tuple-element.37.refs_0_), channel_id=1, source_target_pairs={{0,56},{8,0},{16,8},{24,16},{32,24},{40,32},{48,40},{56,48},{4,12}... | collective-permute-start | bytes 196616 | tf_op jit(solution)/shard_map/ppermute | solution.py:275
  133.2 12.3 %collective-permute-start.26 = (bf16[128,256]{1,0:T(8,128)(2,1)S(1)}, bf16[128,256]{1,0:T(8,128)(2,1)S(1)}, u32[]{:S(2)}, u32[]{:S(2)}) collective-permute-start(bf16[128,256]{1,0:T(8,128)(2,1)S(1)} %collective-permute-done.25.refs_2_), channel_id=1, source_target_pairs={{0,8},{8,16},{16,24},{24,32},{32,40},{40,48},{48,56},{56,0},{4,60}... | collective-permute-start | bytes 196616 | tf_op jit(solution)/shard_map/ppermute | solution.py:275
  135.9 9.6 %collective-permute-start.27 = (bf16[128,256]{1,0:T(8,128)(2,1)S(1)}, bf16[128,256]{1,0:T(8,128)(2,1)S(1)}, u32[]{:S(2)}, u32[]{:S(2)}) collective-permute-start(bf16[128,256]{1,0:T(8,128)(2,1)S(1)} %collective-permute-done.25.refs_2_), channel_id=1, source_target_pairs={{0,16},{8,24},{16,32},{24,40},{32,48},{40,56},{48,0},{56,8},{4,52}... | collective-permute-start | bytes 196616 | tf_op jit(solution)/shard_map/ppermute | solution.py:275
  137.6 8.0 %collective-permute-start.29 = (bf16[128,256]{1,0:T(8,128)(2,1)S(1)}, bf16[128,256]{1,0:T(8,128)(2,1)S(1)}, u32[]{:S(2)}, u32[]{:S(2)}) collective-permute-start(bf16[128,256]{1,0:T(8,128)(2,1)S(1)} %collective-permute-done.28.refs_6_), channel_id=1, source_target_pairs={{0,56},{8,0},{16,8},{24,16},{32,24},{40,32},{48,40},{56,48},{4,12}... | collective-permute-start | bytes 196616 | tf_op jit(solution)/shard_map/ppermute | solution.py:275
  140.5 10.4 %collective-permute-start.9 = (f32[2,128,1024]{2,1,0:T(8,128)S(1)}, f32[2,128,1024]{2,1,0:T(8,128)S(1)}, u32[]{:S(2)}, u32[]{:S(2)}) collective-permute-start(f32[2,128,1024]{2,1,0:T(8,128)S(1)} %get-tuple-element.26), channel_id=1, source_target_pairs={{0,4},{4,0},{1,5},{5,1},{2,6},{6,2},{3,7},{7,3},{8,12},{12,8},{9,1... | collective-permute-start | bytes 3145736 | tf_op jit(solution)/shard_map/ppermute | solution.py:54
  (27 other events, 249.4 us)
